TPU v7x, 32 devices: a whole 2x2x4 slice. The times are simulated.
32 devices in a mesh: groups: 2 (over y), rows: 16 (over z, x, core).
Axes of the slice: x: 2, y: 2, z: 4, core: 2. Of those that a mesh axis runs over, the one named last changes fastest.
Arguments:
- response_tiles: bfloat16 [128, 30, 128, 128], P(('groups', 'rows')), parts along dimension 0, may hold values from -0.09375 to 0.09375
- tile_cols: int32 [128, 30], P(('groups', 'rows')), parts along dimension 0, may hold values from 0 to 63, as said below
- tile_count: int32 [128], P(('groups', 'rows')), parts along dimension 0, may hold values from 15 to 30
- heat_start: float32 [16384, 128], P(('groups', 'rows')), parts along dimension 0, may hold values from -6 to 6
- recorded_well_warmth: float32 [1024, 128], P(('groups', 'rows')), parts along dimension 0, may hold values from -18 to 18
- bore_lengths: int32 [32, 32], P(('groups', 'rows')), parts along dimension 0, may hold values from 1 to 24, 512 in all within a row
Outputs:
- heat_rates: float32 [16384, 128], P(('groups', 'rows')), parts along dimension 0
- bore_misfit: float32 [1024, 128], P(('groups', 'rows')), parts along dimension 0
There are 2 independent parts, one for each index of `groups`. A program takes and returns all parts, laid end to end along the dimension named above; each array names one. Nothing has to cross between parts.
Inputs may be any that keep to these rules, and one draw needn't show every extreme that they name: `tile_cols`: for block row i the first tile_count[i] entries are distinct block columns c with |c - i| <= 16; the other entries equal i and are unused.
All inputs are finite; a program needn't handle non-finite values.
Results may differ from a plain program's by a relative error of at most 0.0046.
Values may be sent and summed in bfloat16 or wider, within the bound.
No kernel may reach another device: no remote copies, remote signals or barrier semaphores. Data moves between devices by JAX's collectives and lax.ppermute only.
A program may use at most 64 MiB of HBM per device.

v0:
```python
import jax
import jax.numpy as jnp
from jax import lax
from jax.sharding import PartitionSpec as P

REACH = 4
ITERS = 2


def passed_along(value, axis, steps):
    count = lax.axis_size(axis)
    leading, last = (max(0, -steps), min(count, count - steps))
    return lax.ppermute(value, axis, [(source, source + steps) for source in range(leading, last)])


def bore_members(lengths, seg_rows):
    bore_ends = jnp.cumsum(lengths)
    starts = bore_ends - lengths
    position = jnp.arange(seg_rows, dtype=jnp.int32)
    inside = (position[None, :] >= starts[:, None]) & (position[None, :] < bore_ends[:, None])
    return inside.astype(jnp.float32)


def on_device(
    response_tiles, tile_cols, tile_count, heat_start, recorded_well_warmth, bore_lengths
):
    block_rows = response_tiles.shape[0]
    slot_count = response_tiles.shape[1]
    tile_size = response_tiles.shape[2]
    columns = heat_start.shape[1]
    seg_rows = block_rows * tile_size
    window_blocks = (2 * REACH + 1) * block_rows
    first_block = (lax.axis_index("rows") - REACH) * block_rows
    window_slot = tile_cols - first_block
    in_use = jnp.arange(slot_count, dtype=jnp.int32)[None, :] < tile_count[:, None]
    flat_slot = window_slot.reshape(-1)
    members = bore_members(bore_lengths[0], seg_rows)
    counts = bore_lengths[0].astype(jnp.float32)

    def fetch_window(local_panel):
        received = {}
        for offset in list(range(1, REACH + 1)) + list(range(-REACH, 0)):
            received[offset] = passed_along(local_panel, "rows", offset)
        ordered = [received[offset] for offset in range(REACH, 0, -1)] + [local_panel]
        ordered = ordered + [received[-offset] for offset in range(1, REACH + 1)]
        return jnp.concatenate(ordered, axis=0)

    def predicted_output(field):
        local_panel = field.astype(jnp.bfloat16).reshape(block_rows, tile_size, columns)
        window = fetch_window(local_panel)
        panels = jnp.where(
            in_use[:, :, None, None], window[window_slot], jnp.zeros((), jnp.bfloat16)
        )
        response = jnp.einsum(
            "bkij,bkjt->bit", response_tiles, panels, preferred_element_type=jnp.float32
        )
        return response.reshape(seg_rows, columns)

    def adjoint(residual):
        resid_blocks = residual.reshape(block_rows, tile_size, columns)
        products = jnp.einsum(
            "bkij,bit->bkjt", response_tiles, resid_blocks, preferred_element_type=jnp.float32
        )
        products = jnp.where(in_use[:, :, None, None], products, 0.0)
        window_sums = jnp.zeros((window_blocks, tile_size, columns), jnp.float32)
        window_sums = window_sums.at[flat_slot].add(
            products.reshape(block_rows * slot_count, tile_size, columns)
        )

        def window_block(offset):
            return window_sums[(offset + REACH) * block_rows : (offset + REACH + 1) * block_rows]

        summed = window_block(0)
        for offset in list(range(1, REACH + 1)) + list(range(-REACH, 0)):
            summed = summed + passed_along(window_block(offset), "rows", offset)
        return summed.reshape(seg_rows, columns)

    def well_mean_warmth(field):
        return jnp.dot(members, field, precision=lax.Precision.HIGHEST) / counts[:, None]

    source_power_entries = heat_start
    thermal_profile = predicted_output(source_power_entries)
    for iteration in range(ITERS):
        squared_error_total = well_mean_warmth(thermal_profile) - recorded_well_warmth
        shares = squared_error_total / counts[:, None]
        segment_residual = jnp.dot(members.T, shares, precision=lax.Precision.HIGHEST).astype(
            jnp.bfloat16
        )
        gradient = adjoint(segment_residual)
        grad_norm = lax.psum(jnp.sum(gradient * gradient), "rows")
        operator_product_entries = predicted_output(gradient)
        image_mean = well_mean_warmth(operator_product_entries)
        curvature_sum = lax.psum(jnp.sum(image_mean * image_mean), "rows")
        descent_stride = grad_norm / (curvature_sum + 1e-06)
        source_power_entries = source_power_entries - descent_stride * gradient
        thermal_profile = thermal_profile - descent_stride * operator_product_entries
    return (source_power_entries, well_mean_warmth(thermal_profile) - recorded_well_warmth)


def solution(mesh):
    placed = (
        P(("groups", "rows"), None, None, None),
        P(("groups", "rows"), None),
        P(("groups", "rows")),
        P(("groups", "rows"), None),
        P(("groups", "rows"), None),
        P(("groups", "rows"), None),
    )
    return jax.shard_map(
        on_device,
        mesh=mesh,
        in_specs=placed,
        out_specs=(P(("groups", "rows"), None), P(("groups", "rows"), None)),
        check_vma=False,
    )
```

profile of v0, /device:TPU:0, one launch (start us, length us, event | category | flops | bytes accessed | tf_op | source)
XLA Modules:
  0.0 314.7 jit_solution(9513673071672859147)
XLA Ops:
  1.6 4.9 %collective-permute-start = (bf16[4,128,128]{2,1,0:T(8,128)(2,1)S(1)}, bf16[4,128,128]{2,1,0:T(8,128)(2,1)S(1)}, u32[]{:S(2)}, u32[]{:S(2)}) collective-permute-start(bf16[4,128,128]{2,1,0:T(8,128)(2,1)S(1)} %bitcast.77), channel_id=1, source_target_pairs={{0,4},{1,5},{2,6},{3,7},{4,8},{5,9},{6,10},{7,11},{8,12},{9,13},{1... | collective-permute-start | bytes 393224 | tf_op jit(solution)/shard_map/ppermute | solution.py:13
  9.1 3.5 %collective-permute-start.2 = (bf16[4,128,128]{2,1,0:T(8,128)(2,1)S(1)}, bf16[4,128,128]{2,1,0:T(8,128)(2,1)S(1)}, u32[]{:S(2)}, u32[]{:S(2)}) collective-permute-start(bf16[4,128,128]{2,1,0:T(8,128)(2,1)S(1)} %bitcast.79), channel_id=1, source_target_pairs={{0,2},{1,3},{2,4},{3,5},{4,6},{5,7},{6,8},{7,9},{8,10},{9,11},{10,... | collective-permute-start | bytes 393224 | tf_op jit(solution)/shard_map/ppermute | solution.py:13
  24.4 5.2 %collective-permute-done.5 = bf16[4,128,128]{2,1,0:T(8,128)(2,1)S(1)} collective-permute-done((bf16[4,128,128]{2,1,0:T(8,128)(2,1)S(1)}, bf16[4,128,128]{2,1,0:T(8,128)(2,1)S(1)}, u32[]{:S(2)}, u32[]{:S(2)}) %collective-permute-start.5) | collective-permute-done | bytes 131104 | tf_op jit(solution)/shard_map/ppermute | solution.py:13
  30.6 5.2 %collective-permute-done.7 = bf16[4,128,128]{2,1,0:T(8,128)(2,1)S(1)} collective-permute-done((bf16[4,128,128]{2,1,0:T(8,128)(2,1)S(1)}, bf16[4,128,128]{2,1,0:T(8,128)(2,1)S(1)}, u32[]{:S(2)}, u32[]{:S(2)}) %collective-permute-start.7) | collective-permute-done | bytes 131104 | tf_op jit(solution)/shard_map/ppermute | solution.py:13
  38.7 4.7 %fusion.4 = f32[4,128,128,1]{1,2,3,0:T(8,128)S(1)} fusion(bf16[4,30,128,128]{3,2,1,0:T(8,128)(2,1)} %param.6, bf16[4,30,128,128]{3,2,1,0:T(8,128)(2,1)} %bitcast.65, pred[4,30]{1,0:T(4,128)(4,1)S(1)} %iota_compare_fusion.2), kind=kOutput, calls=%fused_computation.11 | convolution fusion | flops 505282560 | bytes 8126584 | tf_op jit(solution)/shard_map/bkij,bkjt->bit/dot_general | solution.py:54
  44.1 4.3 %broadcast_select_fusion.1 = f32[4,128,30,128]{3,1,2,0:T(8,128)} fusion(pred[4,30]{1,0:T(4,128)(4,1)S(1)} %iota_compare_fusion.2, bf16[4,128,128,1]{2,1,3,0:T(8,128)(2,1)S(1)} %bitcast.75, bf16[4,30,128,128]{3,2,1,0:T(8,128)(2,1)S(1)} %copy-done), kind=kOutput, calls=%fused_computation.10 | convolution fusion | flops 505282560 | bytes 11927672 | tf_op jit(solution)/shard_map/bkij,bit->bkjt/dot_general | solution.py:61
  48.4 9.1 %copy.13 = f32[120,128,128]{2,1,0:T(8,128)} copy(f32[120,128,128]{1,2,0:T(8,128)} %bitcast.62) | data formatting | bytes 15728640 | tf_op jit(solution)/shard_map/reshape | solution.py:67
  57.8 16.9 %scatter_fusion = f32[36,128,128]{2,1,0:T(8,128)S(1)} fusion(f32[36,128,128]{2,1,0:T(8,128)S(1)} %broadcast.52.clone, s32[120]{0:T(128)S(1)} %fusion.39, f32[120,128,128]{2,1,0:T(8,128)} %copy.13), kind=kCustom, calls=%fused_computation.3 | custom fusion | flops 1966080 | bytes 23593440 | tf_op jit(solution)/shard_map/scatter-add | solution.py:66
  94.9 14.7 %collective-permute-done.9 = f32[4,128,128]{2,1,0:T(8,128)S(1)} collective-permute-done((f32[4,128,128]{2,1,0:T(8,128)S(1)}, f32[4,128,128]{2,1,0:T(8,128)S(1)}, u32[]{:S(2)}, u32[]{:S(2)}) %collective-permute-start.9) | collective-permute-done | bytes 262176 | tf_op jit(solution)/shard_map/ppermute | solution.py:13
  112.8 5.9 %collective-permute-start.17 = (bf16[4,128,128]{2,1,0:T(8,128)(2,1)S(1)}, bf16[4,128,128]{2,1,0:T(8,128)(2,1)S(1)}, u32[]{:S(2)}, u32[]{:S(2)}) collective-permute-start(bf16[4,128,128]{2,1,0:T(8,128)(2,1)S(1)} %convert_element_type.28), channel_id=1, source_target_pairs={{0,3},{1,4},{2,5},{3,6},{4,7},{5,8},{6,9},{7,10},{8,11},{9,12},{10... | collective-permute-start | bytes 393224 | tf_op jit(solution)/shard_map/ppermute | solution.py:13
  128.1 6.3 %collective-permute-done.21 = bf16[4,128,128]{2,1,0:T(8,128)(2,1)S(1)} collective-permute-done((bf16[4,128,128]{2,1,0:T(8,128)(2,1)S(1)}, bf16[4,128,128]{2,1,0:T(8,128)(2,1)S(1)}, u32[]{:S(2)}, u32[]{:S(2)}) %collective-permute-start.21) | collective-permute-done | bytes 131104 | tf_op jit(solution)/shard_map/ppermute | solution.py:13
  135.4 4.8 %collective-permute-done.23 = bf16[4,128,128]{2,1,0:T(8,128)(2,1)S(1)} collective-permute-done((bf16[4,128,128]{2,1,0:T(8,128)(2,1)S(1)}, bf16[4,128,128]{2,1,0:T(8,128)(2,1)S(1)}, u32[]{:S(2)}, u32[]{:S(2)}) %collective-permute-start.23) | collective-permute-done | bytes 131104 | tf_op jit(solution)/shard_map/ppermute | solution.py:13
  143.1 4.6 %fusion.2 = f32[4,128,128,1]{1,2,3,0:T(8,128)S(1)} fusion(bf16[4,30,128,128]{3,2,1,0:T(8,128)(2,1)} %param.6, bf16[4,30,128,128]{3,2,1,0:T(8,128)(2,1)} %bitcast.66, pred[4,30]{1,0:T(4,128)(4,1)S(1)} %iota_compare_fusion.2), kind=kOutput, calls=%fused_computation.7 | convolution fusion | flops 505282560 | bytes 8126584 | tf_op jit(solution)/shard_map/bkij,bkjt->bit/dot_general | solution.py:54
  148.5 30.3 %all-reduce.1 = (f32[]{:T(128)}, f32[]{:T(128)}) all-reduce(f32[]{:T(128)} %get-tuple-element.8, f32[]{:T(128)} %fusion.19), channel_id=1, replica_groups=mesh['groups'=2,'rows'=16] {'rows'}, use_global_device_ids=true, to_apply=%region_3.4 | all-reduce | flops 2 | bytes 16 | tf_op jit(solution)/shard_map/psum | solution.py:90
  180.8 6.4 %broadcast_select_fusion = f32[4,128,30,128]{3,1,2,0:T(8,128)} fusion(pred[4,30]{1,0:T(4,128)(4,1)S(1)} %iota_compare_fusion.2, bf16[4,128,128,1]{2,1,3,0:T(8,128)(2,1)S(1)} %bitcast.76, bf16[4,30,128,128]{3,2,1,0:T(8,128)(2,1)} %param.6), kind=kOutput, calls=%fused_computation.9 | convolution fusion | flops 505282560 | bytes 11927672 | tf_op jit(solution)/shard_map/bkij,bit->bkjt/dot_general | solution.py:61
  187.2 9.1 %copy.15 = f32[120,128,128]{2,1,0:T(8,128)} copy(f32[120,128,128]{1,2,0:T(8,128)} %bitcast.63) | data formatting | bytes 15728640 | tf_op jit(solution)/shard_map/reshape | solution.py:67
  196.6 16.9 %scatter_fusion.1 = f32[36,128,128]{2,1,0:T(8,128)S(1)} fusion(f32[36,128,128]{2,1,0:T(8,128)S(1)} %broadcast.52, s32[120]{0:T(128)S(1)} %fusion.39, f32[120,128,128]{2,1,0:T(8,128)} %copy.15), kind=kCustom, calls=%fused_computation.4 | custom fusion | flops 1966080 | bytes 23593440 | tf_op jit(solution)/shard_map/scatter-add | solution.py:66
  228.3 3.9 %collective-permute-done.28 = f32[4,128,128]{2,1,0:T(8,128)S(1)} collective-permute-done((f32[4,128,128]{2,1,0:T(8,128)S(1)}, f32[4,128,128]{2,1,0:T(8,128)S(1)}, u32[]{:S(2)}, u32[]{:S(2)}) %collective-permute-start.28) | collective-permute-done | bytes 262176 | tf_op jit(solution)/shard_map/ppermute | solution.py:13
  234.2 12.5 %collective-permute-start.32 = (bf16[4,128,128]{2,1,0:T(8,128)(2,1)S(1)}, bf16[4,128,128]{2,1,0:T(8,128)(2,1)S(1)}, u32[]{:S(2)}, u32[]{:S(2)}) collective-permute-start(bf16[4,128,128]{2,1,0:T(8,128)(2,1)S(1)} %get-tuple-element.6), channel_id=1, source_target_pairs={{0,4},{1,5},{2,6},{3,7},{4,8},{5,9},{6,10},{7,11},{8,12},{9,13},{1... | collective-permute-start | bytes 393224 | tf_op jit(solution)/shard_map/ppermute | solution.py:13
  246.7 4.7 %collective-permute-start.33 = (bf16[4,128,128]{2,1,0:T(8,128)(2,1)S(1)}, bf16[4,128,128]{2,1,0:T(8,128)(2,1)S(1)}, u32[]{:S(2)}, u32[]{:S(2)}) collective-permute-start(bf16[4,128,128]{2,1,0:T(8,128)(2,1)S(1)} %get-tuple-element.6), channel_id=1, source_target_pairs={{0,3},{1,4},{2,5},{3,6},{4,7},{5,8},{6,9},{7,10},{8,11},{9,12},{10... | collective-permute-start | bytes 393224 | tf_op jit(solution)/shard_map/ppermute | solution.py:13
  261.5 6.1 %collective-permute-done.37 = bf16[4,128,128]{2,1,0:T(8,128)(2,1)S(1)} collective-permute-done((bf16[4,128,128]{2,1,0:T(8,128)(2,1)S(1)}, bf16[4,128,128]{2,1,0:T(8,128)(2,1)S(1)}, u32[]{:S(2)}, u32[]{:S(2)}) %collective-permute-start.37) | collective-permute-done | bytes 131104 | tf_op jit(solution)/shard_map/ppermute | solution.py:13
  268.4 4.8 %collective-permute-done.39 = bf16[4,128,128]{2,1,0:T(8,128)(2,1)S(1)} collective-permute-done((bf16[4,128,128]{2,1,0:T(8,128)(2,1)S(1)}, bf16[4,128,128]{2,1,0:T(8,128)(2,1)S(1)}, u32[]{:S(2)}, u32[]{:S(2)}) %collective-permute-start.39) | collective-permute-done | bytes 131104 | tf_op jit(solution)/shard_map/ppermute | solution.py:13
  276.2 4.6 %fusion = f32[4,128,128,1]{1,2,3,0:T(8,128)S(1)} fusion(bf16[4,30,128,128]{3,2,1,0:T(8,128)(2,1)} %param.6, bf16[4,30,128,128]{3,2,1,0:T(8,128)(2,1)} %bitcast.64, pred[4,30]{1,0:T(4,128)(4,1)S(1)} %iota_compare_fusion.2), kind=kOutput, calls=%fused_computation.5 | convolution fusion | flops 505282560 | bytes 8126584 | tf_op jit(solution)/shard_map/bkij,bkjt->bit/dot_general | solution.py:54
  281.7 30.1 %all-reduce = (f32[]{:T(128)}, f32[]{:T(128)}) all-reduce(f32[]{:T(128)} %multiply_reduce_fusion, f32[]{:T(128)} %fusion.20), channel_id=1, replica_groups=mesh['groups'=2,'rows'=16] {'rows'}, use_global_device_ids=true, to_apply=%region_8.9 | all-reduce | flops 2 | bytes 16 | tf_op jit(solution)/shard_map/psum | solution.py:90
  (133 shorter events, 91.4 us)
Async XLA Ops:
  1.6 18.7 %collective-permute-start = (bf16[4,128,128]{2,1,0:T(8,128)(2,1)S(1)}, bf16[4,128,128]{2,1,0:T(8,128)(2,1)S(1)}, u32[]{:S(2)}, u32[]{:S(2)}) collective-permute-start(bf16[4,128,128]{2,1,0:T(8,128)(2,1)S(1)} %bitcast.77), channel_id=1, source_target_pairs={{0,4},{1,5},{2,6},{3,7},{4,8},{5,9},{6,10},{7,11},{8,12},{9,13},{1... | collective-permute-start | bytes 393224 | tf_op jit(solution)/shard_map/ppermute | solution.py:13
  6.5 15.1 %collective-permute-start.1 = (bf16[4,128,128]{2,1,0:T(8,128)(2,1)S(1)}, bf16[4,128,128]{2,1,0:T(8,128)(2,1)S(1)}, u32[]{:S(2)}, u32[]{:S(2)}) collective-permute-start(bf16[4,128,128]{2,1,0:T(8,128)(2,1)S(1)} %bitcast.78), channel_id=1, source_target_pairs={{0,3},{1,4},{2,5},{3,6},{4,7},{5,8},{6,9},{7,10},{8,11},{9,12},{10... | collective-permute-start | bytes 393224 | tf_op jit(solution)/shard_map/ppermute | solution.py:13
  9.1 13.9 %collective-permute-start.2 = (bf16[4,128,128]{2,1,0:T(8,128)(2,1)S(1)}, bf16[4,128,128]{2,1,0:T(8,128)(2,1)S(1)}, u32[]{:S(2)}, u32[]{:S(2)}) collective-permute-start(bf16[4,128,128]{2,1,0:T(8,128)(2,1)S(1)} %bitcast.79), channel_id=1, source_target_pairs={{0,2},{1,3},{2,4},{3,5},{4,6},{5,7},{6,8},{7,9},{8,10},{9,11},{10,... | collective-permute-start | bytes 393224 | tf_op jit(solution)/shard_map/ppermute | solution.py:13
  12.6 11.8 %collective-permute-start.3 = (bf16[4,128,128]{2,1,0:T(8,128)(2,1)S(1)}, bf16[4,128,128]{2,1,0:T(8,128)(2,1)S(1)}, u32[]{:S(2)}, u32[]{:S(2)}) collective-permute-start(bf16[4,128,128]{2,1,0:T(8,128)(2,1)S(1)} %bitcast.80), channel_id=1, source_target_pairs={{0,1},{1,2},{2,3},{3,4},{4,5},{5,6},{6,7},{7,8},{8,9},{9,10},{10,1... | collective-permute-start | bytes 393224 | tf_op jit(solution)/shard_map/ppermute | solution.py:13
  23.0 12.8 %collective-permute-start.7 = (bf16[4,128,128]{2,1,0:T(8,128)(2,1)S(1)}, bf16[4,128,128]{2,1,0:T(8,128)(2,1)S(1)}, u32[]{:S(2)}, u32[]{:S(2)}) collective-permute-start(bf16[4,128,128]{2,1,0:T(8,128)(2,1)S(1)} %bitcast.84), channel_id=1, source_target_pairs={{4,0},{5,1},{6,2},{7,3},{8,4},{9,5},{10,6},{11,7},{12,8},{13,9},{1... | collective-permute-start | bytes 393224 | tf_op jit(solution)/shard_map/ppermute | solution.py:13
  80.7 11.0 %collective-permute-start.12 = (f32[4,128,128]{2,1,0:T(8,128)S(1)}, f32[4,128,128]{2,1,0:T(8,128)S(1)}, u32[]{:S(2)}, u32[]{:S(2)}) collective-permute-start(f32[4,128,128]{2,1,0:T(8,128)S(1)} %get-tuple-element.24), channel_id=1, source_target_pairs={{4,0},{5,1},{6,2},{7,3},{8,4},{9,5},{10,6},{11,7},{12,8},{13,9},{1... | collective-permute-start | bytes 786440 | tf_op jit(solution)/shard_map/ppermute | solution.py:13
  82.0 12.9 %collective-permute-start.13 = (f32[4,128,128]{2,1,0:T(8,128)S(1)}, f32[4,128,128]{2,1,0:T(8,128)S(1)}, u32[]{:S(2)}, u32[]{:S(2)}) collective-permute-start(f32[4,128,128]{2,1,0:T(8,128)S(1)} %get-tuple-element.23), channel_id=1, source_target_pairs={{3,0},{4,1},{5,2},{6,3},{7,4},{8,5},{9,6},{10,7},{11,8},{12,9},{13... | collective-permute-start | bytes 786440 | tf_op jit(solution)/shard_map/ppermute | solution.py:13
  83.3 11.6 %collective-permute-start.14 = (f32[4,128,128]{2,1,0:T(8,128)S(1)}, f32[4,128,128]{2,1,0:T(8,128)S(1)}, u32[]{:S(2)}, u32[]{:S(2)}) collective-permute-start(f32[4,128,128]{2,1,0:T(8,128)S(1)} %get-tuple-element.22), channel_id=1, source_target_pairs={{2,0},{3,1},{4,2},{5,3},{6,4},{7,5},{8,6},{9,7},{10,8},{11,9},{12,... | collective-permute-start | bytes 786440 | tf_op jit(solution)/shard_map/ppermute | solution.py:13
  84.6 10.3 %collective-permute-start.15 = (f32[4,128,128]{2,1,0:T(8,128)S(1)}, f32[4,128,128]{2,1,0:T(8,128)S(1)}, u32[]{:S(2)}, u32[]{:S(2)}) collective-permute-start(f32[4,128,128]{2,1,0:T(8,128)S(1)} %get-tuple-element.21), channel_id=1, source_target_pairs={{1,0},{2,1},{3,2},{4,3},{5,4},{6,5},{7,6},{8,7},{9,8},{10,9},{11,1... | collective-permute-start | bytes 786440 | tf_op jit(solution)/shard_map/ppermute | solution.py:13
  91.7 17.9 %collective-permute-start.9 = (f32[4,128,128]{2,1,0:T(8,128)S(1)}, f32[4,128,128]{2,1,0:T(8,128)S(1)}, u32[]{:S(2)}, u32[]{:S(2)}) collective-permute-start(f32[4,128,128]{2,1,0:T(8,128)S(1)} %get-tuple-element.27), channel_id=1, source_target_pairs={{0,2},{1,3},{2,4},{3,5},{4,6},{5,7},{6,8},{7,9},{8,10},{9,11},{10,... | collective-permute-start | bytes 786440 | tf_op jit(solution)/shard_map/ppermute | solution.py:13
  110.4 13.6 %collective-permute-start.16 = (bf16[4,128,128]{2,1,0:T(8,128)(2,1)S(1)}, bf16[4,128,128]{2,1,0:T(8,128)(2,1)S(1)}, u32[]{:S(2)}, u32[]{:S(2)}) collective-permute-start(bf16[4,128,128]{2,1,0:T(8,128)(2,1)S(1)} %convert_element_type.28), channel_id=1, source_target_pairs={{0,4},{1,5},{2,6},{3,7},{4,8},{5,9},{6,10},{7,11},{8,12},{9,13},{1... | collective-permute-start | bytes 393224 | tf_op jit(solution)/shard_map/ppermute | solution.py:13
  112.8 12.5 %collective-permute-start.17 = (bf16[4,128,128]{2,1,0:T(8,128)(2,1)S(1)}, bf16[4,128,128]{2,1,0:T(8,128)(2,1)S(1)}, u32[]{:S(2)}, u32[]{:S(2)}) collective-permute-start(bf16[4,128,128]{2,1,0:T(8,128)(2,1)S(1)} %convert_element_type.28), channel_id=1, source_target_pairs={{0,3},{1,4},{2,5},{3,6},{4,7},{5,8},{6,9},{7,10},{8,11},{9,12},{10... | collective-permute-start | bytes 393224 | tf_op jit(solution)/shard_map/ppermute | solution.py:13
  124.0 10.4 %collective-permute-start.21 = (bf16[4,128,128]{2,1,0:T(8,128)(2,1)S(1)}, bf16[4,128,128]{2,1,0:T(8,128)(2,1)S(1)}, u32[]{:S(2)}, u32[]{:S(2)}) collective-permute-start(bf16[4,128,128]{2,1,0:T(8,128)(2,1)S(1)} %convert_element_type.28), channel_id=1, source_target_pairs={{2,0},{3,1},{4,2},{5,3},{6,4},{7,5},{8,6},{9,7},{10,8},{11,9},{12,... | collective-permute-start | bytes 393224 | tf_op jit(solution)/shard_map/ppermute | solution.py:13
  125.3 10.0 %collective-permute-start.22 = (bf16[4,128,128]{2,1,0:T(8,128)(2,1)S(1)}, bf16[4,128,128]{2,1,0:T(8,128)(2,1)S(1)}, u32[]{:S(2)}, u32[]{:S(2)}) collective-permute-start(bf16[4,128,128]{2,1,0:T(8,128)(2,1)S(1)} %convert_element_type.28), channel_id=1, source_target_pairs={{3,0},{4,1},{5,2},{6,3},{7,4},{8,5},{9,6},{10,7},{11,8},{12,9},{13... | collective-permute-start | bytes 393224 | tf_op jit(solution)/shard_map/ppermute | solution.py:13
  126.7 13.4 %collective-permute-start.23 = (bf16[4,128,128]{2,1,0:T(8,128)(2,1)S(1)}, bf16[4,128,128]{2,1,0:T(8,128)(2,1)S(1)}, u32[]{:S(2)}, u32[]{:S(2)}) collective-permute-start(bf16[4,128,128]{2,1,0:T(8,128)(2,1)S(1)} %convert_element_type.28), channel_id=1, source_target_pairs={{4,0},{5,1},{6,2},{7,3},{8,4},{9,5},{10,6},{11,7},{12,8},{13,9},{1... | collective-permute-start | bytes 393224 | tf_op jit(solution)/shard_map/ppermute | solution.py:13
  216.8 10.3 %collective-permute-start.26 = (f32[4,128,128]{2,1,0:T(8,128)S(1)}, f32[4,128,128]{2,1,0:T(8,128)S(1)}, u32[]{:S(2)}, u32[]{:S(2)}) collective-permute-start(f32[4,128,128]{2,1,0:T(8,128)S(1)} %get-tuple-element.18), channel_id=1, source_target_pairs={{0,3},{1,4},{2,5},{3,6},{4,7},{5,8},{6,9},{7,10},{8,11},{9,12},{10... | collective-permute-start | bytes 786440 | tf_op jit(solution)/shard_map/ppermute | solution.py:13
  218.1 10.3 %collective-permute-start.27 = (f32[4,128,128]{2,1,0:T(8,128)S(1)}, f32[4,128,128]{2,1,0:T(8,128)S(1)}, u32[]{:S(2)}, u32[]{:S(2)}) collective-permute-start(f32[4,128,128]{2,1,0:T(8,128)S(1)} %get-tuple-element.17), channel_id=1, source_target_pairs={{0,4},{1,5},{2,6},{3,7},{4,8},{5,9},{6,10},{7,11},{8,12},{9,13},{1... | collective-permute-start | bytes 786440 | tf_op jit(solution)/shard_map/ppermute | solution.py:13
  219.4 12.9 %collective-permute-start.28 = (f32[4,128,128]{2,1,0:T(8,128)S(1)}, f32[4,128,128]{2,1,0:T(8,128)S(1)}, u32[]{:S(2)}, u32[]{:S(2)}) collective-permute-start(f32[4,128,128]{2,1,0:T(8,128)S(1)} %get-tuple-element.16), channel_id=1, source_target_pairs={{4,0},{5,1},{6,2},{7,3},{8,4},{9,5},{10,6},{11,7},{12,8},{13,9},{1... | collective-permute-start | bytes 786440 | tf_op jit(solution)/shard_map/ppermute | solution.py:13
  220.7 11.6 %collective-permute-start.29 = (f32[4,128,128]{2,1,0:T(8,128)S(1)}, f32[4,128,128]{2,1,0:T(8,128)S(1)}, u32[]{:S(2)}, u32[]{:S(2)}) collective-permute-start(f32[4,128,128]{2,1,0:T(8,128)S(1)} %get-tuple-element.15), channel_id=1, source_target_pairs={{3,0},{4,1},{5,2},{6,3},{7,4},{8,5},{9,6},{10,7},{11,8},{12,9},{13... | collective-permute-start | bytes 786440 | tf_op jit(solution)/shard_map/ppermute | solution.py:13
  223.5 10.6 %collective-permute-start.30 = (f32[4,128,128]{2,1,0:T(8,128)S(1)}, f32[4,128,128]{2,1,0:T(8,128)S(1)}, u32[]{:S(2)}, u32[]{:S(2)}) collective-permute-start(f32[4,128,128]{2,1,0:T(8,128)S(1)} %get-tuple-element.14), channel_id=1, source_target_pairs={{2,0},{3,1},{4,2},{5,3},{6,4},{7,5},{8,6},{9,7},{10,8},{11,9},{12,... | collective-permute-start | bytes 786440 | tf_op jit(solution)/shard_map/ppermute | solution.py:13
  234.2 23.1 %collective-permute-start.32 = (bf16[4,128,128]{2,1,0:T(8,128)(2,1)S(1)}, bf16[4,128,128]{2,1,0:T(8,128)(2,1)S(1)}, u32[]{:S(2)}, u32[]{:S(2)}) collective-permute-start(bf16[4,128,128]{2,1,0:T(8,128)(2,1)S(1)} %get-tuple-element.6), channel_id=1, source_target_pairs={{0,4},{1,5},{2,6},{3,7},{4,8},{5,9},{6,10},{7,11},{8,12},{9,13},{1... | collective-permute-start | bytes 393224 | tf_op jit(solution)/shard_map/ppermute | solution.py:13
  246.7 12.0 %collective-permute-start.33 = (bf16[4,128,128]{2,1,0:T(8,128)(2,1)S(1)}, bf16[4,128,128]{2,1,0:T(8,128)(2,1)S(1)}, u32[]{:S(2)}, u32[]{:S(2)}) collective-permute-start(bf16[4,128,128]{2,1,0:T(8,128)(2,1)S(1)} %get-tuple-element.6), channel_id=1, source_target_pairs={{0,3},{1,4},{2,5},{3,6},{4,7},{5,8},{6,9},{7,10},{8,11},{9,12},{10... | collective-permute-start | bytes 393224 | tf_op jit(solution)/shard_map/ppermute | solution.py:13
  257.4 10.2 %collective-permute-start.37 = (bf16[4,128,128]{2,1,0:T(8,128)(2,1)S(1)}, bf16[4,128,128]{2,1,0:T(8,128)(2,1)S(1)}, u32[]{:S(2)}, u32[]{:S(2)}) collective-permute-start(bf16[4,128,128]{2,1,0:T(8,128)(2,1)S(1)} %get-tuple-element.6), channel_id=1, source_target_pairs={{2,0},{3,1},{4,2},{5,3},{6,4},{7,5},{8,6},{9,7},{10,8},{11,9},{12,... | collective-permute-start | bytes 393224 | tf_op jit(solution)/shard_map/ppermute | solution.py:13
  260.0 13.2 %collective-permute-start.39 = (bf16[4,128,128]{2,1,0:T(8,128)(2,1)S(1)}, bf16[4,128,128]{2,1,0:T(8,128)(2,1)S(1)}, u32[]{:S(2)}, u32[]{:S(2)}) collective-permute-start(bf16[4,128,128]{2,1,0:T(8,128)(2,1)S(1)} %get-tuple-element.6), channel_id=1, source_target_pairs={{4,0},{5,1},{6,2},{7,3},{8,4},{9,5},{10,6},{11,7},{12,8},{13,9},{1... | collective-permute-start | bytes 393224 | tf_op jit(solution)/shard_map/ppermute | solution.py:13
  (19 other events, 174.1 us)
where the time goes:
time: 317 us; the launch traced here: 315 us
  starting transfers between devices  89.3 us (28%)
  waiting for transfers between devices  63.3 us (20%)
  blocking collectives  60.4 us (19%)
  other arithmetic  40 us (13%)
  local copies, waits for them, and re-layouts  29.3 us (9%)
  matrix products  28.4 us (9%)
  between operations  4.06 us (1%)
    ppermute x40, starting transfers between devices, passed_along(): lax.ppermute(value, axis, [(source, source + steps) for source in range(l...  89.3 us
    ppermute x40, waiting for transfers between devices, passed_along(): lax.ppermute(value, axis, [(source, source + steps) for source in range(l...  63.3 us
    psum x2, blocking collectives, on_device(): grad_norm = lax.psum(jnp.sum(gradient * gradient), 'rows')  60.4 us
    scatter-add x2, other arithmetic, adjoint(): window_sums.at[flat_slot]  33.7 us
    reshape x2, local copies, waits for them, and re-layouts, adjoint(): products.reshape(block_rows * slot_count, tile_size, columns)  18.2 us
    dot_general x3, matrix products, predicted_output(): jnp.einsum('bkij,bkjt->bit', response_tiles, panels, preferred_element_ty...  13.8 us
    dot_general x2, matrix products, adjoint(): jnp.einsum('bkij,bit->bkjt', response_tiles, resid_blocks, preferred_elem...  10.7 us
    gather x3, local copies, waits for them, and re-layouts, predicted_output(): window[window_slot]  8.81 us
  transfers between devices with their start and end apart: 40, of which 16 were waited for; matrix products, arithmetic and copies ran while one was open for 2% of the time, Pallas kernels for 0%

commit v1 on v0

v1 whole, which is shorter than its diff:
```python
import functools

import jax
import jax.numpy as jnp
from jax import lax
from jax.experimental import pallas as pl
from jax.experimental.pallas import tpu as pltpu
from jax.sharding import PartitionSpec as P

REACH = 4
ITERS = 2
CHIP_REACH = REACH // 2
WINDOW = 2 * CHIP_REACH + 1
F32 = jnp.float32
BF16 = jnp.bfloat16
VMEM = pl.BlockSpec(memory_space=pltpu.VMEM)
SMEM = pl.BlockSpec(memory_space=pltpu.SMEM)
ANY = pl.BlockSpec(memory_space=pl.ANY)


def hop_offsets(chip):
    near = 1 - 2 * lax.rem(chip, 2)
    far = 2 - 4 * lax.rem(chip // 2, 2)
    return (near, -near, far, -far)


def hop_pairs(ranks):
    chips = ranks // 2
    groups = []
    for step in (1, 2):
        for phase in (0, 1):
            pairs = []
            for chip in range(chips - step):
                if (chip // step) % 2 == phase:
                    for core in (0, 1):
                        low, high = 2 * chip + core, 2 * (chip + step) + core
                        pairs += [(low, high), (high, low)]
            groups.append(pairs)
    return groups


def bounds(lengths, bores):
    upto = lax.broadcasted_iota(jnp.int32, (bores, bores), 1) <= lax.broadcasted_iota(
        jnp.int32, (bores, bores), 0
    )
    ends = jnp.sum(jnp.where(upto, lengths.astype(F32), 0.0), axis=1, keepdims=True)
    here = lax.broadcasted_iota(jnp.int32, (bores, bores), 1) == lax.broadcasted_iota(
        jnp.int32, (bores, bores), 0
    )
    counts = jnp.sum(jnp.where(here, lengths.astype(F32), 0.0), axis=1, keepdims=True)
    return ends, counts


def compress_kernel(me_ref, cols_ref, count_ref, lengths_ref, tiles_hbm, *rest):
    outs = rest[: WINDOW]
    slab, tiles, sems = rest[WINDOW:]
    block_rows, slots, tile = tiles.shape[0], tiles.shape[1], tiles.shape[2]
    bores = slab.shape[1]
    per_chip = 2 * block_rows
    half = slots // 2
    copies = []
    for row in range(block_rows):
        for part in range(2):
            where = pl.ds(part * half, half)
            copy = pltpu.make_async_copy(
                tiles_hbm.at[row, where], tiles.at[row, where], sems.at[row, part]
            )
            copy.start()
            copies.append(copy)
    chip = me_ref[0] // 2
    first_block = (chip - CHIP_REACH) * per_chip
    ends, counts = bounds(lengths_ref[...], bores)
    starts = ends - counts
    slab[...] = jnp.zeros_like(slab)
    for row in range(block_rows):
        position = (
            lax.broadcasted_iota(jnp.int32, (bores, tile), 1) + row * tile
        ).astype(F32)
        members = ((position >= starts) & (position < ends)).astype(F32).astype(BF16)
        used = count_ref[row]
        for part in range(2):
            copies[2 * row + part].wait()
            for slot in range(part * half, part * half + half):
                place = jnp.where(
                    slot < used, cols_ref[row, slot] - first_block, WINDOW * per_chip
                )
                slab[place] += jnp.dot(
                    members, tiles[row, slot], preferred_element_type=F32
                )
    for out, offset in zip(outs, (0,) + hop_offsets(chip)):
        out[...] = slab[pl.ds((offset + CHIP_REACH) * per_chip, per_chip)]


def split(value):
    high = value.astype(BF16)
    return high, (value - high.astype(F32)).astype(BF16)


def gram_kernel(me_ref, *rest):
    mine, other = rest[:WINDOW], rest[WINDOW : 2 * WINDOW]
    heat_mine, heat_other = rest[2 * WINDOW : 2 * WINDOW + 2]
    outs = rest[2 * WINDOW + 2 : 3 * WINDOW + 2]
    high, low, heat, left, shifted = rest[3 * WINDOW + 2 :]
    blocks, bores, tile = mine[0].shape
    chip, core = me_ref[0] // 2, lax.rem(me_ref[0], 2)
    seg_rows = heat_mine.shape[0]
    offsets = (0,) + hop_offsets(chip)
    for pieces, side in ((mine, core), (other, 1 - core)):
        for piece, offset in zip(pieces, offsets):
            at = pl.multiple_of((offset + CHIP_REACH) * 2 * bores + side * bores, bores)
            for block in range(blocks):
                top, rest_of = split(piece[block])
                high[pl.ds(at, bores), block * tile : (block + 1) * tile] = top
                low[pl.ds(at, bores), block * tile : (block + 1) * tile] = rest_of
    heat[pl.ds(pl.multiple_of(core * seg_rows, seg_rows), seg_rows)] = heat_mine[...]
    heat[pl.ds(pl.multiple_of((1 - core) * seg_rows, seg_rows), seg_rows)] = heat_other[...]
    for slot in range(WINDOW):
        at = pl.multiple_of(slot * 2 * bores + core * bores, bores)
        left[slot * bores : (slot + 1) * bores] = high[pl.ds(at, bores)]
        left[(WINDOW + slot) * bores : (WINDOW + slot + 1) * bores] = low[pl.ds(at, bores)]
    rows = WINDOW * bores
    transposed = (((1,), (1,)), ((), ()))
    both = lax.dot_general(left[...], high[...], transposed, preferred_element_type=F32)
    cross = lax.dot_general(left[:rows], low[...], transposed, preferred_element_type=F32)
    gram = both[:rows] + both[rows:] + cross
    warm = jnp.dot(left[...], heat[...], preferred_element_type=F32)
    warm = warm[:rows] + warm[rows:]
    span = 2 * bores
    width = 3 * 2 * span
    lane = lax.broadcasted_iota(jnp.int32, (bores, width), 1)
    padded = jnp.concatenate(
        [gram, jnp.zeros((rows, width - WINDOW * span), F32)], axis=1
    )
    for slot in range(WINDOW):
        offset = slot - CHIP_REACH
        base = padded[slot * bores : (slot + 1) * bores]
        odd = lax.rem(chip + offset + 2, 2)
        places = []
        for parity in (0, 1):
            shift = (CHIP_REACH - offset + parity) * span
            moved = pltpu.roll(base, shift % width, 1) if shift % width else base
            keep = (lane >= shift) & (lane < (WINDOW + parity) * span)
            places.append(jnp.where(keep, moved, 0.0))
        shifted[slot, :, :width] = jnp.where(odd == 1, places[1], places[0])
        shifted[slot, :, width:] = warm[slot * bores : (slot + 1) * bores]
    for out, offset in zip(outs, offsets):
        out[...] = shifted[offset + CHIP_REACH]


def total_kernel(me_ref, lengths_ref, recorded_ref, *rest):
    parts, out = rest[:WINDOW], rest[WINDOW]
    bores, columns = recorded_ref.shape
    width = out.shape[1] - columns
    span = 2 * bores
    odd = lax.rem(me_ref[0] // 2, 2)
    _, counts = bounds(lengths_ref[...], bores)
    total = parts[0][...]
    for part in parts[1:]:
        total = total + part[...]
    lane = lax.broadcasted_iota(jnp.int32, (bores, width), 1)
    free = ((odd == 1) & (lane < span)) | ((odd == 0) & (lane >= WINDOW * span))
    out[:, :width] = jnp.where(free, counts, total[:, :width])
    out[:, width:] = total[:, width:] / counts - recorded_ref[...]


def transpose_kernel(me_ref, *rest):
    mine, other = rest[:WINDOW], rest[WINDOW : 2 * WINDOW]
    high, low = rest[2 * WINDOW : 2 * WINDOW + 2]
    (rows_of,) = rest[2 * WINDOW + 2 :]
    blocks, bores, tile = mine[0].shape
    own_blocks = blocks // 2
    chip, core = me_ref[0] // 2, lax.rem(me_ref[0], 2)
    for pieces, side in ((mine, core), (other, 1 - core)):
        for piece, offset in zip(pieces, (0,) + hop_offsets(chip)):
            at = pl.multiple_of((offset + CHIP_REACH) * 2 * bores + side * bores, bores)
            for block in range(own_blocks):
                rows_of[block, pl.ds(at, bores)] = piece[core * own_blocks + block]
    for block in range(own_blocks):
        top, rest_of = split(rows_of[block].T)
        high[block * tile : (block + 1) * tile] = top
        low[block * tile : (block + 1) * tile] = rest_of


def descend_kernel(ranks, me_ref, heat_ref, high_ref, low_ref, *rest):
    pieces = rest[:ranks]
    heat_out, misfit_out = rest[ranks : ranks + 2]
    lower, band, counts, misfit, warm, shares = rest[ranks + 2 :]
    bores, columns = misfit_out.shape
    width = lower.shape[1]
    plane = 4 * bores
    planes = ranks // 4
    span = 2 * bores
    me = me_ref[0]
    lane = lax.broadcasted_iota(jnp.int32, (bores, width), 1)
    for index, piece in enumerate(pieces):
        rank = jnp.bitwise_xor(me, index)
        at = pl.multiple_of(rank * bores, bores)
        odd = lax.rem(rank // 2, 2) == 1
        count = jnp.where(odd, piece[:, :1], piece[:, width - 1 : width])
        free = (odd & (lane < span)) | (jnp.logical_not(odd) & (lane >= WINDOW * span))
        lower[pl.ds(at, bores)] = jnp.where(free, 0.0, piece[:, :width])
        misfit[pl.ds(at, bores)] = piece[:, width:]
        counts[pl.ds(at, bores)] = jnp.broadcast_to(count, (bores, columns))
    half_row = lax.broadcasted_iota(jnp.int32, (plane, plane), 0) < span
    half_col = lax.broadcasted_iota(jnp.int32, (plane, plane), 1) >= span
    for p in range(planes):
        rows = lower[p * plane : (p + 1) * plane]
        diagonal = rows[:, 2 * plane :]
        diagonal = jnp.where(half_row & half_col, diagonal.T, diagonal)
        after = []
        for step in (1, 2):
            if p + step < planes:
                following = lower[(p + step) * plane : (p + step + 1) * plane]
                after.append(following[:, (2 - step) * plane : (3 - step) * plane].T)
            else:
                after.append(jnp.zeros((plane, plane), F32))
        whole = [rows[:, :plane], rows[:, plane : 2 * plane], diagonal] + after
        for index, part in enumerate(whole):
            top, rest_of = split(part)
            band[p, :plane, index * plane : (index + 1) * plane] = top
            band[p, plane:, index * plane : (index + 1) * plane] = rest_of
    shares[:, : 2 * plane] = jnp.zeros((ITERS, 2 * plane, columns), BF16)
    shares[:, (planes + 2) * plane :] = jnp.zeros((ITERS, 2 * plane, columns), BF16)
    steps = []
    for iteration in range(ITERS):
        shares[iteration, 2 * plane : (planes + 2) * plane] = (
            misfit[...] / counts[...]
        ).astype(BF16)
        power = jnp.zeros((plane, columns), F32)
        curvature = jnp.zeros((plane, columns), F32)
        for p in range(planes):
            both = jnp.dot(
                band[p],
                shares[iteration, p * plane : (p + 5) * plane],
                preferred_element_type=F32,
            )
            swept = both[:plane] + both[plane:]
            here = shares[iteration, (p + 2) * plane : (p + 3) * plane].astype(F32)
            image = swept / counts[p * plane : (p + 1) * plane]
            warm[p * plane : (p + 1) * plane] = image
            power = power + here * swept
            curvature = curvature + image * image
        step = jnp.sum(power) / (jnp.sum(curvature) + 1e-06)
        steps.append(step)
        misfit[...] = misfit[...] - step * warm[...]
    misfit_out[...] = misfit[pl.ds(pl.multiple_of(me * bores, bores), bores)]
    first = pl.multiple_of((me // 2 - CHIP_REACH) * span + 2 * plane, span)
    heat = heat_ref[...]
    for iteration in range(ITERS):
        near = shares[iteration, pl.ds(first, WINDOW * span)]
        gradient = jnp.dot(high_ref[...], near, preferred_element_type=F32) + jnp.dot(
            low_ref[...], near, preferred_element_type=F32
        )
        heat = heat - steps[iteration] * gradient
    heat_out[...] = heat


def on_device(
    ranks, response_tiles, tile_cols, tile_count, heat_start, recorded, bore_lengths
):
    block_rows, slots, tile = response_tiles.shape[:3]
    seg_rows, columns = heat_start.shape
    bores = bore_lengths.shape[1]
    per_chip = 2 * block_rows
    rows = WINDOW * bores
    span = 2 * bores
    width = 6 * span
    me = lax.axis_index("rows").astype(jnp.int32).reshape(1)
    hops = hop_pairs(ranks)
    limit = pltpu.CompilerParams(vmem_limit_bytes=48 << 20)

    def send(value, pairs):
        return lax.ppermute(value, "rows", pairs)

    def swap(value, bit):
        return send(value, [(rank, rank ^ bit) for rank in range(ranks)])

    heat_low = heat_start.astype(BF16)
    heat_other = swap(heat_low, 1)
    piece = jax.ShapeDtypeStruct((per_chip, bores, tile), F32)
    sent = pl.pallas_call(
        compress_kernel,
        out_shape=(piece,) * WINDOW,
        in_specs=[SMEM, SMEM, SMEM, VMEM, ANY],
        out_specs=(VMEM,) * WINDOW,
        scratch_shapes=[
            pltpu.VMEM((WINDOW * per_chip + 1, bores, tile), F32),
            pltpu.VMEM((block_rows, slots, tile, tile), BF16),
            pltpu.SemaphoreType.DMA((block_rows, 2)),
        ],
        compiler_params=limit,
        name="compress",
    )(me, tile_cols, tile_count, bore_lengths, response_tiles)
    mine = [sent[0]] + [send(value, pairs) for value, pairs in zip(sent[1:], hops)]
    other = [swap(value, 1) for value in mine]
    packed = jax.ShapeDtypeStruct((bores, width + columns), F32)
    partial = pl.pallas_call(
        gram_kernel,
        out_shape=(packed,) * WINDOW,
        in_specs=[SMEM] + [VMEM] * (2 * WINDOW + 2),
        out_specs=(VMEM,) * WINDOW,
        scratch_shapes=[
            pltpu.VMEM((WINDOW * span, per_chip * tile), BF16),
            pltpu.VMEM((WINDOW * span, per_chip * tile), BF16),
            pltpu.VMEM((2 * seg_rows, columns), BF16),
            pltpu.VMEM((2 * rows, per_chip * tile), BF16),
            pltpu.VMEM((WINDOW, bores, width + columns), F32),
        ],
        compiler_params=limit,
        name="gram",
    )(me, *mine, *other, heat_low, heat_other)
    parts = [partial[0]] + [send(value, pairs) for value, pairs in zip(partial[1:], hops)]
    turned = jax.ShapeDtypeStruct((seg_rows, WINDOW * span), BF16)
    high, low = pl.pallas_call(
        transpose_kernel,
        out_shape=(turned, turned),
        in_specs=[SMEM] + [VMEM] * (2 * WINDOW),
        out_specs=(VMEM, VMEM),
        scratch_shapes=[pltpu.VMEM((block_rows, WINDOW * span, tile), F32)],
        compiler_params=limit,
        name="turn",
    )(me, *mine, *other)
    total = pl.pallas_call(
        total_kernel,
        out_shape=packed,
        in_specs=[SMEM] + [VMEM] * (2 + WINDOW),
        out_specs=VMEM,
        name="total",
    )(me, bore_lengths, recorded, *parts)
    gathered = [total] + [None] * (ranks - 1)
    known = [0]
    direct = [index for index in range(4, min(ranks, 16), 4)]
    for index in direct:
        gathered[index] = swap(total, index)
    known += direct
    bit = 16
    order = []
    while bit < ranks:
        order.append(bit)
        bit *= 2
    for bit in order + [2, 1]:
        for index in list(known):
            gathered[index ^ bit] = swap(gathered[index], bit)
            known.append(index ^ bit)
    return pl.pallas_call(
        functools.partial(descend_kernel, ranks),
        out_shape=(
            jax.ShapeDtypeStruct((seg_rows, columns), F32),
            jax.ShapeDtypeStruct((bores, columns), F32),
        ),
        in_specs=[SMEM] + [VMEM] * (3 + ranks),
        out_specs=(VMEM, VMEM),
        scratch_shapes=[
            pltpu.VMEM((ranks * bores, width), F32),
            pltpu.VMEM((ranks // 4, 8 * bores, 20 * bores), BF16),
            pltpu.VMEM((ranks * bores, columns), F32),
            pltpu.VMEM((ranks * bores, columns), F32),
            pltpu.VMEM((ranks * bores, columns), F32),
            pltpu.VMEM((ITERS, (ranks + 16) * bores, columns), BF16),
        ],
        compiler_params=limit,
        name="descend",
    )(me, heat_start, high, low, *gathered)


def solution(mesh):
    placed = (
        P(("groups", "rows"), None, None, None),
        P(("groups", "rows"), None),
        P(("groups", "rows")),
        P(("groups", "rows"), None),
        P(("groups", "rows"), None),
        P(("groups", "rows"), None),
    )
    return jax.shard_map(
        functools.partial(on_device, mesh.shape["rows"]),
        mesh=mesh,
        in_specs=placed,
        out_specs=(P(("groups", "rows"), None), P(("groups", "rows"), None)),
        check_vma=False,
    )
```

time: 317 us -> 61 us (0.19)
  starting transfers between devices: 89.3 us -> 27.3 us
  blocking collectives: 60.4 us -> 0 us
  waiting for transfers between devices: 63.3 us -> 13.9 us
  other arithmetic: 40 us -> 1.03 us
  matrix products: 28.4 us -> 0 us
  local copies, waits for them, and re-layouts: 29.3 us -> 6.21 us
  Pallas kernels: 0 us -> 11.3 us
  between operations: 4.06 us -> 0.83 us
    ppermute x40 -> x29, starting transfers between devices: 89.3 us -> 27.3 us  [send(): return lax.ppermute(value, 'rows', pairs)]
    psum x2 -> x0, blocking collectives: 60.4 us -> none  [on_device(): grad_norm = lax.psum(jnp.sum(gradient * gradient), 'rows')]
    ppermute x40 -> x29, waiting for transfers between devices: 63.3 us -> 13.9 us  [send(): return lax.ppermute(value, 'rows', pairs)]
    scatter-add x2 -> x0, other arithmetic: 33.7 us -> none  [adjoint(): window_sums.at[flat_slot]]
    dot_general x12 -> x0, matrix products: 28.4 us -> none  [the longest x3 13.8 us: predicted_output(): jnp.einsum('bkij,bkjt->bit', response_tiles, panels, preferred_element_ty...]
    reshape x3 -> x0, local copies, waits for them, and re-layouts: 18.2 us -> none  [the longest x2 18.2 us: adjoint(): products.reshape(block_rows * slot_count, tile_size, columns)]
    pallas_call x0 -> x5, Pallas kernels: none -> 11.3 us  [the longest x1 5.31 us: on_device(): pl.pallas_call(compress_kernel, out_shape=(piece,) * WINDOW, in_specs=[SM...]
    gather x3 -> x0, local copies, waits for them, and re-layouts: 8.81 us -> none  [predicted_output(): window[window_slot]]
  transfers between devices with their start and end apart: 40 -> 29, of which waited for: 16 -> 9; matrix products, arithmetic and copies ran while one was open for 2% -> 0% of each run, Pallas kernels for 0% -> 9%
where the time goes in v1:
time: 61 us; the launch traced here: 60.6 us
  starting transfers between devices  27.3 us (45%)
  waiting for transfers between devices  13.9 us (23%)
  Pallas kernels  11.3 us (19%)
  local copies, waits for them, and re-layouts  6.21 us (10%)
  other arithmetic  1.03 us (2%)
  between operations  0.83 us (1%)
    ppermute x29, starting transfers between devices, send(): return lax.ppermute(value, 'rows', pairs)  27.3 us
    ppermute x29, waiting for transfers between devices, send(): return lax.ppermute(value, 'rows', pairs)  13.9 us
    unnamed x22, local copies, waits for them, and re-layouts  6.21 us
    pallas_call x1, Pallas kernels, on_device(): pl.pallas_call(compress_kernel, out_shape=(piece,) * WINDOW, in_specs=[SM...  5.31 us
    pallas_call x1, Pallas kernels, on_device(): pl.pallas_call(functools.partial(descend_kernel, ranks), out_shape=(jax.S...  2.74 us
    pallas_call x1, Pallas kernels, on_device(): pl.pallas_call(total_kernel, out_shape=packed, in_specs=[SMEM] + [VMEM] *...  1.72 us
    pallas_call x1, Pallas kernels, on_device(): pl.pallas_call(gram_kernel, out_shape=(packed,) * WINDOW, in_specs=[SMEM]...  1.24 us
  transfers between devices with their start and end apart: 29, of which 9 were waited for; matrix products, arithmetic and copies ran while one was open for 0% of the time, Pallas kernels for 9%

profile of v1, /device:TPU:0, one launch (start us, length us, event | category | flops | bytes accessed | tf_op | source)
XLA Modules:
  0.0 60.6 jit_solution(7096725383627420269)
XLA Ops:
  0.6 1.0 %convert_element_type.3.rest_10_ = bf16[512,128]{1,0:T(8,128)(2,1)S(1)} convert(f32[512,128]{1,0:T(8,128)} %heat_ref.1) | non-fusion elementwise | flops 65536 | bytes 393216 | tf_op jit(solution)/shard_map/convert_element_type | solution.py:278
  2.2 2.1 %copy-done = bf16[4,30,128,128]{3,2,1,0:T(8,128)(2,1)S(1)} copy-done((bf16[4,30,128,128]{3,2,1,0:T(8,128)(2,1)S(1)}, bf16[4,30,128,128]{3,2,1,0:T(8,128)(2,1)}, u32[]{:S(2)}) %copy-start) | copy-done | bytes 3932184
  6.3 5.3 %compress.1 = (f32[8,32,128]{2,1,0:T(8,128)S(1)}, f32[8,32,128]{2,1,0:T(8,128)S(1)}, f32[8,32,128]{2,1,0:T(8,128)S(1)}, f32[8,32,128]{2,1,0:T(8,128)S(1)}, f32[8,32,128]{2,1,0:T(8,128)S(1)}) custom-call(s32[1]{0:T(128)} %bitcast.me_ref, s32[4,30]{1,0:T(4,128)S(1)} %copy-done.4, s32[4]{0:T(128)S(1)} %copy-done.6, s32[1,32]{1,0:T(1,128)S(1)} %copy-done.5, ...), custom_call_target="tpu_custom_call" | custom-call | tf_op jit(solution)/shard_map/compress/pallas_call | solution.py:281
  11.6 2.6 %collective-permute-start = (f32[8,32,128]{2,1,0:T(8,128)S(1)}, f32[8,32,128]{2,1,0:T(8,128)S(1)}, u32[]{:S(2)}, u32[]{:S(2)}) collective-permute-start(f32[8,32,128]{2,1,0:T(8,128)S(1)} %get-tuple-element.15), channel_id=1, source_target_pairs={{0,2},{2,0},{1,3},{3,1},{4,6},{6,4},{5,7},{7,5},{8,10},{10,8},{9,1... | collective-permute-start | bytes 393224 | tf_op jit(solution)/shard_map/ppermute | solution.py:273
  14.8 2.9 %collective-permute-start.2 = (f32[8,32,128]{2,1,0:T(8,128)S(1)}, f32[8,32,128]{2,1,0:T(8,128)S(1)}, u32[]{:S(2)}, u32[]{:S(2)}) collective-permute-start(f32[8,32,128]{2,1,0:T(8,128)S(1)} %get-tuple-element.17), channel_id=1, source_target_pairs={{0,4},{4,0},{1,5},{5,1},{2,6},{6,2},{3,7},{7,3},{8,12},{12,8},{9,1... | collective-permute-start | bytes 393224 | tf_op jit(solution)/shard_map/ppermute | solution.py:273
  19.1 5.2 %collective-permute-done.2.rest_3_ = f32[8,32,128]{2,1,0:T(8,128)S(1)} collective-permute-done((f32[8,32,128]{2,1,0:T(8,128)S(1)}, f32[8,32,128]{2,1,0:T(8,128)S(1)}, u32[]{:S(2)}, u32[]{:S(2)}) %collective-permute-start.2) | collective-permute-done | bytes 131104 | tf_op jit(solution)/shard_map/ppermute | solution.py:273
  24.9 0.8 %collective-permute-done.7.rest_8_ = f32[8,32,128]{2,1,0:T(8,128)S(1)} collective-permute-done((f32[8,32,128]{2,1,0:T(8,128)S(1)}, f32[8,32,128]{2,1,0:T(8,128)S(1)}, u32[]{:S(2)}, u32[]{:S(2)}) %collective-permute-start.7) | collective-permute-done | bytes 131104 | tf_op jit(solution)/shard_map/ppermute | solution.py:273
  25.9 1.2 %gram.1 = (f32[32,512]{1,0:T(8,128)S(1)}, f32[32,512]{1,0:T(8,128)S(1)}, f32[32,512]{1,0:T(8,128)S(1)}, f32[32,512]{1,0:T(8,128)S(1)}, f32[32,512]{1,0:T(8,128)S(1)}) custom-call(s32[1]{0:T(128)} %bitcast.me_ref, f32[8,32,128]{2,1,0:T(8,128)S(1)} %get-tuple-element.14.rest_0_, f32[8,32,128]{2,1,0:T(8,128)S(1)} %collective-permute-done.rest_1_, ...), custom_call_target="tpu_custom_call" | custom-call | tf_op jit(solution)/shard_map/gram/pallas_call | solution.py:297
  27.7 0.7 %collective-permute-start.10 = (f32[32,512]{1,0:T(8,128)S(1)}, f32[32,512]{1,0:T(8,128)S(1)}, u32[]{:S(2)}, u32[]{:S(2)}) collective-permute-start(f32[32,512]{1,0:T(8,128)S(1)} %get-tuple-element.22), channel_id=1, source_target_pairs={{0,2},{2,0},{1,3},{3,1},{4,6},{6,4},{5,7},{7,5},{8,10},{10,8},{9,1... | collective-permute-start | bytes 196616 | tf_op jit(solution)/shard_map/ppermute | solution.py:273
  29.1 4.2 %collective-permute-start.12 = (f32[32,512]{1,0:T(8,128)S(1)}, f32[32,512]{1,0:T(8,128)S(1)}, u32[]{:S(2)}, u32[]{:S(2)}) collective-permute-start(f32[32,512]{1,0:T(8,128)S(1)} %get-tuple-element.24), channel_id=1, source_target_pairs={{0,4},{4,0},{1,5},{5,1},{2,6},{6,2},{3,7},{7,3},{8,12},{12,8},{9,1... | collective-permute-start | bytes 196616 | tf_op jit(solution)/shard_map/ppermute | solution.py:273
  34.1 2.7 %collective-permute-done.12.rest_3_ = f32[32,512]{1,0:T(8,128)S(1)} collective-permute-done((f32[32,512]{1,0:T(8,128)S(1)}, f32[32,512]{1,0:T(8,128)S(1)}, u32[]{:S(2)}, u32[]{:S(2)}) %collective-permute-start.12) | collective-permute-done | bytes 65568 | tf_op jit(solution)/shard_map/ppermute | solution.py:273
  37.4 1.7 %total.1.rest_0_ = f32[32,512]{1,0:T(8,128)} custom-call(s32[1]{0:T(128)} %bitcast.me_ref, s32[1,32]{1,0:T(1,128)} %lengths_ref.3, f32[32,128]{1,0:T(8,128)} %recorded_ref.1, f32[32,512]{1,0:T(8,128)} %copy-done.3, f32[32,512]{1,0:T(8,128)} %copy-done.7, f32[32,512]{1,0:T(8,128)} %copy-done.8, f32[32,512]{1,0:T(8,128)} %copy-done.9, f32[32,512]{1,0:T(8,128)} %copy-done.10), custom_call_target="tpu_custom_call" | custom-call | tf_op jit(solution)/shard_map/total/pallas_call | solution.py:323
  39.2 3.7 %collective-permute-start.25 = (f32[32,512]{1,0:T(8,128)}, f32[32,512]{1,0:T(8,128)S(1)}, u32[]{:S(2)}, u32[]{:S(2)}) collective-permute-start(f32[32,512]{1,0:T(8,128)} %total.1.rest_0_), channel_id=1, source_target_pairs={{0,12},{1,13},{2,14},{3,15},{4,8},{5,9},{6,10},{7,11},{8,4},{9,5},... | collective-permute-start | bytes 196616 | tf_op jit(solution)/shard_map/ppermute | solution.py:273
  42.9 2.0 %collective-permute-start.21 = (f32[32,512]{1,0:T(8,128)}, f32[32,512]{1,0:T(8,128)S(1)}, u32[]{:S(2)}, u32[]{:S(2)}) collective-permute-start(f32[32,512]{1,0:T(8,128)} %total.1.rest_0_), channel_id=1, source_target_pairs={{0,8},{1,9},{2,10},{3,11},{4,12},{5,13},{6,14},{7,15},{8,0},{9,1},... | collective-permute-start | bytes 196616 | tf_op jit(solution)/shard_map/ppermute | solution.py:273
  45.4 1.4 %collective-permute-start.15 = (f32[32,512]{1,0:T(8,128)}, f32[32,512]{1,0:T(8,128)S(1)}, u32[]{:S(2)}, u32[]{:S(2)}) collective-permute-start(f32[32,512]{1,0:T(8,128)} %total.1.rest_0_), channel_id=1, source_target_pairs={{0,2},{1,3},{2,0},{3,1},{4,6},{5,7},{6,4},{7,5},{8,10},{9,11},{10,... | collective-permute-start | bytes 196616 | tf_op jit(solution)/shard_map/ppermute | solution.py:273
  46.8 1.3 %collective-permute-start.27 = (f32[32,512]{1,0:T(8,128)S(1)}, f32[32,512]{1,0:T(8,128)S(1)}, u32[]{:S(2)}, u32[]{:S(2)}) collective-permute-start(f32[32,512]{1,0:T(8,128)S(1)} %collective-permute-done.25.rest_12_), channel_id=1, source_target_pairs={{0,2},{1,3},{2,0},{3,1},{4,6},{5,7},{6,4},{7,5},{8,10},{9,11},{10,... | collective-permute-start | bytes 196616 | tf_op jit(solution)/shard_map/ppermute | solution.py:273
  48.5 0.8 %collective-permute-done.17.rest_4_ = f32[32,512]{1,0:T(8,128)S(1)} collective-permute-done((f32[32,512]{1,0:T(8,128)}, f32[32,512]{1,0:T(8,128)S(1)}, u32[]{:S(2)}, u32[]{:S(2)}) %collective-permute-start.17) | collective-permute-done | bytes 65568 | tf_op jit(solution)/shard_map/ppermute | solution.py:273
  49.3 1.9 %collective-permute-start.23 = (f32[32,512]{1,0:T(8,128)S(1)}, f32[32,512]{1,0:T(8,128)S(1)}, u32[]{:S(2)}, u32[]{:S(2)}) collective-permute-start(f32[32,512]{1,0:T(8,128)S(1)} %collective-permute-done.21.rest_8_), channel_id=1, source_target_pairs={{0,2},{1,3},{2,0},{3,1},{4,6},{5,7},{6,4},{7,5},{8,10},{9,11},{10,... | collective-permute-start | bytes 196616 | tf_op jit(solution)/shard_map/ppermute | solution.py:273
  51.3 0.7 %collective-permute-start.19 = (f32[32,512]{1,0:T(8,128)S(1)}, f32[32,512]{1,0:T(8,128)S(1)}, u32[]{:S(2)}, u32[]{:S(2)}) collective-permute-start(f32[32,512]{1,0:T(8,128)S(1)} %collective-permute-done.17.rest_4_), channel_id=1, source_target_pairs={{0,2},{1,3},{2,0},{3,1},{4,6},{5,7},{6,4},{7,5},{8,10},{9,11},{10,... | collective-permute-start | bytes 196616 | tf_op jit(solution)/shard_map/ppermute | solution.py:273
  52.5 1.1 %collective-permute-done.23.rest_10_ = f32[32,512]{1,0:T(8,128)S(1)} collective-permute-done((f32[32,512]{1,0:T(8,128)S(1)}, f32[32,512]{1,0:T(8,128)S(1)}, u32[]{:S(2)}, u32[]{:S(2)}) %collective-permute-start.23) | collective-permute-done | bytes 65568 | tf_op jit(solution)/shard_map/ppermute | solution.py:273
  54.1 1.7 %collective-permute-done.19.rest_6_ = f32[32,512]{1,0:T(8,128)S(1)} collective-permute-done((f32[32,512]{1,0:T(8,128)S(1)}, f32[32,512]{1,0:T(8,128)S(1)}, u32[]{:S(2)}, u32[]{:S(2)}) %collective-permute-start.19) | collective-permute-done | bytes 65568 | tf_op jit(solution)/shard_map/ppermute | solution.py:273
  56.2 0.9 %collective-permute-done.20.rest_7_ = f32[32,512]{1,0:T(8,128)S(1)} collective-permute-done((f32[32,512]{1,0:T(8,128)S(1)}, f32[32,512]{1,0:T(8,128)S(1)}, u32[]{:S(2)}, u32[]{:S(2)}) %collective-permute-start.20) | collective-permute-done | bytes 65568 | tf_op jit(solution)/shard_map/ppermute | solution.py:273
  57.0 0.8 %copy-done.2 = f32[32,512]{1,0:T(8,128)S(1)} copy-done((f32[32,512]{1,0:T(8,128)S(1)}, f32[32,512]{1,0:T(8,128)}, u32[]{:S(2)}) %copy-start.2) | copy-done | bytes 65560
  57.9 2.7 %descend.1 = (f32[512,128]{1,0:T(8,128)}, f32[32,128]{1,0:T(8,128)}) custom-call(s32[1]{0:T(128)} %bitcast.me_ref, f32[512,128]{1,0:T(8,128)S(1)} %copy-done.1, bf16[512,320]{1,0:T(8,128)(2,1)S(1)} %get-tuple-element.19.high_ref, bf16[512,320]{1,0:T(8,128)(2,1)S(1)} %get-tuple-element.20.low_ref, f32[32,512]{1,0:T(8,128)S(1)} %copy-done.2, ...), custom_call_target="tpu_custom_call" | custom-call | tf_op jit(solution)/shard_map/descend/pallas_call | solution.py:345
  (62 shorter events, 10.1 us)
Async XLA Ops:
  1.7 16.7 %collective-permute-start.9 = (bf16[512,128]{1,0:T(8,128)(2,1)S(1)}, bf16[512,128]{1,0:T(8,128)(2,1)S(1)}, u32[]{:S(2)}, u32[]{:S(2)}) collective-permute-start(bf16[512,128]{1,0:T(8,128)(2,1)S(1)} %convert_element_type.3.rest_10_), channel_id=1, source_target_pairs={{0,1},{1,0},{2,3},{3,2},{4,5},{5,4},{6,7},{7,6},{8,9},{9,8},{10,11... | collective-permute-start | bytes 393224 | tf_op jit(solution)/shard_map/ppermute | solution.py:273
  11.6 6.9 %collective-permute-start = (f32[8,32,128]{2,1,0:T(8,128)S(1)}, f32[8,32,128]{2,1,0:T(8,128)S(1)}, u32[]{:S(2)}, u32[]{:S(2)}) collective-permute-start(f32[8,32,128]{2,1,0:T(8,128)S(1)} %get-tuple-element.15), channel_id=1, source_target_pairs={{0,2},{2,0},{1,3},{3,1},{4,6},{6,4},{5,7},{7,5},{8,10},{10,8},{9,1... | collective-permute-start | bytes 393224 | tf_op jit(solution)/shard_map/ppermute | solution.py:273
  14.2 4.8 %collective-permute-start.1 = (f32[8,32,128]{2,1,0:T(8,128)S(1)}, f32[8,32,128]{2,1,0:T(8,128)S(1)}, u32[]{:S(2)}, u32[]{:S(2)}) collective-permute-start(f32[8,32,128]{2,1,0:T(8,128)S(1)} %get-tuple-element.16), channel_id=1, source_target_pairs={{2,4},{4,2},{3,5},{5,3},{6,8},{8,6},{7,9},{9,7},{10,12},{12,10},{1... | collective-permute-start | bytes 393224 | tf_op jit(solution)/shard_map/ppermute | solution.py:273
  14.8 9.5 %collective-permute-start.2 = (f32[8,32,128]{2,1,0:T(8,128)S(1)}, f32[8,32,128]{2,1,0:T(8,128)S(1)}, u32[]{:S(2)}, u32[]{:S(2)}) collective-permute-start(f32[8,32,128]{2,1,0:T(8,128)S(1)} %get-tuple-element.17), channel_id=1, source_target_pairs={{0,4},{4,0},{1,5},{5,1},{2,6},{6,2},{3,7},{7,3},{8,12},{12,8},{9,1... | collective-permute-start | bytes 393224 | tf_op jit(solution)/shard_map/ppermute | solution.py:273
  17.7 6.6 %collective-permute-start.3 = (f32[8,32,128]{2,1,0:T(8,128)S(1)}, f32[8,32,128]{2,1,0:T(8,128)S(1)}, u32[]{:S(2)}, u32[]{:S(2)}) collective-permute-start(f32[8,32,128]{2,1,0:T(8,128)S(1)} %get-tuple-element.18), channel_id=1, source_target_pairs={{4,8},{8,4},{5,9},{9,5},{6,10},{10,6},{7,11},{11,7},{20,24},{24,20... | collective-permute-start | bytes 393224 | tf_op jit(solution)/shard_map/ppermute | solution.py:273
  18.4 6.4 %collective-permute-start.4 = (f32[8,32,128]{2,1,0:T(8,128)S(1)}, f32[8,32,128]{2,1,0:T(8,128)S(1)}, u32[]{:S(2)}, u32[]{:S(2)}) collective-permute-start(f32[8,32,128]{2,1,0:T(8,128)S(1)} %get-tuple-element.14.rest_0_), channel_id=1, source_target_pairs={{0,1},{1,0},{2,3},{3,2},{4,5},{5,4},{6,7},{7,6},{8,9},{9,8},{10,11... | collective-permute-start | bytes 393224 | tf_op jit(solution)/shard_map/ppermute | solution.py:273
  18.5 6.3 %collective-permute-start.5 = (f32[8,32,128]{2,1,0:T(8,128)S(1)}, f32[8,32,128]{2,1,0:T(8,128)S(1)}, u32[]{:S(2)}, u32[]{:S(2)}) collective-permute-start(f32[8,32,128]{2,1,0:T(8,128)S(1)} %collective-permute-done.rest_1_), channel_id=1, source_target_pairs={{0,1},{1,0},{2,3},{3,2},{4,5},{5,4},{6,7},{7,6},{8,9},{9,8},{10,11... | collective-permute-start | bytes 393224 | tf_op jit(solution)/shard_map/ppermute | solution.py:273
  19.0 5.9 %collective-permute-start.6 = (f32[8,32,128]{2,1,0:T(8,128)S(1)}, f32[8,32,128]{2,1,0:T(8,128)S(1)}, u32[]{:S(2)}, u32[]{:S(2)}) collective-permute-start(f32[8,32,128]{2,1,0:T(8,128)S(1)} %collective-permute-done.1.rest_2_), channel_id=1, source_target_pairs={{0,1},{1,0},{2,3},{3,2},{4,5},{5,4},{6,7},{7,6},{8,9},{9,8},{10,11... | collective-permute-start | bytes 393224 | tf_op jit(solution)/shard_map/ppermute | solution.py:273
  27.7 6.3 %collective-permute-start.10 = (f32[32,512]{1,0:T(8,128)S(1)}, f32[32,512]{1,0:T(8,128)S(1)}, u32[]{:S(2)}, u32[]{:S(2)}) collective-permute-start(f32[32,512]{1,0:T(8,128)S(1)} %get-tuple-element.22), channel_id=1, source_target_pairs={{0,2},{2,0},{1,3},{3,1},{4,6},{6,4},{5,7},{7,5},{8,10},{10,8},{9,1... | collective-permute-start | bytes 196616 | tf_op jit(solution)/shard_map/ppermute | solution.py:273
  28.5 5.6 %collective-permute-start.11 = (f32[32,512]{1,0:T(8,128)S(1)}, f32[32,512]{1,0:T(8,128)S(1)}, u32[]{:S(2)}, u32[]{:S(2)}) collective-permute-start(f32[32,512]{1,0:T(8,128)S(1)} %get-tuple-element.23), channel_id=1, source_target_pairs={{2,4},{4,2},{3,5},{5,3},{6,8},{8,6},{7,9},{9,7},{10,12},{12,10},{1... | collective-permute-start | bytes 196616 | tf_op jit(solution)/shard_map/ppermute | solution.py:273
  29.1 7.7 %collective-permute-start.12 = (f32[32,512]{1,0:T(8,128)S(1)}, f32[32,512]{1,0:T(8,128)S(1)}, u32[]{:S(2)}, u32[]{:S(2)}) collective-permute-start(f32[32,512]{1,0:T(8,128)S(1)} %get-tuple-element.24), channel_id=1, source_target_pairs={{0,4},{4,0},{1,5},{5,1},{2,6},{6,2},{3,7},{7,3},{8,12},{12,8},{9,1... | collective-permute-start | bytes 196616 | tf_op jit(solution)/shard_map/ppermute | solution.py:273
  33.4 3.4 %collective-permute-start.13 = (f32[32,512]{1,0:T(8,128)S(1)}, f32[32,512]{1,0:T(8,128)S(1)}, u32[]{:S(2)}, u32[]{:S(2)}) collective-permute-start(f32[32,512]{1,0:T(8,128)S(1)} %get-tuple-element.25), channel_id=1, source_target_pairs={{4,8},{8,4},{5,9},{9,5},{6,10},{10,6},{7,11},{11,7},{20,24},{24,20... | collective-permute-start | bytes 196616 | tf_op jit(solution)/shard_map/ppermute | solution.py:273
  39.2 7.6 %collective-permute-start.25 = (f32[32,512]{1,0:T(8,128)}, f32[32,512]{1,0:T(8,128)S(1)}, u32[]{:S(2)}, u32[]{:S(2)}) collective-permute-start(f32[32,512]{1,0:T(8,128)} %total.1.rest_0_), channel_id=1, source_target_pairs={{0,12},{1,13},{2,14},{3,15},{4,8},{5,9},{6,10},{7,11},{8,4},{9,5},... | collective-permute-start | bytes 196616 | tf_op jit(solution)/shard_map/ppermute | solution.py:273
  42.9 5.7 %collective-permute-start.21 = (f32[32,512]{1,0:T(8,128)}, f32[32,512]{1,0:T(8,128)S(1)}, u32[]{:S(2)}, u32[]{:S(2)}) collective-permute-start(f32[32,512]{1,0:T(8,128)} %total.1.rest_0_), channel_id=1, source_target_pairs={{0,8},{1,9},{2,10},{3,11},{4,12},{5,13},{6,14},{7,15},{8,0},{9,1},... | collective-permute-start | bytes 196616 | tf_op jit(solution)/shard_map/ppermute | solution.py:273
  44.9 4.5 %collective-permute-start.17 = (f32[32,512]{1,0:T(8,128)}, f32[32,512]{1,0:T(8,128)S(1)}, u32[]{:S(2)}, u32[]{:S(2)}) collective-permute-start(f32[32,512]{1,0:T(8,128)} %total.1.rest_0_), channel_id=1, source_target_pairs={{0,4},{1,5},{2,6},{3,7},{4,0},{5,1},{6,2},{7,3},{8,12},{9,13},{10,... | collective-permute-start | bytes 196616 | tf_op jit(solution)/shard_map/ppermute | solution.py:273
  45.4 5.9 %collective-permute-start.15 = (f32[32,512]{1,0:T(8,128)}, f32[32,512]{1,0:T(8,128)S(1)}, u32[]{:S(2)}, u32[]{:S(2)}) collective-permute-start(f32[32,512]{1,0:T(8,128)} %total.1.rest_0_), channel_id=1, source_target_pairs={{0,2},{1,3},{2,0},{3,1},{4,6},{5,7},{6,4},{7,5},{8,10},{9,11},{10,... | collective-permute-start | bytes 196616 | tf_op jit(solution)/shard_map/ppermute | solution.py:273
  46.8 4.5 %collective-permute-start.14 = (f32[32,512]{1,0:T(8,128)}, f32[32,512]{1,0:T(8,128)S(1)}, u32[]{:S(2)}, u32[]{:S(2)}) collective-permute-start(f32[32,512]{1,0:T(8,128)} %total.1.rest_0_), channel_id=1, source_target_pairs={{0,1},{1,0},{2,3},{3,2},{4,5},{5,4},{6,7},{7,6},{8,9},{9,8},{10,11... | collective-permute-start | bytes 196616 | tf_op jit(solution)/shard_map/ppermute | solution.py:273
  46.8 5.2 %collective-permute-start.27 = (f32[32,512]{1,0:T(8,128)S(1)}, f32[32,512]{1,0:T(8,128)S(1)}, u32[]{:S(2)}, u32[]{:S(2)}) collective-permute-start(f32[32,512]{1,0:T(8,128)S(1)} %collective-permute-done.25.rest_12_), channel_id=1, source_target_pairs={{0,2},{1,3},{2,0},{3,1},{4,6},{5,7},{6,4},{7,5},{8,10},{9,11},{10,... | collective-permute-start | bytes 196616 | tf_op jit(solution)/shard_map/ppermute | solution.py:273
  48.5 3.7 %collective-permute-start.26 = (f32[32,512]{1,0:T(8,128)S(1)}, f32[32,512]{1,0:T(8,128)S(1)}, u32[]{:S(2)}, u32[]{:S(2)}) collective-permute-start(f32[32,512]{1,0:T(8,128)S(1)} %collective-permute-done.25.rest_12_), channel_id=1, source_target_pairs={{0,1},{1,0},{2,3},{3,2},{4,5},{5,4},{6,7},{7,6},{8,9},{9,8},{10,11... | collective-permute-start | bytes 196616 | tf_op jit(solution)/shard_map/ppermute | solution.py:273
  49.3 4.3 %collective-permute-start.23 = (f32[32,512]{1,0:T(8,128)S(1)}, f32[32,512]{1,0:T(8,128)S(1)}, u32[]{:S(2)}, u32[]{:S(2)}) collective-permute-start(f32[32,512]{1,0:T(8,128)S(1)} %collective-permute-done.21.rest_8_), channel_id=1, source_target_pairs={{0,2},{1,3},{2,0},{3,1},{4,6},{5,7},{6,4},{7,5},{8,10},{9,11},{10,... | collective-permute-start | bytes 196616 | tf_op jit(solution)/shard_map/ppermute | solution.py:273
  51.3 4.5 %collective-permute-start.19 = (f32[32,512]{1,0:T(8,128)S(1)}, f32[32,512]{1,0:T(8,128)S(1)}, u32[]{:S(2)}, u32[]{:S(2)}) collective-permute-start(f32[32,512]{1,0:T(8,128)S(1)} %collective-permute-done.17.rest_4_), channel_id=1, source_target_pairs={{0,2},{1,3},{2,0},{3,1},{4,6},{5,7},{6,4},{7,5},{8,10},{9,11},{10,... | collective-permute-start | bytes 196616 | tf_op jit(solution)/shard_map/ppermute | solution.py:273
  52.0 4.2 %collective-permute-start.18 = (f32[32,512]{1,0:T(8,128)S(1)}, f32[32,512]{1,0:T(8,128)S(1)}, u32[]{:S(2)}, u32[]{:S(2)}) collective-permute-start(f32[32,512]{1,0:T(8,128)S(1)} %collective-permute-done.17.rest_4_), channel_id=1, source_target_pairs={{0,1},{1,0},{2,3},{3,2},{4,5},{5,4},{6,7},{7,6},{8,9},{9,8},{10,11... | collective-permute-start | bytes 196616 | tf_op jit(solution)/shard_map/ppermute | solution.py:273
  52.2 3.9 %collective-permute-start.16 = (f32[32,512]{1,0:T(8,128)S(1)}, f32[32,512]{1,0:T(8,128)S(1)}, u32[]{:S(2)}, u32[]{:S(2)}) collective-permute-start(f32[32,512]{1,0:T(8,128)S(1)} %collective-permute-done.15.rest_2_), channel_id=1, source_target_pairs={{0,1},{1,0},{2,3},{3,2},{4,5},{5,4},{6,7},{7,6},{8,9},{9,8},{10,11... | collective-permute-start | bytes 196616 | tf_op jit(solution)/shard_map/ppermute | solution.py:273
  53.6 2.5 %collective-permute-start.24 = (f32[32,512]{1,0:T(8,128)S(1)}, f32[32,512]{1,0:T(8,128)S(1)}, u32[]{:S(2)}, u32[]{:S(2)}) collective-permute-start(f32[32,512]{1,0:T(8,128)S(1)} %collective-permute-done.23.rest_10_), channel_id=1, source_target_pairs={{0,1},{1,0},{2,3},{3,2},{4,5},{5,4},{6,7},{7,6},{8,9},{9,8},{10,11... | collective-permute-start | bytes 196616 | tf_op jit(solution)/shard_map/ppermute | solution.py:273
  (16 other events, 77.8 us)

commit v2 on v1

--- a/solution.py
+++ b/solution.py
@@ -14,28 +14,26 @@
 F32 = jnp.float32
 BF16 = jnp.bfloat16
 VMEM = pl.BlockSpec(memory_space=pltpu.VMEM)
-SMEM = pl.BlockSpec(memory_space=pltpu.SMEM)
-ANY = pl.BlockSpec(memory_space=pl.ANY)
+HBM = pl.BlockSpec(memory_space=pltpu.HBM)
 
 
 def hop_offsets(chip):
     near = 1 - 2 * lax.rem(chip, 2)
     far = 2 - 4 * lax.rem(chip // 2, 2)
-    return (near, -near, far, -far)
+    return (-near, -far, far, near)
 
 
 def hop_pairs(ranks):
     chips = ranks // 2
     groups = []
-    for step in (1, 2):
-        for phase in (0, 1):
-            pairs = []
-            for chip in range(chips - step):
-                if (chip // step) % 2 == phase:
-                    for core in (0, 1):
-                        low, high = 2 * chip + core, 2 * (chip + step) + core
-                        pairs += [(low, high), (high, low)]
-            groups.append(pairs)
+    for step, phase in ((1, 1), (2, 1), (2, 0), (1, 0)):
+        pairs = []
+        for chip in range(chips - step):
+            if (chip // step) % 2 == phase:
+                for core in (0, 1):
+                    low, high = 2 * chip + core, 2 * (chip + step) + core
+                    pairs += [(low, high), (high, low)]
+        groups.append(pairs)
     return groups
 
 
@@ -51,42 +49,64 @@
     return ends, counts
 
 
-def compress_kernel(me_ref, cols_ref, count_ref, lengths_ref, tiles_hbm, *rest):
+def compress_kernel(cols_hbm, count_hbm, lengths_hbm, tiles_hbm, *rest):
     outs = rest[: WINDOW]
-    slab, tiles, sems = rest[WINDOW:]
+    cols_ref, count_ref, lengths_ref, slab, tiles, small_sems, sems = rest[WINDOW:]
+    small = []
+    for index, (source, target) in enumerate(
+        ((cols_hbm, cols_ref), (count_hbm, count_ref), (lengths_hbm, lengths_ref))
+    ):
+        copy = pltpu.make_async_copy(source, target, small_sems.at[index])
+        copy.start()
+        small.append(copy)
     block_rows, slots, tile = tiles.shape[0], tiles.shape[1], tiles.shape[2]
     bores = slab.shape[1]
     per_chip = 2 * block_rows
-    half = slots // 2
     copies = []
     for row in range(block_rows):
-        for part in range(2):
-            where = pl.ds(part * half, half)
-            copy = pltpu.make_async_copy(
-                tiles_hbm.at[row, where], tiles.at[row, where], sems.at[row, part]
-            )
-            copy.start()
-            copies.append(copy)
-    chip = me_ref[0] // 2
+        copy = pltpu.make_async_copy(tiles_hbm.at[row], tiles.at[row], sems.at[row])
+        copy.start()
+        copies.append(copy)
+    slab[...] = jnp.zeros_like(slab)
+    chip = lax.axis_index("rows") // 2
+    for copy in small:
+        copy.wait()
     first_block = (chip - CHIP_REACH) * per_chip
     ends, counts = bounds(lengths_ref[...], bores)
     starts = ends - counts
-    slab[...] = jnp.zeros_like(slab)
+    members = []
     for row in range(block_rows):
         position = (
             lax.broadcasted_iota(jnp.int32, (bores, tile), 1) + row * tile
         ).astype(F32)
-        members = ((position >= starts) & (position < ends)).astype(F32).astype(BF16)
-        used = count_ref[row]
-        for part in range(2):
-            copies[2 * row + part].wait()
-            for slot in range(part * half, part * half + half):
-                place = jnp.where(
-                    slot < used, cols_ref[row, slot] - first_block, WINDOW * per_chip
-                )
-                slab[place] += jnp.dot(
-                    members, tiles[row, slot], preferred_element_type=F32
-                )
+        inside = (position >= starts) & (position < ends)
+        members.append(inside.astype(F32).astype(BF16))
+    empty = jnp.zeros((bores, tile), BF16)
+    for row in range(0, block_rows, 2):
+        upper = jnp.concatenate([members[row], empty], axis=1)
+        under = jnp.concatenate([empty, members[row + 1]], axis=1)
+        left = jnp.concatenate([upper, under], axis=0)
+        copies[row].wait()
+        copies[row + 1].wait()
+        for slot in range(0, slots, 2):
+            right = jnp.concatenate(
+                [
+                    jnp.concatenate([tiles[at, slot], tiles[at, slot + 1]], axis=1)
+                    for at in (row, row + 1)
+                ],
+                axis=0,
+            )
+            product = jnp.dot(left, right, preferred_element_type=F32)
+            for i in range(2):
+                for j in range(2):
+                    place = jnp.where(
+                        slot + j < count_ref[row + i],
+                        cols_ref[row + i, slot + j] - first_block,
+                        WINDOW * per_chip,
+                    )
+                    slab[place] += product[
+                        i * bores : (i + 1) * bores, j * tile : (j + 1) * tile
+                    ]
     for out, offset in zip(outs, (0,) + hop_offsets(chip)):
         out[...] = slab[pl.ds((offset + CHIP_REACH) * per_chip, per_chip)]
 
@@ -96,13 +116,14 @@
     return high, (value - high.astype(F32)).astype(BF16)
 
 
-def gram_kernel(me_ref, *rest):
+def gram_kernel(lengths_ref, recorded_ref, *rest):
     mine, other = rest[:WINDOW], rest[WINDOW : 2 * WINDOW]
     heat_mine, heat_other = rest[2 * WINDOW : 2 * WINDOW + 2]
     outs = rest[2 * WINDOW + 2 : 3 * WINDOW + 2]
     high, low, heat, left, shifted = rest[3 * WINDOW + 2 :]
     blocks, bores, tile = mine[0].shape
-    chip, core = me_ref[0] // 2, lax.rem(me_ref[0], 2)
+    me = lax.axis_index("rows")
+    chip, core = me // 2, lax.rem(me, 2)
     seg_rows = heat_mine.shape[0]
     offsets = (0,) + hop_offsets(chip)
     for pieces, side in ((mine, core), (other, 1 - core)):
@@ -143,33 +164,27 @@
             places.append(jnp.where(keep, moved, 0.0))
         shifted[slot, :, :width] = jnp.where(odd == 1, places[1], places[0])
         shifted[slot, :, width:] = warm[slot * bores : (slot + 1) * bores]
+    _, counts = bounds(lengths_ref[...], bores)
+    odd = lax.rem(chip, 2)
+    free = ((odd == 1) & (lane < span)) | ((odd == 0) & (lane >= WINDOW * span))
+    shifted[CHIP_REACH, :, :width] = jnp.where(
+        free, counts, shifted[CHIP_REACH, :, :width]
+    )
+    shifted[CHIP_REACH, :, width:] = (
+        shifted[CHIP_REACH, :, width:] - counts * recorded_ref[...]
+    )
     for out, offset in zip(outs, offsets):
         out[...] = shifted[offset + CHIP_REACH]
 
 
-def total_kernel(me_ref, lengths_ref, recorded_ref, *rest):
-    parts, out = rest[:WINDOW], rest[WINDOW]
-    bores, columns = recorded_ref.shape
-    width = out.shape[1] - columns
-    span = 2 * bores
-    odd = lax.rem(me_ref[0] // 2, 2)
-    _, counts = bounds(lengths_ref[...], bores)
-    total = parts[0][...]
-    for part in parts[1:]:
-        total = total + part[...]
-    lane = lax.broadcasted_iota(jnp.int32, (bores, width), 1)
-    free = ((odd == 1) & (lane < span)) | ((odd == 0) & (lane >= WINDOW * span))
-    out[:, :width] = jnp.where(free, counts, total[:, :width])
-    out[:, width:] = total[:, width:] / counts - recorded_ref[...]
-
-
-def transpose_kernel(me_ref, *rest):
+def transpose_kernel(*rest):
     mine, other = rest[:WINDOW], rest[WINDOW : 2 * WINDOW]
     high, low = rest[2 * WINDOW : 2 * WINDOW + 2]
     (rows_of,) = rest[2 * WINDOW + 2 :]
     blocks, bores, tile = mine[0].shape
     own_blocks = blocks // 2
-    chip, core = me_ref[0] // 2, lax.rem(me_ref[0], 2)
+    me = lax.axis_index("rows")
+    chip, core = me // 2, lax.rem(me, 2)
     for pieces, side in ((mine, core), (other, 1 - core)):
         for piece, offset in zip(pieces, (0,) + hop_offsets(chip)):
             at = pl.multiple_of((offset + CHIP_REACH) * 2 * bores + side * bores, bores)
@@ -181,16 +196,18 @@
         low[block * tile : (block + 1) * tile] = rest_of
 
 
-def descend_kernel(ranks, me_ref, heat_ref, high_ref, low_ref, *rest):
+def descend_kernel(ranks, heat_hbm, high_ref, low_ref, *rest):
     pieces = rest[:ranks]
     heat_out, misfit_out = rest[ranks : ranks + 2]
-    lower, band, counts, misfit, warm, shares = rest[ranks + 2 :]
+    lower, band, counts, misfit, warm, shares, heat_ref, heat_sem = rest[ranks + 2 :]
+    fetch = pltpu.make_async_copy(heat_hbm, heat_ref, heat_sem)
+    fetch.start()
     bores, columns = misfit_out.shape
     width = lower.shape[1]
     plane = 4 * bores
     planes = ranks // 4
     span = 2 * bores
-    me = me_ref[0]
+    me = lax.axis_index("rows")
     lane = lax.broadcasted_iota(jnp.int32, (bores, width), 1)
     for index, piece in enumerate(pieces):
         rank = jnp.bitwise_xor(me, index)
@@ -199,7 +216,7 @@
         count = jnp.where(odd, piece[:, :1], piece[:, width - 1 : width])
         free = (odd & (lane < span)) | (jnp.logical_not(odd) & (lane >= WINDOW * span))
         lower[pl.ds(at, bores)] = jnp.where(free, 0.0, piece[:, :width])
-        misfit[pl.ds(at, bores)] = piece[:, width:]
+        misfit[pl.ds(at, bores)] = piece[:, width:] / count
         counts[pl.ds(at, bores)] = jnp.broadcast_to(count, (bores, columns))
     half_row = lax.broadcasted_iota(jnp.int32, (plane, plane), 0) < span
     half_col = lax.broadcasted_iota(jnp.int32, (plane, plane), 1) >= span
@@ -245,6 +262,7 @@
         misfit[...] = misfit[...] - step * warm[...]
     misfit_out[...] = misfit[pl.ds(pl.multiple_of(me * bores, bores), bores)]
     first = pl.multiple_of((me // 2 - CHIP_REACH) * span + 2 * plane, span)
+    fetch.wait()
     heat = heat_ref[...]
     for iteration in range(ITERS):
         near = shares[iteration, pl.ds(first, WINDOW * span)]
@@ -265,7 +283,6 @@
     rows = WINDOW * bores
     span = 2 * bores
     width = 6 * span
-    me = lax.axis_index("rows").astype(jnp.int32).reshape(1)
     hops = hop_pairs(ranks)
     limit = pltpu.CompilerParams(vmem_limit_bytes=48 << 20)
 
@@ -281,23 +298,27 @@
     sent = pl.pallas_call(
         compress_kernel,
         out_shape=(piece,) * WINDOW,
-        in_specs=[SMEM, SMEM, SMEM, VMEM, ANY],
+        in_specs=[HBM] * 4,
         out_specs=(VMEM,) * WINDOW,
         scratch_shapes=[
+            pltpu.SMEM(tile_cols.shape, jnp.int32),
+            pltpu.SMEM(tile_count.shape, jnp.int32),
+            pltpu.VMEM(bore_lengths.shape, jnp.int32),
             pltpu.VMEM((WINDOW * per_chip + 1, bores, tile), F32),
             pltpu.VMEM((block_rows, slots, tile, tile), BF16),
-            pltpu.SemaphoreType.DMA((block_rows, 2)),
+            pltpu.SemaphoreType.DMA((3,)),
+            pltpu.SemaphoreType.DMA((block_rows,)),
         ],
-        compiler_params=limit,
+        compiler_params=pltpu.CompilerParams(vmem_limit_bytes=60 << 20),
         name="compress",
-    )(me, tile_cols, tile_count, bore_lengths, response_tiles)
+    )(tile_cols, tile_count, bore_lengths, response_tiles)
     mine = [sent[0]] + [send(value, pairs) for value, pairs in zip(sent[1:], hops)]
     other = [swap(value, 1) for value in mine]
     packed = jax.ShapeDtypeStruct((bores, width + columns), F32)
     partial = pl.pallas_call(
         gram_kernel,
         out_shape=(packed,) * WINDOW,
-        in_specs=[SMEM] + [VMEM] * (2 * WINDOW + 2),
+        in_specs=[VMEM] * (2 * WINDOW + 4),
         out_specs=(VMEM,) * WINDOW,
         scratch_shapes=[
             pltpu.VMEM((WINDOW * span, per_chip * tile), BF16),
@@ -308,28 +329,24 @@
         ],
         compiler_params=limit,
         name="gram",
-    )(me, *mine, *other, heat_low, heat_other)
+    )(bore_lengths, recorded, *mine, *other, heat_low, heat_other)
     parts = [partial[0]] + [send(value, pairs) for value, pairs in zip(partial[1:], hops)]
     turned = jax.ShapeDtypeStruct((seg_rows, WINDOW * span), BF16)
     high, low = pl.pallas_call(
         transpose_kernel,
         out_shape=(turned, turned),
-        in_specs=[SMEM] + [VMEM] * (2 * WINDOW),
+        in_specs=[VMEM] * (2 * WINDOW),
         out_specs=(VMEM, VMEM),
         scratch_shapes=[pltpu.VMEM((block_rows, WINDOW * span, tile), F32)],
         compiler_params=limit,
         name="turn",
-    )(me, *mine, *other)
-    total = pl.pallas_call(
-        total_kernel,
-        out_shape=packed,
-        in_specs=[SMEM] + [VMEM] * (2 + WINDOW),
-        out_specs=VMEM,
-        name="total",
-    )(me, bore_lengths, recorded, *parts)
+    )(*mine, *other)
+    total = parts[0]
+    for part in parts[1:]:
+        total = total + part
     gathered = [total] + [None] * (ranks - 1)
     known = [0]
-    direct = [index for index in range(4, min(ranks, 16), 4)]
+    direct = [index for index in range(4, min(ranks, 16), 4)][::-1]
     for index in direct:
         gathered[index] = swap(total, index)
     known += direct
@@ -348,7 +365,7 @@
             jax.ShapeDtypeStruct((seg_rows, columns), F32),
             jax.ShapeDtypeStruct((bores, columns), F32),
         ),
-        in_specs=[SMEM] + [VMEM] * (3 + ranks),
+        in_specs=[HBM] + [VMEM] * (2 + ranks),
         out_specs=(VMEM, VMEM),
         scratch_shapes=[
             pltpu.VMEM((ranks * bores, width), F32),
@@ -357,10 +374,12 @@
             pltpu.VMEM((ranks * bores, columns), F32),
             pltpu.VMEM((ranks * bores, columns), F32),
             pltpu.VMEM((ITERS, (ranks + 16) * bores, columns), BF16),
+            pltpu.VMEM((seg_rows, columns), F32),
+            pltpu.SemaphoreType.DMA,
         ],
         compiler_params=limit,
         name="descend",
-    )(me, heat_start, high, low, *gathered)
+    )(heat_start, high, low, *gathered)
 
 
 def solution(mesh):

time: 61 us -> 54.3 us (0.89)
  local copies, waits for them, and re-layouts: 6.21 us -> 1.82 us
  Pallas kernels: 11.3 us -> 8.37 us
  starting transfers between devices: 27.3 us -> 28.4 us
    unnamed x22 -> x10, local copies, waits for them, and re-layouts: 6.21 us -> 1.82 us
    pallas_call x4 -> x3, Pallas kernels: 8.6 us -> 5.27 us  [the longest x1 3.69 us: on_device(): pl.pallas_call(compress_kernel, out_shape=(piece,) * WINDOW, in_specs=[HB...]
    ppermute x29, starting transfers between devices: 27.3 us -> 28.4 us  [send(): return lax.ppermute(value, 'rows', pairs)]
  transfers between devices with their start and end apart: 29 -> 29, of which waited for: 9 -> 11; matrix products, arithmetic and copies ran while one was open for 0% -> 0% of each run, Pallas kernels for 9% -> 7%
where the time goes in v2:
time: 54.3 us; the launch traced here: 54 us
  starting transfers between devices  28.4 us (52%)
  waiting for transfers between devices  13.6 us (25%)
  Pallas kernels  8.37 us (15%)
  local copies, waits for them, and re-layouts  1.82 us (3%)
  other arithmetic  1.03 us (2%)
  between operations  0.81 us (1%)
    ppermute x29, starting transfers between devices, send(): return lax.ppermute(value, 'rows', pairs)  28.4 us
    ppermute x29, waiting for transfers between devices, send(): return lax.ppermute(value, 'rows', pairs)  13.6 us
    pallas_call x1, Pallas kernels, on_device(): pl.pallas_call(compress_kernel, out_shape=(piece,) * WINDOW, in_specs=[HB...  3.69 us
    pallas_call x1, Pallas kernels, on_device(): pl.pallas_call(functools.partial(descend_kernel, ranks), out_shape=(jax.S...  3.1 us
    unnamed x10, local copies, waits for them, and re-layouts  1.82 us
    pallas_call x1, Pallas kernels, on_device(): pl.pallas_call(gram_kernel, out_shape=(packed,) * WINDOW, in_specs=[VMEM]...  1.25 us
  transfers between devices with their start and end apart: 29, of which 11 were waited for; matrix products, arithmetic and copies ran while one was open for 0% of the time, Pallas kernels for 7%

profile of v2, /device:TPU:0, one launch (start us, length us, event | category | flops | bytes accessed | tf_op | source)
XLA Modules:
  0.0 54.0 jit_solution(14535838750438099254)
XLA Ops:
  0.7 1.0 %convert_element_type.3.rest_10_ = bf16[512,128]{1,0:T(8,128)(2,1)S(1)} convert(f32[512,128]{1,0:T(8,128)} %heat_hbm.1) | non-fusion elementwise | flops 65536 | bytes 393216 | tf_op jit(solution)/shard_map/convert_element_type | solution.py:295
  2.2 3.7 %compress.1 = (f32[8,32,128]{2,1,0:T(8,128)}, f32[8,32,128]{2,1,0:T(8,128)}, f32[8,32,128]{2,1,0:T(8,128)}, f32[8,32,128]{2,1,0:T(8,128)}, f32[8,32,128]{2,1,0:T(8,128)}) custom-call(s32[4,30]{1,0:T(4,128)} %cols_hbm.1, s32[4]{0:T(128)} %count_hbm.1, s32[1,32]{1,0:T(1,128)} %lengths_ref.1, bf16[4,30,128,128]{3,2,1,0:T(8,128)(2,1)} %tiles_hbm.1), custom_call_target="tpu_custom_call" | custom-call | tf_op jit(solution)/shard_map/compress/pallas_call | solution.py:298
  7.2 8.0 %collective-permute-start.2 = (f32[8,32,128]{2,1,0:T(8,128)}, f32[8,32,128]{2,1,0:T(8,128)S(1)}, u32[]{:S(2)}, u32[]{:S(2)}) collective-permute-start(f32[8,32,128]{2,1,0:T(8,128)} %get-tuple-element.17), channel_id=1, source_target_pairs={{0,4},{4,0},{1,5},{5,1},{2,6},{6,2},{3,7},{7,3},{8,12},{12,8},{9,1... | collective-permute-start | bytes 393224 | tf_op jit(solution)/shard_map/ppermute | solution.py:290
  15.2 1.7 %collective-permute-start.3 = (f32[8,32,128]{2,1,0:T(8,128)}, f32[8,32,128]{2,1,0:T(8,128)S(1)}, u32[]{:S(2)}, u32[]{:S(2)}) collective-permute-start(f32[8,32,128]{2,1,0:T(8,128)} %get-tuple-element.18), channel_id=1, source_target_pairs={{0,2},{2,0},{1,3},{3,1},{4,6},{6,4},{5,7},{7,5},{8,10},{10,8},{9,1... | collective-permute-start | bytes 393224 | tf_op jit(solution)/shard_map/ppermute | solution.py:290
  17.5 1.5 %collective-permute-done.2.rest_3_ = f32[8,32,128]{2,1,0:T(8,128)S(1)} collective-permute-done((f32[8,32,128]{2,1,0:T(8,128)}, f32[8,32,128]{2,1,0:T(8,128)S(1)}, u32[]{:S(2)}, u32[]{:S(2)}) %collective-permute-start.2) | collective-permute-done | bytes 131104 | tf_op jit(solution)/shard_map/ppermute | solution.py:290
  19.0 1.5 %collective-permute-done.3.rest_4_ = f32[8,32,128]{2,1,0:T(8,128)S(1)} collective-permute-done((f32[8,32,128]{2,1,0:T(8,128)}, f32[8,32,128]{2,1,0:T(8,128)S(1)}, u32[]{:S(2)}, u32[]{:S(2)}) %collective-permute-start.3) | collective-permute-done | bytes 131104 | tf_op jit(solution)/shard_map/ppermute | solution.py:290
  20.5 1.3 %collective-permute-done.8.rest_9_ = f32[8,32,128]{2,1,0:T(8,128)S(1)} collective-permute-done((f32[8,32,128]{2,1,0:T(8,128)S(1)}, f32[8,32,128]{2,1,0:T(8,128)S(1)}, u32[]{:S(2)}, u32[]{:S(2)}) %collective-permute-start.8) | collective-permute-done | bytes 131104 | tf_op jit(solution)/shard_map/ppermute | solution.py:290
  21.9 0.9 %copy-done.1 = f32[8,32,128]{2,1,0:T(8,128)S(1)} copy-done((f32[8,32,128]{2,1,0:T(8,128)S(1)}, f32[8,32,128]{2,1,0:T(8,128)}, u32[]{:S(2)}) %copy-start.1) | copy-done | bytes 131096
  22.8 1.3 %gram.1 = (f32[32,512]{1,0:T(8,128)S(1)}, f32[32,512]{1,0:T(8,128)S(1)}, f32[32,512]{1,0:T(8,128)S(1)}, f32[32,512]{1,0:T(8,128)S(1)}, f32[32,512]{1,0:T(8,128)S(1)}) custom-call(s32[1,32]{1,0:T(1,128)S(1)} %copy-done.4, f32[32,128]{1,0:T(8,128)S(1)} %copy-done.3, f32[8,32,128]{2,1,0:T(8,128)S(1)} %copy-done.1, ...), custom_call_target="tpu_custom_call" | custom-call | tf_op jit(solution)/shard_map/gram/pallas_call | solution.py:318
  25.4 6.1 %collective-permute-start.12 = (f32[32,512]{1,0:T(8,128)S(1)}, f32[32,512]{1,0:T(8,128)S(1)}, u32[]{:S(2)}, u32[]{:S(2)}) collective-permute-start(f32[32,512]{1,0:T(8,128)S(1)} %get-tuple-element.24), channel_id=1, source_target_pairs={{0,4},{4,0},{1,5},{5,1},{2,6},{6,2},{3,7},{7,3},{8,12},{12,8},{9,1... | collective-permute-start | bytes 196616 | tf_op jit(solution)/shard_map/ppermute | solution.py:290
  31.5 0.7 %collective-permute-start.13 = (f32[32,512]{1,0:T(8,128)S(1)}, f32[32,512]{1,0:T(8,128)S(1)}, u32[]{:S(2)}, u32[]{:S(2)}) collective-permute-start(f32[32,512]{1,0:T(8,128)S(1)} %get-tuple-element.25), channel_id=1, source_target_pairs={{0,2},{2,0},{1,3},{3,1},{4,6},{6,4},{5,7},{7,5},{8,10},{10,8},{9,1... | collective-permute-start | bytes 196616 | tf_op jit(solution)/shard_map/ppermute | solution.py:290
  32.2 1.6 %collective-permute-done.12 = f32[32,512]{1,0:T(8,128)S(1)} collective-permute-done((f32[32,512]{1,0:T(8,128)S(1)}, f32[32,512]{1,0:T(8,128)S(1)}, u32[]{:S(2)}, u32[]{:S(2)}) %collective-permute-start.12) | collective-permute-done | bytes 65568 | tf_op jit(solution)/shard_map/ppermute | solution.py:290
  33.8 2.0 %collective-permute-done.13 = f32[32,512]{1,0:T(8,128)S(1)} collective-permute-done((f32[32,512]{1,0:T(8,128)S(1)}, f32[32,512]{1,0:T(8,128)S(1)}, u32[]{:S(2)}, u32[]{:S(2)}) %collective-permute-start.13) | collective-permute-done | bytes 65568 | tf_op jit(solution)/shard_map/ppermute | solution.py:290
  35.8 2.5 %collective-permute-start.25 = (f32[32,512]{1,0:T(8,128)S(1)}, f32[32,512]{1,0:T(8,128)S(1)}, u32[]{:S(2)}, u32[]{:S(2)}) collective-permute-start(f32[32,512]{1,0:T(8,128)S(1)} %add_add_fusion.rest_0_), channel_id=1, source_target_pairs={{0,12},{1,13},{2,14},{3,15},{4,8},{5,9},{6,10},{7,11},{8,4},{9,5},... | collective-permute-start | bytes 196616 | tf_op jit(solution)/shard_map/ppermute | solution.py:290
  38.3 1.9 %collective-permute-start.17 = (f32[32,512]{1,0:T(8,128)S(1)}, f32[32,512]{1,0:T(8,128)S(1)}, u32[]{:S(2)}, u32[]{:S(2)}) collective-permute-start(f32[32,512]{1,0:T(8,128)S(1)} %add_add_fusion.rest_0_), channel_id=1, source_target_pairs={{0,4},{1,5},{2,6},{3,7},{4,0},{5,1},{6,2},{7,3},{8,12},{9,13},{10,... | collective-permute-start | bytes 196616 | tf_op jit(solution)/shard_map/ppermute | solution.py:290
  40.3 0.7 %collective-permute-start.15 = (f32[32,512]{1,0:T(8,128)S(1)}, f32[32,512]{1,0:T(8,128)S(1)}, u32[]{:S(2)}, u32[]{:S(2)}) collective-permute-start(f32[32,512]{1,0:T(8,128)S(1)} %add_add_fusion.rest_0_), channel_id=1, source_target_pairs={{0,2},{1,3},{2,0},{3,1},{4,6},{5,7},{6,4},{7,5},{8,10},{9,11},{10,... | collective-permute-start | bytes 196616 | tf_op jit(solution)/shard_map/ppermute | solution.py:290
  40.9 1.4 %collective-permute-done.25.rest_12_ = f32[32,512]{1,0:T(8,128)S(1)} collective-permute-done((f32[32,512]{1,0:T(8,128)S(1)}, f32[32,512]{1,0:T(8,128)S(1)}, u32[]{:S(2)}, u32[]{:S(2)}) %collective-permute-start.25) | collective-permute-done | bytes 65568 | tf_op jit(solution)/shard_map/ppermute | solution.py:290
  42.6 1.1 %collective-permute-done.21.rest_8_ = f32[32,512]{1,0:T(8,128)S(1)} collective-permute-done((f32[32,512]{1,0:T(8,128)S(1)}, f32[32,512]{1,0:T(8,128)S(1)}, u32[]{:S(2)}, u32[]{:S(2)}) %collective-permute-start.21) | collective-permute-done | bytes 65568 | tf_op jit(solution)/shard_map/ppermute | solution.py:290
  43.7 0.7 %collective-permute-start.23 = (f32[32,512]{1,0:T(8,128)S(1)}, f32[32,512]{1,0:T(8,128)S(1)}, u32[]{:S(2)}, u32[]{:S(2)}) collective-permute-start(f32[32,512]{1,0:T(8,128)S(1)} %collective-permute-done.21.rest_8_), channel_id=1, source_target_pairs={{0,2},{1,3},{2,0},{3,1},{4,6},{5,7},{6,4},{7,5},{8,10},{9,11},{10,... | collective-permute-start | bytes 196616 | tf_op jit(solution)/shard_map/ppermute | solution.py:290
  45.0 0.9 %collective-permute-start.19 = (f32[32,512]{1,0:T(8,128)S(1)}, f32[32,512]{1,0:T(8,128)S(1)}, u32[]{:S(2)}, u32[]{:S(2)}) collective-permute-start(f32[32,512]{1,0:T(8,128)S(1)} %collective-permute-done.17.rest_4_), channel_id=1, source_target_pairs={{0,2},{1,3},{2,0},{3,1},{4,6},{5,7},{6,4},{7,5},{8,10},{9,11},{10,... | collective-permute-start | bytes 196616 | tf_op jit(solution)/shard_map/ppermute | solution.py:290
  47.1 1.2 %collective-permute-done.23.rest_10_ = f32[32,512]{1,0:T(8,128)S(1)} collective-permute-done((f32[32,512]{1,0:T(8,128)S(1)}, f32[32,512]{1,0:T(8,128)S(1)}, u32[]{:S(2)}, u32[]{:S(2)}) %collective-permute-start.23) | collective-permute-done | bytes 65568 | tf_op jit(solution)/shard_map/ppermute | solution.py:290
  48.8 0.8 %collective-permute-done.19.rest_6_ = f32[32,512]{1,0:T(8,128)S(1)} collective-permute-done((f32[32,512]{1,0:T(8,128)S(1)}, f32[32,512]{1,0:T(8,128)S(1)}, u32[]{:S(2)}, u32[]{:S(2)}) %collective-permute-start.19) | collective-permute-done | bytes 65568 | tf_op jit(solution)/shard_map/ppermute | solution.py:290
  49.6 0.9 %copy-done.2 = f32[8,32,128]{2,1,0:T(8,128)S(1)} copy-done((f32[8,32,128]{2,1,0:T(8,128)S(1)}, f32[8,32,128]{2,1,0:T(8,128)}, u32[]{:S(2)}) %copy-start.2) | copy-done | bytes 131096
  50.9 3.1 %descend.1 = (f32[512,128]{1,0:T(8,128)}, f32[32,128]{1,0:T(8,128)}) custom-call(f32[512,128]{1,0:T(8,128)S(1)} %copy-done, bf16[512,320]{1,0:T(8,128)(2,1)S(1)} %get-tuple-element.19.high_ref, bf16[512,320]{1,0:T(8,128)(2,1)S(1)} %get-tuple-element.20.low_ref, f32[32,512]{1,0:T(8,128)S(1)} %add_add_fusion.rest_0_, ...), custom_call_target="tpu_custom_call" | custom-call | tf_op jit(solution)/shard_map/descend/pallas_call | solution.py:362
  (50 shorter events, 6.7 us)
Async XLA Ops:
  1.7 15.2 %collective-permute-start.9 = (bf16[512,128]{1,0:T(8,128)(2,1)S(1)}, bf16[512,128]{1,0:T(8,128)(2,1)S(1)}, u32[]{:S(2)}, u32[]{:S(2)}) collective-permute-start(bf16[512,128]{1,0:T(8,128)(2,1)S(1)} %convert_element_type.3.rest_10_), channel_id=1, source_target_pairs={{0,1},{1,0},{2,3},{3,2},{4,5},{5,4},{6,7},{7,6},{8,9},{9,8},{10,11... | collective-permute-start | bytes 393224 | tf_op jit(solution)/shard_map/ppermute | solution.py:290
  5.9 11.0 %collective-permute-start = (f32[8,32,128]{2,1,0:T(8,128)}, f32[8,32,128]{2,1,0:T(8,128)S(1)}, u32[]{:S(2)}, u32[]{:S(2)}) collective-permute-start(f32[8,32,128]{2,1,0:T(8,128)} %get-tuple-element.15), channel_id=1, source_target_pairs={{2,4},{4,2},{3,5},{5,3},{6,8},{8,6},{7,9},{9,7},{10,12},{12,10},{1... | collective-permute-start | bytes 393224 | tf_op jit(solution)/shard_map/ppermute | solution.py:290
  6.6 10.9 %collective-permute-start.1 = (f32[8,32,128]{2,1,0:T(8,128)}, f32[8,32,128]{2,1,0:T(8,128)S(1)}, u32[]{:S(2)}, u32[]{:S(2)}) collective-permute-start(f32[8,32,128]{2,1,0:T(8,128)} %get-tuple-element.16), channel_id=1, source_target_pairs={{4,8},{8,4},{5,9},{9,5},{6,10},{10,6},{7,11},{11,7},{20,24},{24,20... | collective-permute-start | bytes 393224 | tf_op jit(solution)/shard_map/ppermute | solution.py:290
  7.2 11.8 %collective-permute-start.2 = (f32[8,32,128]{2,1,0:T(8,128)}, f32[8,32,128]{2,1,0:T(8,128)S(1)}, u32[]{:S(2)}, u32[]{:S(2)}) collective-permute-start(f32[8,32,128]{2,1,0:T(8,128)} %get-tuple-element.17), channel_id=1, source_target_pairs={{0,4},{4,0},{1,5},{5,1},{2,6},{6,2},{3,7},{7,3},{8,12},{12,8},{9,1... | collective-permute-start | bytes 393224 | tf_op jit(solution)/shard_map/ppermute | solution.py:290
  15.2 5.3 %collective-permute-start.3 = (f32[8,32,128]{2,1,0:T(8,128)}, f32[8,32,128]{2,1,0:T(8,128)S(1)}, u32[]{:S(2)}, u32[]{:S(2)}) collective-permute-start(f32[8,32,128]{2,1,0:T(8,128)} %get-tuple-element.18), channel_id=1, source_target_pairs={{0,2},{2,0},{1,3},{3,1},{4,6},{6,4},{5,7},{7,5},{8,10},{10,8},{9,1... | collective-permute-start | bytes 393224 | tf_op jit(solution)/shard_map/ppermute | solution.py:290
  16.9 3.6 %collective-permute-start.4 = (f32[8,32,128]{2,1,0:T(8,128)}, f32[8,32,128]{2,1,0:T(8,128)S(1)}, u32[]{:S(2)}, u32[]{:S(2)}) collective-permute-start(f32[8,32,128]{2,1,0:T(8,128)} %get-tuple-element.14.rest_0_), channel_id=1, source_target_pairs={{0,1},{1,0},{2,3},{3,2},{4,5},{5,4},{6,7},{7,6},{8,9},{9,8},{10,11... | collective-permute-start | bytes 393224 | tf_op jit(solution)/shard_map/ppermute | solution.py:290
  16.9 3.6 %collective-permute-start.5 = (f32[8,32,128]{2,1,0:T(8,128)S(1)}, f32[8,32,128]{2,1,0:T(8,128)S(1)}, u32[]{:S(2)}, u32[]{:S(2)}) collective-permute-start(f32[8,32,128]{2,1,0:T(8,128)S(1)} %collective-permute-done.rest_1_), channel_id=1, source_target_pairs={{0,1},{1,0},{2,3},{3,2},{4,5},{5,4},{6,7},{7,6},{8,9},{9,8},{10,11... | collective-permute-start | bytes 393224 | tf_op jit(solution)/shard_map/ppermute | solution.py:290
  17.4 3.1 %collective-permute-start.6 = (f32[8,32,128]{2,1,0:T(8,128)S(1)}, f32[8,32,128]{2,1,0:T(8,128)S(1)}, u32[]{:S(2)}, u32[]{:S(2)}) collective-permute-start(f32[8,32,128]{2,1,0:T(8,128)S(1)} %collective-permute-done.1.rest_2_), channel_id=1, source_target_pairs={{0,1},{1,0},{2,3},{3,2},{4,5},{5,4},{6,7},{7,6},{8,9},{9,8},{10,11... | collective-permute-start | bytes 393224 | tf_op jit(solution)/shard_map/ppermute | solution.py:290
  24.0 8.2 %collective-permute-start.10 = (f32[32,512]{1,0:T(8,128)S(1)}, f32[32,512]{1,0:T(8,128)S(1)}, u32[]{:S(2)}, u32[]{:S(2)}) collective-permute-start(f32[32,512]{1,0:T(8,128)S(1)} %get-tuple-element.22), channel_id=1, source_target_pairs={{2,4},{4,2},{3,5},{5,3},{6,8},{8,6},{7,9},{9,7},{10,12},{12,10},{1... | collective-permute-start | bytes 196616 | tf_op jit(solution)/shard_map/ppermute | solution.py:290
  24.7 7.5 %collective-permute-start.11 = (f32[32,512]{1,0:T(8,128)S(1)}, f32[32,512]{1,0:T(8,128)S(1)}, u32[]{:S(2)}, u32[]{:S(2)}) collective-permute-start(f32[32,512]{1,0:T(8,128)S(1)} %get-tuple-element.23), channel_id=1, source_target_pairs={{4,8},{8,4},{5,9},{9,5},{6,10},{10,6},{7,11},{11,7},{20,24},{24,20... | collective-permute-start | bytes 196616 | tf_op jit(solution)/shard_map/ppermute | solution.py:290
  25.4 8.4 %collective-permute-start.12 = (f32[32,512]{1,0:T(8,128)S(1)}, f32[32,512]{1,0:T(8,128)S(1)}, u32[]{:S(2)}, u32[]{:S(2)}) collective-permute-start(f32[32,512]{1,0:T(8,128)S(1)} %get-tuple-element.24), channel_id=1, source_target_pairs={{0,4},{4,0},{1,5},{5,1},{2,6},{6,2},{3,7},{7,3},{8,12},{12,8},{9,1... | collective-permute-start | bytes 196616 | tf_op jit(solution)/shard_map/ppermute | solution.py:290
  31.5 4.3 %collective-permute-start.13 = (f32[32,512]{1,0:T(8,128)S(1)}, f32[32,512]{1,0:T(8,128)S(1)}, u32[]{:S(2)}, u32[]{:S(2)}) collective-permute-start(f32[32,512]{1,0:T(8,128)S(1)} %get-tuple-element.25), channel_id=1, source_target_pairs={{0,2},{2,0},{1,3},{3,1},{4,6},{6,4},{5,7},{7,5},{8,10},{10,8},{9,1... | collective-permute-start | bytes 196616 | tf_op jit(solution)/shard_map/ppermute | solution.py:290
  35.8 6.5 %collective-permute-start.25 = (f32[32,512]{1,0:T(8,128)S(1)}, f32[32,512]{1,0:T(8,128)S(1)}, u32[]{:S(2)}, u32[]{:S(2)}) collective-permute-start(f32[32,512]{1,0:T(8,128)S(1)} %add_add_fusion.rest_0_), channel_id=1, source_target_pairs={{0,12},{1,13},{2,14},{3,15},{4,8},{5,9},{6,10},{7,11},{8,4},{9,5},... | collective-permute-start | bytes 196616 | tf_op jit(solution)/shard_map/ppermute | solution.py:290
  38.3 5.4 %collective-permute-start.21 = (f32[32,512]{1,0:T(8,128)S(1)}, f32[32,512]{1,0:T(8,128)S(1)}, u32[]{:S(2)}, u32[]{:S(2)}) collective-permute-start(f32[32,512]{1,0:T(8,128)S(1)} %add_add_fusion.rest_0_), channel_id=1, source_target_pairs={{0,8},{1,9},{2,10},{3,11},{4,12},{5,13},{6,14},{7,15},{8,0},{9,1},... | collective-permute-start | bytes 196616 | tf_op jit(solution)/shard_map/ppermute | solution.py:290
  38.3 5.4 %collective-permute-start.17 = (f32[32,512]{1,0:T(8,128)S(1)}, f32[32,512]{1,0:T(8,128)S(1)}, u32[]{:S(2)}, u32[]{:S(2)}) collective-permute-start(f32[32,512]{1,0:T(8,128)S(1)} %add_add_fusion.rest_0_), channel_id=1, source_target_pairs={{0,4},{1,5},{2,6},{3,7},{4,0},{5,1},{6,2},{7,3},{8,12},{9,13},{10,... | collective-permute-start | bytes 196616 | tf_op jit(solution)/shard_map/ppermute | solution.py:290
  40.3 4.7 %collective-permute-start.15 = (f32[32,512]{1,0:T(8,128)S(1)}, f32[32,512]{1,0:T(8,128)S(1)}, u32[]{:S(2)}, u32[]{:S(2)}) collective-permute-start(f32[32,512]{1,0:T(8,128)S(1)} %add_add_fusion.rest_0_), channel_id=1, source_target_pairs={{0,2},{1,3},{2,0},{3,1},{4,6},{5,7},{6,4},{7,5},{8,10},{9,11},{10,... | collective-permute-start | bytes 196616 | tf_op jit(solution)/shard_map/ppermute | solution.py:290
  40.9 4.1 %collective-permute-start.14 = (f32[32,512]{1,0:T(8,128)S(1)}, f32[32,512]{1,0:T(8,128)S(1)}, u32[]{:S(2)}, u32[]{:S(2)}) collective-permute-start(f32[32,512]{1,0:T(8,128)S(1)} %add_add_fusion.rest_0_), channel_id=1, source_target_pairs={{0,1},{1,0},{2,3},{3,2},{4,5},{5,4},{6,7},{7,6},{8,9},{9,8},{10,11... | collective-permute-start | bytes 196616 | tf_op jit(solution)/shard_map/ppermute | solution.py:290
  42.3 4.3 %collective-permute-start.27 = (f32[32,512]{1,0:T(8,128)S(1)}, f32[32,512]{1,0:T(8,128)S(1)}, u32[]{:S(2)}, u32[]{:S(2)}) collective-permute-start(f32[32,512]{1,0:T(8,128)S(1)} %collective-permute-done.25.rest_12_), channel_id=1, source_target_pairs={{0,2},{1,3},{2,0},{3,1},{4,6},{5,7},{6,4},{7,5},{8,10},{9,11},{10,... | collective-permute-start | bytes 196616 | tf_op jit(solution)/shard_map/ppermute | solution.py:290
  43.7 2.9 %collective-permute-start.26 = (f32[32,512]{1,0:T(8,128)S(1)}, f32[32,512]{1,0:T(8,128)S(1)}, u32[]{:S(2)}, u32[]{:S(2)}) collective-permute-start(f32[32,512]{1,0:T(8,128)S(1)} %collective-permute-done.25.rest_12_), channel_id=1, source_target_pairs={{0,1},{1,0},{2,3},{3,2},{4,5},{5,4},{6,7},{7,6},{8,9},{9,8},{10,11... | collective-permute-start | bytes 196616 | tf_op jit(solution)/shard_map/ppermute | solution.py:290
  43.7 4.6 %collective-permute-start.23 = (f32[32,512]{1,0:T(8,128)S(1)}, f32[32,512]{1,0:T(8,128)S(1)}, u32[]{:S(2)}, u32[]{:S(2)}) collective-permute-start(f32[32,512]{1,0:T(8,128)S(1)} %collective-permute-done.21.rest_8_), channel_id=1, source_target_pairs={{0,2},{1,3},{2,0},{3,1},{4,6},{5,7},{6,4},{7,5},{8,10},{9,11},{10,... | collective-permute-start | bytes 196616 | tf_op jit(solution)/shard_map/ppermute | solution.py:290
  45.0 3.3 %collective-permute-start.22 = (f32[32,512]{1,0:T(8,128)S(1)}, f32[32,512]{1,0:T(8,128)S(1)}, u32[]{:S(2)}, u32[]{:S(2)}) collective-permute-start(f32[32,512]{1,0:T(8,128)S(1)} %collective-permute-done.21.rest_8_), channel_id=1, source_target_pairs={{0,1},{1,0},{2,3},{3,2},{4,5},{5,4},{6,7},{7,6},{8,9},{9,8},{10,11... | collective-permute-start | bytes 196616 | tf_op jit(solution)/shard_map/ppermute | solution.py:290
  45.0 4.6 %collective-permute-start.19 = (f32[32,512]{1,0:T(8,128)S(1)}, f32[32,512]{1,0:T(8,128)S(1)}, u32[]{:S(2)}, u32[]{:S(2)}) collective-permute-start(f32[32,512]{1,0:T(8,128)S(1)} %collective-permute-done.17.rest_4_), channel_id=1, source_target_pairs={{0,2},{1,3},{2,0},{3,1},{4,6},{5,7},{6,4},{7,5},{8,10},{9,11},{10,... | collective-permute-start | bytes 196616 | tf_op jit(solution)/shard_map/ppermute | solution.py:290
  46.6 4.3 %collective-permute-start.18 = (f32[32,512]{1,0:T(8,128)S(1)}, f32[32,512]{1,0:T(8,128)S(1)}, u32[]{:S(2)}, u32[]{:S(2)}) collective-permute-start(f32[32,512]{1,0:T(8,128)S(1)} %collective-permute-done.17.rest_4_), channel_id=1, source_target_pairs={{0,1},{1,0},{2,3},{3,2},{4,5},{5,4},{6,7},{7,6},{8,9},{9,8},{10,11... | collective-permute-start | bytes 196616 | tf_op jit(solution)/shard_map/ppermute | solution.py:290
  46.6 4.3 %collective-permute-start.16 = (f32[32,512]{1,0:T(8,128)S(1)}, f32[32,512]{1,0:T(8,128)S(1)}, u32[]{:S(2)}, u32[]{:S(2)}) collective-permute-start(f32[32,512]{1,0:T(8,128)S(1)} %collective-permute-done.15.rest_2_), channel_id=1, source_target_pairs={{0,1},{1,0},{2,3},{3,2},{4,5},{5,4},{6,7},{7,6},{8,9},{9,8},{10,11... | collective-permute-start | bytes 196616 | tf_op jit(solution)/shard_map/ppermute | solution.py:290
  (10 other events, 103.7 us)

commit v3 on v2

--- a/solution.py
+++ b/solution.py
@@ -33,6 +33,8 @@
                 for core in (0, 1):
                     low, high = 2 * chip + core, 2 * (chip + step) + core
                     pairs += [(low, high), (high, low)]
+        busy = {source for source, _ in pairs}
+        pairs += [(rank, rank ^ 1) for rank in range(ranks) if rank not in busy]
         groups.append(pairs)
     return groups
 
@@ -116,12 +118,18 @@
     return high, (value - high.astype(F32)).astype(BF16)
 
 
+def block_of(piece, block, tile):
+    if len(piece.shape) == 3:
+        return piece[block]
+    return piece[:, pl.ds(pl.multiple_of(block * tile, tile), tile)]
+
+
 def gram_kernel(lengths_ref, recorded_ref, *rest):
     mine, other = rest[:WINDOW], rest[WINDOW : 2 * WINDOW]
     heat_mine, heat_other = rest[2 * WINDOW : 2 * WINDOW + 2]
     outs = rest[2 * WINDOW + 2 : 3 * WINDOW + 2]
     high, low, heat, left, shifted = rest[3 * WINDOW + 2 :]
-    blocks, bores, tile = mine[0].shape
+    blocks, bores, tile = other[0].shape
     me = lax.axis_index("rows")
     chip, core = me // 2, lax.rem(me, 2)
     seg_rows = heat_mine.shape[0]
@@ -130,7 +138,7 @@
         for piece, offset in zip(pieces, offsets):
             at = pl.multiple_of((offset + CHIP_REACH) * 2 * bores + side * bores, bores)
             for block in range(blocks):
-                top, rest_of = split(piece[block])
+                top, rest_of = split(block_of(piece, block, tile))
                 high[pl.ds(at, bores), block * tile : (block + 1) * tile] = top
                 low[pl.ds(at, bores), block * tile : (block + 1) * tile] = rest_of
     heat[pl.ds(pl.multiple_of(core * seg_rows, seg_rows), seg_rows)] = heat_mine[...]
@@ -181,7 +189,7 @@
     mine, other = rest[:WINDOW], rest[WINDOW : 2 * WINDOW]
     high, low = rest[2 * WINDOW : 2 * WINDOW + 2]
     (rows_of,) = rest[2 * WINDOW + 2 :]
-    blocks, bores, tile = mine[0].shape
+    blocks, bores, tile = other[0].shape
     own_blocks = blocks // 2
     me = lax.axis_index("rows")
     chip, core = me // 2, lax.rem(me, 2)
@@ -189,17 +197,19 @@
         for piece, offset in zip(pieces, (0,) + hop_offsets(chip)):
             at = pl.multiple_of((offset + CHIP_REACH) * 2 * bores + side * bores, bores)
             for block in range(own_blocks):
-                rows_of[block, pl.ds(at, bores)] = piece[core * own_blocks + block]
+                rows_of[block, pl.ds(at, bores)] = block_of(
+                    piece, core * own_blocks + block, tile
+                )
     for block in range(own_blocks):
         top, rest_of = split(rows_of[block].T)
         high[block * tile : (block + 1) * tile] = top
         low[block * tile : (block + 1) * tile] = rest_of
 
 
-def descend_kernel(ranks, heat_hbm, high_ref, low_ref, *rest):
-    pieces = rest[:ranks]
-    heat_out, misfit_out = rest[ranks : ranks + 2]
-    lower, band, counts, misfit, warm, shares, heat_ref, heat_sem = rest[ranks + 2 :]
+def descend_kernel(ranks, places, heat_hbm, high_ref, low_ref, *rest):
+    pieces, rest = rest[: len(places)], rest[len(places) :]
+    heat_out, misfit_out = rest[:2]
+    lower, band, counts, misfit, warm, shares, heat_ref, heat_sem = rest[2:]
     fetch = pltpu.make_async_copy(heat_hbm, heat_ref, heat_sem)
     fetch.start()
     bores, columns = misfit_out.shape
@@ -209,15 +219,19 @@
     span = 2 * bores
     me = lax.axis_index("rows")
     lane = lax.broadcasted_iota(jnp.int32, (bores, width), 1)
-    for index, piece in enumerate(pieces):
-        rank = jnp.bitwise_xor(me, index)
-        at = pl.multiple_of(rank * bores, bores)
-        odd = lax.rem(rank // 2, 2) == 1
-        count = jnp.where(odd, piece[:, :1], piece[:, width - 1 : width])
-        free = (odd & (lane < span)) | (jnp.logical_not(odd) & (lane >= WINDOW * span))
-        lower[pl.ds(at, bores)] = jnp.where(free, 0.0, piece[:, :width])
-        misfit[pl.ds(at, bores)] = piece[:, width:] / count
-        counts[pl.ds(at, bores)] = jnp.broadcast_to(count, (bores, columns))
+    for indices, piece in zip(places, pieces):
+        for part, index in enumerate(indices):
+            here = slice(part * bores, (part + 1) * bores)
+            rank = jnp.bitwise_xor(me, index)
+            at = pl.multiple_of(rank * bores, bores)
+            odd = lax.rem(rank // 2, 2) == 1
+            count = jnp.where(odd, piece[here, :1], piece[here, width - 1 : width])
+            free = (odd & (lane < span)) | (
+                jnp.logical_not(odd) & (lane >= WINDOW * span)
+            )
+            lower[pl.ds(at, bores)] = jnp.where(free, 0.0, piece[here, :width])
+            misfit[pl.ds(at, bores)] = piece[here, width:] / count
+            counts[pl.ds(at, bores)] = jnp.broadcast_to(count, (bores, columns))
     half_row = lax.broadcasted_iota(jnp.int32, (plane, plane), 0) < span
     half_col = lax.broadcasted_iota(jnp.int32, (plane, plane), 1) >= span
     for p in range(planes):
@@ -292,8 +306,6 @@
     def swap(value, bit):
         return send(value, [(rank, rank ^ bit) for rank in range(ranks)])
 
-    heat_low = heat_start.astype(BF16)
-    heat_other = swap(heat_low, 1)
     piece = jax.ShapeDtypeStruct((per_chip, bores, tile), F32)
     sent = pl.pallas_call(
         compress_kernel,
@@ -313,7 +325,13 @@
         name="compress",
     )(tile_cols, tile_count, bore_lengths, response_tiles)
     mine = [sent[0]] + [send(value, pairs) for value, pairs in zip(sent[1:], hops)]
+    mine[1], heat_late, own = lax.optimization_barrier((mine[1], heat_start, mine[0]))
+    heat_low = heat_late.astype(BF16)
+    heat_other = swap(heat_low, 1)
+    own = own.transpose(1, 0, 2).reshape(bores, per_chip * tile)
+    mine[2], own = lax.optimization_barrier((mine[2], own))
     other = [swap(value, 1) for value in mine]
+    mine[0] = own
     packed = jax.ShapeDtypeStruct((bores, width + columns), F32)
     partial = pl.pallas_call(
         gram_kernel,
@@ -341,31 +359,35 @@
         compiler_params=limit,
         name="turn",
     )(*mine, *other)
-    total = parts[0]
+    total, high, low = lax.optimization_barrier((parts[0], high, low))
     for part in parts[1:]:
         total = total + part
-    gathered = [total] + [None] * (ranks - 1)
-    known = [0]
-    direct = [index for index in range(4, min(ranks, 16), 4)][::-1]
-    for index in direct:
-        gathered[index] = swap(total, index)
-    known += direct
+    column = {0: total}
+    for index in (8, 4, 12):
+        if index < ranks:
+            column[index] = swap(total, index)
     bit = 16
-    order = []
     while bit < ranks:
-        order.append(bit)
+        column.update({index ^ bit: swap(value, bit) for index, value in list(column.items())})
         bit *= 2
-    for bit in order + [2, 1]:
-        for index in list(known):
-            gathered[index ^ bit] = swap(gathered[index], bit)
-            known.append(index ^ bit)
+    beside = {index: swap(value, 2) for index, value in column.items()}
+    across = {
+        index: swap(jnp.concatenate([value, beside[index]], axis=0), 1)
+        for index, value in column.items()
+    }
+    places = tuple(
+        [(index,) for index in column]
+        + [(index ^ 2,) for index in column]
+        + [(index ^ 1, index ^ 3) for index in column]
+    )
+    gathered = list(column.values()) + list(beside.values()) + list(across.values())
     return pl.pallas_call(
-        functools.partial(descend_kernel, ranks),
+        functools.partial(descend_kernel, ranks, places),
         out_shape=(
             jax.ShapeDtypeStruct((seg_rows, columns), F32),
             jax.ShapeDtypeStruct((bores, columns), F32),
         ),
-        in_specs=[HBM] + [VMEM] * (2 + ranks),
+        in_specs=[HBM] + [VMEM] * (2 + len(gathered)),
         out_specs=(VMEM, VMEM),
         scratch_shapes=[
             pltpu.VMEM((ranks * bores, width), F32),

time: 54.3 us -> 46.2 us (0.85)
  starting transfers between devices: 28.4 us -> 25.1 us
  waiting for transfers between devices: 13.6 us -> 10.6 us
  other arithmetic: 1.03 us -> 0.08 us
  local copies, waits for them, and re-layouts: 1.82 us -> 0.93 us
    ppermute x29 -> x25, starting transfers between devices: 28.4 us -> 25.1 us  [send(): return lax.ppermute(value, 'rows', pairs)]
    ppermute x29 -> x25, waiting for transfers between devices: 13.6 us -> 10.6 us  [send(): return lax.ppermute(value, 'rows', pairs)]
    unnamed x10 -> x6, local copies, waits for them, and re-layouts: 1.82 us -> 0.01 us
    convert_element_type x1, other arithmetic: 1.01 us -> 0.02 us  [on_device(): heat_low = heat_late.astype(BF16)]
    reshape x0 -> x1, local copies, waits for them, and re-layouts: none -> 0.92 us  [on_device(): own = own.transpose(1, 0, 2).reshape(bores, per_chip * tile)]
  transfers between devices with their start and end apart: 29 -> 25, of which waited for: 11 -> 13; matrix products, arithmetic and copies ran while one was open for 0% -> 2% of each run, Pallas kernels for 7% -> 1%
where the time goes in v3:
time: 46.2 us; the launch traced here: 46 us
  starting transfers between devices  25.1 us (54%)
  waiting for transfers between devices  10.6 us (23%)
  Pallas kernels  8.57 us (19%)
  local copies, waits for them, and re-layouts  0.93 us (2%)
  between operations  0.81 us (2%)
    ppermute x25, starting transfers between devices, send(): return lax.ppermute(value, 'rows', pairs)  25.1 us
    ppermute x25, waiting for transfers between devices, send(): return lax.ppermute(value, 'rows', pairs)  10.6 us
    pallas_call x1, Pallas kernels, on_device(): pl.pallas_call(compress_kernel, out_shape=(piece,) * WINDOW, in_specs=[HB...  3.88 us
    pallas_call x1, Pallas kernels, on_device(): pl.pallas_call(functools.partial(descend_kernel, ranks, places), out_shap...  3.08 us
    pallas_call x1, Pallas kernels, on_device(): pl.pallas_call(gram_kernel, out_shape=(packed,) * WINDOW, in_specs=[VMEM]...  1.28 us
  transfers between devices with their start and end apart: 25, of which 13 were waited for; matrix products, arithmetic and copies ran while one was open for 2% of the time, Pallas kernels for 1%

profile of v3, /device:TPU:0, one launch (start us, length us, event | category | flops | bytes accessed | tf_op | source)
XLA Modules:
  0.0 46.0 jit_solution(2020612179521329403)
XLA Ops:
  0.7 3.9 %compress.1 = (f32[8,32,128]{2,1,0:T(8,128)}, f32[8,32,128]{2,1,0:T(8,128)}, f32[8,32,128]{2,1,0:T(8,128)}, f32[8,32,128]{2,1,0:T(8,128)}, f32[8,32,128]{2,1,0:T(8,128)}) custom-call(s32[4,30]{1,0:T(4,128)} %cols_hbm.1, s32[4]{0:T(128)} %count_hbm.1, s32[1,32]{1,0:T(1,128)} %lengths_ref.1, bf16[4,30,128,128]{3,2,1,0:T(8,128)(2,1)} %tiles_hbm.1), custom_call_target="tpu_custom_call" | custom-call | tf_op jit(solution)/shard_map/compress/pallas_call | solution.py:310
  5.1 5.4 %collective-permute-start.2 = (f32[8,32,128]{2,1,0:T(8,128)}, f32[8,32,128]{2,1,0:T(8,128)S(1)}, u32[]{:S(2)}, u32[]{:S(2)}) collective-permute-start(f32[8,32,128]{2,1,0:T(8,128)} %get-tuple-element.29), channel_id=1, source_target_pairs={{0,4},{4,0},{1,5},{5,1},{2,6},{6,2},{3,7},{7,3},{8,12},{12,8},{9,1... | collective-permute-start | bytes 393224 | tf_op jit(solution)/shard_map/ppermute | solution.py:304
  10.5 1.6 %collective-permute-start.3 = (f32[8,32,128]{2,1,0:T(8,128)}, f32[8,32,128]{2,1,0:T(8,128)S(1)}, u32[]{:S(2)}, u32[]{:S(2)}) collective-permute-start(f32[8,32,128]{2,1,0:T(8,128)} %get-tuple-element.30), channel_id=1, source_target_pairs={{0,2},{2,0},{1,3},{3,1},{4,6},{6,4},{5,7},{7,5},{8,10},{10,8},{9,1... | collective-permute-start | bytes 393224 | tf_op jit(solution)/shard_map/ppermute | solution.py:304
  12.2 0.9 %copy_bitcast_fusion.rest_0_ = f32[32,1024]{1,0:T(8,128)S(1)} fusion(f32[8,32,128]{2,1,0:T(8,128)} %get-tuple-element.25), kind=kLoop, calls=%fused_computation | loop fusion | bytes 262144 | tf_op jit(solution)/shard_map/reshape | solution.py:331
  13.1 0.6 %collective-permute-start.6 = (f32[8,32,128]{2,1,0:T(8,128)S(1)}, f32[8,32,128]{2,1,0:T(8,128)S(1)}, u32[]{:S(2)}, u32[]{:S(2)}) collective-permute-start(f32[8,32,128]{2,1,0:T(8,128)S(1)} %collective-permute-done.rest_2_), channel_id=1, source_target_pairs={{0,1},{1,0},{2,3},{3,2},{4,5},{5,4},{6,7},{7,6},{8,9},{9,8},{10,11... | collective-permute-start | bytes 393224 | tf_op jit(solution)/shard_map/ppermute | solution.py:304
  13.8 1.4 %collective-permute-done.2.rest_3_ = f32[8,32,128]{2,1,0:T(8,128)S(1)} collective-permute-done((f32[8,32,128]{2,1,0:T(8,128)}, f32[8,32,128]{2,1,0:T(8,128)S(1)}, u32[]{:S(2)}, u32[]{:S(2)}) %collective-permute-start.2) | collective-permute-done | bytes 131104 | tf_op jit(solution)/shard_map/ppermute | solution.py:304
  15.2 0.5 %collective-permute-done.3.rest_4_ = f32[8,32,128]{2,1,0:T(8,128)S(1)} collective-permute-done((f32[8,32,128]{2,1,0:T(8,128)}, f32[8,32,128]{2,1,0:T(8,128)S(1)}, u32[]{:S(2)}, u32[]{:S(2)}) %collective-permute-start.3) | collective-permute-done | bytes 131104 | tf_op jit(solution)/shard_map/ppermute | solution.py:304
  15.7 0.5 %collective-permute-start.8 = (f32[8,32,128]{2,1,0:T(8,128)S(1)}, f32[8,32,128]{2,1,0:T(8,128)S(1)}, u32[]{:S(2)}, u32[]{:S(2)}) collective-permute-start(f32[8,32,128]{2,1,0:T(8,128)S(1)} %collective-permute-done.3.rest_4_), channel_id=1, source_target_pairs={{0,1},{1,0},{2,3},{3,2},{4,5},{5,4},{6,7},{7,6},{8,9},{9,8},{10,11... | collective-permute-start | bytes 393224 | tf_op jit(solution)/shard_map/ppermute | solution.py:304
  16.5 0.5 %collective-permute-done.7.rest_8_ = f32[8,32,128]{2,1,0:T(8,128)S(1)} collective-permute-done((f32[8,32,128]{2,1,0:T(8,128)S(1)}, f32[8,32,128]{2,1,0:T(8,128)S(1)}, u32[]{:S(2)}, u32[]{:S(2)}) %collective-permute-start.7) | collective-permute-done | bytes 131104 | tf_op jit(solution)/shard_map/ppermute | solution.py:304
  17.3 1.3 %gram.1 = (f32[32,512]{1,0:T(8,128)S(1)}, f32[32,512]{1,0:T(8,128)S(1)}, f32[32,512]{1,0:T(8,128)S(1)}, f32[32,512]{1,0:T(8,128)S(1)}, f32[32,512]{1,0:T(8,128)S(1)}) custom-call(s32[1,32]{1,0:T(1,128)S(1)} %copy-done.2, f32[32,128]{1,0:T(8,128)S(1)} %copy-done.1, f32[32,1024]{1,0:T(8,128)S(1)} %copy_bitcast_fusion.rest_0_, ...), custom_call_target="tpu_custom_call" | custom-call | tf_op jit(solution)/shard_map/gram/pallas_call | solution.py:336
  19.1 3.7 %collective-permute-start.12 = (f32[32,512]{1,0:T(8,128)S(1)}, f32[32,512]{1,0:T(8,128)S(1)}, u32[]{:S(2)}, u32[]{:S(2)}) collective-permute-start(f32[32,512]{1,0:T(8,128)S(1)} %get-tuple-element.40), channel_id=1, source_target_pairs={{0,4},{4,0},{1,5},{5,1},{2,6},{6,2},{3,7},{7,3},{8,12},{12,8},{9,1... | collective-permute-start | bytes 196616 | tf_op jit(solution)/shard_map/ppermute | solution.py:304
  22.8 1.6 %collective-permute-start.13 = (f32[32,512]{1,0:T(8,128)S(1)}, f32[32,512]{1,0:T(8,128)S(1)}, u32[]{:S(2)}, u32[]{:S(2)}) collective-permute-start(f32[32,512]{1,0:T(8,128)S(1)} %get-tuple-element.41), channel_id=1, source_target_pairs={{0,2},{2,0},{1,3},{3,1},{4,6},{6,4},{5,7},{7,5},{8,10},{10,8},{9,1... | collective-permute-start | bytes 196616 | tf_op jit(solution)/shard_map/ppermute | solution.py:304
  24.8 0.6 %collective-permute-done.12 = f32[32,512]{1,0:T(8,128)S(1)} collective-permute-done((f32[32,512]{1,0:T(8,128)S(1)}, f32[32,512]{1,0:T(8,128)S(1)}, u32[]{:S(2)}, u32[]{:S(2)}) %collective-permute-start.12) | collective-permute-done | bytes 65568 | tf_op jit(solution)/shard_map/ppermute | solution.py:304
  25.4 1.7 %collective-permute-done.13 = f32[32,512]{1,0:T(8,128)S(1)} collective-permute-done((f32[32,512]{1,0:T(8,128)S(1)}, f32[32,512]{1,0:T(8,128)S(1)}, u32[]{:S(2)}, u32[]{:S(2)}) %collective-permute-start.13) | collective-permute-done | bytes 65568 | tf_op jit(solution)/shard_map/ppermute | solution.py:304
  27.1 1.9 %collective-permute-start.16 = (f32[32,512]{1,0:T(8,128)S(1)}, f32[32,512]{1,0:T(8,128)S(1)}, u32[]{:S(2)}, u32[]{:S(2)}) collective-permute-start(f32[32,512]{1,0:T(8,128)S(1)} %add_add_fusion.rest_0_), channel_id=1, source_target_pairs={{0,12},{1,13},{2,14},{3,15},{4,8},{5,9},{6,10},{7,11},{8,4},{9,5},... | collective-permute-start | bytes 196616 | tf_op jit(solution)/shard_map/ppermute | solution.py:304
  29.0 1.3 %collective-permute-start.17 = (f32[32,512]{1,0:T(8,128)S(1)}, f32[32,512]{1,0:T(8,128)S(1)}, u32[]{:S(2)}, u32[]{:S(2)}) collective-permute-start(f32[32,512]{1,0:T(8,128)S(1)} %add_add_fusion.rest_0_), channel_id=1, source_target_pairs={{0,2},{1,3},{2,0},{3,1},{4,6},{5,7},{6,4},{7,5},{8,10},{9,11},{10,... | collective-permute-start | bytes 196616 | tf_op jit(solution)/shard_map/ppermute | solution.py:304
  30.3 2.9 %collective-permute-start.14 = (f32[32,512]{1,0:T(8,128)S(1)}, f32[32,512]{1,0:T(8,128)S(1)}, u32[]{:S(2)}, u32[]{:S(2)}) collective-permute-start(f32[32,512]{1,0:T(8,128)S(1)} %add_add_fusion.rest_0_), channel_id=1, source_target_pairs={{0,8},{1,9},{2,10},{3,11},{4,12},{5,13},{6,14},{7,15},{8,0},{9,1},... | collective-permute-start | bytes 196616 | tf_op jit(solution)/shard_map/ppermute | solution.py:304
  33.5 2.0 %collective-permute-start.20 = (f32[32,512]{1,0:T(8,128)S(1)}, f32[32,512]{1,0:T(8,128)S(1)}, u32[]{:S(2)}, u32[]{:S(2)}) collective-permute-start(f32[32,512]{1,0:T(8,128)S(1)} %collective-permute-done.16.rest_3_), channel_id=1, source_target_pairs={{0,2},{1,3},{2,0},{3,1},{4,6},{5,7},{6,4},{7,5},{8,10},{9,11},{10,... | collective-permute-start | bytes 196616 | tf_op jit(solution)/shard_map/ppermute | solution.py:304
  35.6 0.8 %collective-permute-start.19 = (f32[32,512]{1,0:T(8,128)S(1)}, f32[32,512]{1,0:T(8,128)S(1)}, u32[]{:S(2)}, u32[]{:S(2)}) collective-permute-start(f32[32,512]{1,0:T(8,128)S(1)} %collective-permute-done.15.rest_2_), channel_id=1, source_target_pairs={{0,2},{1,3},{2,0},{3,1},{4,6},{5,7},{6,4},{7,5},{8,10},{9,11},{10,... | collective-permute-start | bytes 196616 | tf_op jit(solution)/shard_map/ppermute | solution.py:304
  36.5 1.2 %collective-permute-start.18 = (f32[32,512]{1,0:T(8,128)S(1)}, f32[32,512]{1,0:T(8,128)S(1)}, u32[]{:S(2)}, u32[]{:S(2)}) collective-permute-start(f32[32,512]{1,0:T(8,128)S(1)} %collective-permute-done.14.rest_1_), channel_id=1, source_target_pairs={{0,2},{1,3},{2,0},{3,1},{4,6},{5,7},{6,4},{7,5},{8,10},{9,11},{10,... | collective-permute-start | bytes 196616 | tf_op jit(solution)/shard_map/ppermute | solution.py:304
  38.0 2.6 %collective-permute-done.19.rest_6_ = f32[32,512]{1,0:T(8,128)S(1)} collective-permute-done((f32[32,512]{1,0:T(8,128)S(1)}, f32[32,512]{1,0:T(8,128)S(1)}, u32[]{:S(2)}, u32[]{:S(2)}) %collective-permute-start.19) | collective-permute-done | bytes 65568 | tf_op jit(solution)/shard_map/ppermute | solution.py:304
  40.7 0.9 %collective-permute-done.18.rest_5_ = f32[32,512]{1,0:T(8,128)S(1)} collective-permute-done((f32[32,512]{1,0:T(8,128)S(1)}, f32[32,512]{1,0:T(8,128)S(1)}, u32[]{:S(2)}, u32[]{:S(2)}) %collective-permute-start.18) | collective-permute-done | bytes 65568 | tf_op jit(solution)/shard_map/ppermute | solution.py:304
  42.0 0.9 %collective-permute-done.22.rest_9_ = f32[64,512]{1,0:T(8,128)S(1)} collective-permute-done((f32[64,512]{1,0:T(8,128)S(1)}, f32[64,512]{1,0:T(8,128)S(1)}, u32[]{:S(2)}, u32[]{:S(2)}) %collective-permute-start.22) | collective-permute-done | bytes 131104 | tf_op jit(solution)/shard_map/ppermute | solution.py:304
  43.0 3.1 %descend.1 = (f32[512,128]{1,0:T(8,128)}, f32[32,128]{1,0:T(8,128)}) custom-call(f32[512,128]{1,0:T(8,128)S(1)} %copy-done, bf16[512,320]{1,0:T(8,128)(2,1)S(1)} %get-tuple-element.35.high_ref, bf16[512,320]{1,0:T(8,128)(2,1)S(1)} %get-tuple-element.36.low_ref, f32[32,512]{1,0:T(8,128)S(1)} %add_add_fusion.rest_0_, ...), custom_call_target="tpu_custom_call" | custom-call | tf_op jit(solution)/shard_map/descend/pallas_call | solution.py:384
  (43 shorter events, 3.4 us)
Async XLA Ops:
  4.5 7.6 %collective-permute-start.1 = (f32[8,32,128]{2,1,0:T(8,128)}, f32[8,32,128]{2,1,0:T(8,128)S(1)}, u32[]{:S(2)}, u32[]{:S(2)}) collective-permute-start(f32[8,32,128]{2,1,0:T(8,128)} %get-tuple-element.23), channel_id=1, source_target_pairs={{2,4},{4,2},{3,5},{5,3},{6,8},{8,6},{7,9},{9,7},{10,12},{12,10},{1... | collective-permute-start | bytes 393224 | tf_op jit(solution)/shard_map/ppermute | solution.py:304
  5.0 8.1 %collective-permute-start = (f32[8,32,128]{2,1,0:T(8,128)}, f32[8,32,128]{2,1,0:T(8,128)S(1)}, u32[]{:S(2)}, u32[]{:S(2)}) collective-permute-start(f32[8,32,128]{2,1,0:T(8,128)} %get-tuple-element.22), channel_id=1, source_target_pairs={{4,8},{8,4},{5,9},{9,5},{6,10},{10,6},{7,11},{11,7},{0,1},{1,0},{2... | collective-permute-start | bytes 393224 | tf_op jit(solution)/shard_map/ppermute | solution.py:304
  5.1 10.1 %collective-permute-start.2 = (f32[8,32,128]{2,1,0:T(8,128)}, f32[8,32,128]{2,1,0:T(8,128)S(1)}, u32[]{:S(2)}, u32[]{:S(2)}) collective-permute-start(f32[8,32,128]{2,1,0:T(8,128)} %get-tuple-element.29), channel_id=1, source_target_pairs={{0,4},{4,0},{1,5},{5,1},{2,6},{6,2},{3,7},{7,3},{8,12},{12,8},{9,1... | collective-permute-start | bytes 393224 | tf_op jit(solution)/shard_map/ppermute | solution.py:304
  10.5 5.2 %collective-permute-start.3 = (f32[8,32,128]{2,1,0:T(8,128)}, f32[8,32,128]{2,1,0:T(8,128)S(1)}, u32[]{:S(2)}, u32[]{:S(2)}) collective-permute-start(f32[8,32,128]{2,1,0:T(8,128)} %get-tuple-element.30), channel_id=1, source_target_pairs={{0,2},{2,0},{1,3},{3,1},{4,6},{6,4},{5,7},{7,5},{8,10},{10,8},{9,1... | collective-permute-start | bytes 393224 | tf_op jit(solution)/shard_map/ppermute | solution.py:304
  12.2 3.6 %collective-permute-start.4 = (f32[8,32,128]{2,1,0:T(8,128)}, f32[8,32,128]{2,1,0:T(8,128)S(1)}, u32[]{:S(2)}, u32[]{:S(2)}) collective-permute-start(f32[8,32,128]{2,1,0:T(8,128)} %get-tuple-element.25), channel_id=1, source_target_pairs={{0,1},{1,0},{2,3},{3,2},{4,5},{5,4},{6,7},{7,6},{8,9},{9,8},{10,11... | collective-permute-start | bytes 393224 | tf_op jit(solution)/shard_map/ppermute | solution.py:304
  13.1 3.1 %collective-permute-start.6 = (f32[8,32,128]{2,1,0:T(8,128)S(1)}, f32[8,32,128]{2,1,0:T(8,128)S(1)}, u32[]{:S(2)}, u32[]{:S(2)}) collective-permute-start(f32[8,32,128]{2,1,0:T(8,128)S(1)} %collective-permute-done.rest_2_), channel_id=1, source_target_pairs={{0,1},{1,0},{2,3},{3,2},{4,5},{5,4},{6,7},{7,6},{8,9},{9,8},{10,11... | collective-permute-start | bytes 393224 | tf_op jit(solution)/shard_map/ppermute | solution.py:304
  13.7 2.5 %collective-permute-start.9 = (bf16[512,128]{1,0:T(8,128)(2,1)S(1)}, bf16[512,128]{1,0:T(8,128)(2,1)S(1)}, u32[]{:S(2)}, u32[]{:S(2)}) collective-permute-start(bf16[512,128]{1,0:T(8,128)(2,1)S(1)} %convert_element_type.3.rest_10_), channel_id=1, source_target_pairs={{0,1},{1,0},{2,3},{3,2},{4,5},{5,4},{6,7},{7,6},{8,9},{9,8},{10,11... | collective-permute-start | bytes 393224 | tf_op jit(solution)/shard_map/ppermute | solution.py:304
  15.2 1.3 %collective-permute-start.5 = (f32[8,32,128]{2,1,0:T(8,128)S(1)}, f32[8,32,128]{2,1,0:T(8,128)S(1)}, u32[]{:S(2)}, u32[]{:S(2)}) collective-permute-start(f32[8,32,128]{2,1,0:T(8,128)S(1)} %collective-permute-done.1.rest_1_), channel_id=1, source_target_pairs={{0,1},{1,0},{2,3},{3,2},{4,5},{5,4},{6,7},{7,6},{8,9},{9,8},{10,11... | collective-permute-start | bytes 393224 | tf_op jit(solution)/shard_map/ppermute | solution.py:304
  15.7 1.5 %collective-permute-start.8 = (f32[8,32,128]{2,1,0:T(8,128)S(1)}, f32[8,32,128]{2,1,0:T(8,128)S(1)}, u32[]{:S(2)}, u32[]{:S(2)}) collective-permute-start(f32[8,32,128]{2,1,0:T(8,128)S(1)} %collective-permute-done.3.rest_4_), channel_id=1, source_target_pairs={{0,1},{1,0},{2,3},{3,2},{4,5},{5,4},{6,7},{7,6},{8,9},{9,8},{10,11... | collective-permute-start | bytes 393224 | tf_op jit(solution)/shard_map/ppermute | solution.py:304
  18.6 6.2 %collective-permute-start.10 = (f32[32,512]{1,0:T(8,128)S(1)}, f32[32,512]{1,0:T(8,128)S(1)}, u32[]{:S(2)}, u32[]{:S(2)}) collective-permute-start(f32[32,512]{1,0:T(8,128)S(1)} %get-tuple-element.38), channel_id=1, source_target_pairs={{2,4},{4,2},{3,5},{5,3},{6,8},{8,6},{7,9},{9,7},{10,12},{12,10},{1... | collective-permute-start | bytes 196616 | tf_op jit(solution)/shard_map/ppermute | solution.py:304
  18.9 5.8 %collective-permute-start.11 = (f32[32,512]{1,0:T(8,128)S(1)}, f32[32,512]{1,0:T(8,128)S(1)}, u32[]{:S(2)}, u32[]{:S(2)}) collective-permute-start(f32[32,512]{1,0:T(8,128)S(1)} %get-tuple-element.39), channel_id=1, source_target_pairs={{4,8},{8,4},{5,9},{9,5},{6,10},{10,6},{7,11},{11,7},{0,1},{1,0},{2... | collective-permute-start | bytes 196616 | tf_op jit(solution)/shard_map/ppermute | solution.py:304
  19.1 6.3 %collective-permute-start.12 = (f32[32,512]{1,0:T(8,128)S(1)}, f32[32,512]{1,0:T(8,128)S(1)}, u32[]{:S(2)}, u32[]{:S(2)}) collective-permute-start(f32[32,512]{1,0:T(8,128)S(1)} %get-tuple-element.40), channel_id=1, source_target_pairs={{0,4},{4,0},{1,5},{5,1},{2,6},{6,2},{3,7},{7,3},{8,12},{12,8},{9,1... | collective-permute-start | bytes 196616 | tf_op jit(solution)/shard_map/ppermute | solution.py:304
  22.8 4.3 %collective-permute-start.13 = (f32[32,512]{1,0:T(8,128)S(1)}, f32[32,512]{1,0:T(8,128)S(1)}, u32[]{:S(2)}, u32[]{:S(2)}) collective-permute-start(f32[32,512]{1,0:T(8,128)S(1)} %get-tuple-element.41), channel_id=1, source_target_pairs={{0,2},{2,0},{1,3},{3,1},{4,6},{6,4},{5,7},{7,5},{8,10},{10,8},{9,1... | collective-permute-start | bytes 196616 | tf_op jit(solution)/shard_map/ppermute | solution.py:304
  27.1 6.4 %collective-permute-start.16 = (f32[32,512]{1,0:T(8,128)S(1)}, f32[32,512]{1,0:T(8,128)S(1)}, u32[]{:S(2)}, u32[]{:S(2)}) collective-permute-start(f32[32,512]{1,0:T(8,128)S(1)} %add_add_fusion.rest_0_), channel_id=1, source_target_pairs={{0,12},{1,13},{2,14},{3,15},{4,8},{5,9},{6,10},{7,11},{8,4},{9,5},... | collective-permute-start | bytes 196616 | tf_op jit(solution)/shard_map/ppermute | solution.py:304
  29.0 6.5 %collective-permute-start.17 = (f32[32,512]{1,0:T(8,128)S(1)}, f32[32,512]{1,0:T(8,128)S(1)}, u32[]{:S(2)}, u32[]{:S(2)}) collective-permute-start(f32[32,512]{1,0:T(8,128)S(1)} %add_add_fusion.rest_0_), channel_id=1, source_target_pairs={{0,2},{1,3},{2,0},{3,1},{4,6},{5,7},{6,4},{7,5},{8,10},{9,11},{10,... | collective-permute-start | bytes 196616 | tf_op jit(solution)/shard_map/ppermute | solution.py:304
  30.3 5.3 %collective-permute-start.15 = (f32[32,512]{1,0:T(8,128)S(1)}, f32[32,512]{1,0:T(8,128)S(1)}, u32[]{:S(2)}, u32[]{:S(2)}) collective-permute-start(f32[32,512]{1,0:T(8,128)S(1)} %add_add_fusion.rest_0_), channel_id=1, source_target_pairs={{0,4},{1,5},{2,6},{3,7},{4,0},{5,1},{6,2},{7,3},{8,12},{9,13},{10,... | collective-permute-start | bytes 196616 | tf_op jit(solution)/shard_map/ppermute | solution.py:304
  30.3 6.2 %collective-permute-start.14 = (f32[32,512]{1,0:T(8,128)S(1)}, f32[32,512]{1,0:T(8,128)S(1)}, u32[]{:S(2)}, u32[]{:S(2)}) collective-permute-start(f32[32,512]{1,0:T(8,128)S(1)} %add_add_fusion.rest_0_), channel_id=1, source_target_pairs={{0,8},{1,9},{2,10},{3,11},{4,12},{5,13},{6,14},{7,15},{8,0},{9,1},... | collective-permute-start | bytes 196616 | tf_op jit(solution)/shard_map/ppermute | solution.py:304
  33.5 4.4 %collective-permute-start.20 = (f32[32,512]{1,0:T(8,128)S(1)}, f32[32,512]{1,0:T(8,128)S(1)}, u32[]{:S(2)}, u32[]{:S(2)}) collective-permute-start(f32[32,512]{1,0:T(8,128)S(1)} %collective-permute-done.16.rest_3_), channel_id=1, source_target_pairs={{0,2},{1,3},{2,0},{3,1},{4,6},{5,7},{6,4},{7,5},{8,10},{9,11},{10,... | collective-permute-start | bytes 196616 | tf_op jit(solution)/shard_map/ppermute | solution.py:304
  35.5 6.1 %collective-permute-start.21 = (f32[64,512]{1,0:T(8,128)S(1)}, f32[64,512]{1,0:T(8,128)S(1)}, u32[]{:S(2)}, u32[]{:S(2)}) collective-permute-start(f32[64,512]{1,0:T(8,128)S(1)} %pad_maximum_fusion), channel_id=1, source_target_pairs={{0,1},{1,0},{2,3},{3,2},{4,5},{5,4},{6,7},{7,6},{8,9},{9,8},{10,11... | collective-permute-start | bytes 393224 | tf_op jit(solution)/shard_map/ppermute | solution.py:304
  35.6 5.0 %collective-permute-start.19 = (f32[32,512]{1,0:T(8,128)S(1)}, f32[32,512]{1,0:T(8,128)S(1)}, u32[]{:S(2)}, u32[]{:S(2)}) collective-permute-start(f32[32,512]{1,0:T(8,128)S(1)} %collective-permute-done.15.rest_2_), channel_id=1, source_target_pairs={{0,2},{1,3},{2,0},{3,1},{4,6},{5,7},{6,4},{7,5},{8,10},{9,11},{10,... | collective-permute-start | bytes 196616 | tf_op jit(solution)/shard_map/ppermute | solution.py:304
  36.5 5.1 %collective-permute-start.18 = (f32[32,512]{1,0:T(8,128)S(1)}, f32[32,512]{1,0:T(8,128)S(1)}, u32[]{:S(2)}, u32[]{:S(2)}) collective-permute-start(f32[32,512]{1,0:T(8,128)S(1)} %collective-permute-done.14.rest_1_), channel_id=1, source_target_pairs={{0,2},{1,3},{2,0},{3,1},{4,6},{5,7},{6,4},{7,5},{8,10},{9,11},{10,... | collective-permute-start | bytes 196616 | tf_op jit(solution)/shard_map/ppermute | solution.py:304
  37.9 3.7 %collective-permute-start.24 = (f32[64,512]{1,0:T(8,128)S(1)}, f32[64,512]{1,0:T(8,128)S(1)}, u32[]{:S(2)}, u32[]{:S(2)}) collective-permute-start(f32[64,512]{1,0:T(8,128)S(1)} %pad_maximum_fusion.3), channel_id=1, source_target_pairs={{0,1},{1,0},{2,3},{3,2},{4,5},{5,4},{6,7},{7,6},{8,9},{9,8},{10,11... | collective-permute-start | bytes 393224 | tf_op jit(solution)/shard_map/ppermute | solution.py:304
  40.6 1.4 %collective-permute-start.23 = (f32[64,512]{1,0:T(8,128)S(1)}, f32[64,512]{1,0:T(8,128)S(1)}, u32[]{:S(2)}, u32[]{:S(2)}) collective-permute-start(f32[64,512]{1,0:T(8,128)S(1)} %pad_maximum_fusion.2), channel_id=1, source_target_pairs={{0,1},{1,0},{2,3},{3,2},{4,5},{5,4},{6,7},{7,6},{8,9},{9,8},{10,11... | collective-permute-start | bytes 393224 | tf_op jit(solution)/shard_map/ppermute | solution.py:304
  41.5 1.4 %collective-permute-start.22 = (f32[64,512]{1,0:T(8,128)S(1)}, f32[64,512]{1,0:T(8,128)S(1)}, u32[]{:S(2)}, u32[]{:S(2)}) collective-permute-start(f32[64,512]{1,0:T(8,128)S(1)} %pad_maximum_fusion.1), channel_id=1, source_target_pairs={{0,1},{1,0},{2,3},{3,2},{4,5},{5,4},{6,7},{7,6},{8,9},{9,8},{10,11... | collective-permute-start | bytes 393224 | tf_op jit(solution)/shard_map/ppermute | solution.py:304
  (4 other events, 46.1 us)

commit v4 on v3

--- a/solution.py
+++ b/solution.py
@@ -238,52 +238,59 @@
         rows = lower[p * plane : (p + 1) * plane]
         diagonal = rows[:, 2 * plane :]
         diagonal = jnp.where(half_row & half_col, diagonal.T, diagonal)
-        after = []
+        whole = {0: diagonal}
         for step in (1, 2):
+            if p - step >= 0:
+                whole[-step] = rows[:, (2 - step) * plane : (3 - step) * plane]
             if p + step < planes:
                 following = lower[(p + step) * plane : (p + step + 1) * plane]
-                after.append(following[:, (2 - step) * plane : (3 - step) * plane].T)
-            else:
-                after.append(jnp.zeros((plane, plane), F32))
-        whole = [rows[:, :plane], rows[:, plane : 2 * plane], diagonal] + after
-        for index, part in enumerate(whole):
+                whole[step] = following[:, (2 - step) * plane : (3 - step) * plane].T
+        for step, part in whole.items():
             top, rest_of = split(part)
-            band[p, :plane, index * plane : (index + 1) * plane] = top
-            band[p, plane:, index * plane : (index + 1) * plane] = rest_of
-    shares[:, : 2 * plane] = jnp.zeros((ITERS, 2 * plane, columns), BF16)
-    shares[:, (planes + 2) * plane :] = jnp.zeros((ITERS, 2 * plane, columns), BF16)
+            at = (step + 2) * plane
+            band[p, :plane, at : at + plane] = top
+            band[p, plane:, at : at + plane] = rest_of
+    shares[: 2 * plane] = jnp.zeros((2 * plane, ITERS * columns), BF16)
+    shares[(planes + 2) * plane :] = jnp.zeros((2 * plane, ITERS * columns), BF16)
+    first = pl.multiple_of((me // 2 - CHIP_REACH) * span + 2 * plane, span)
     steps = []
     for iteration in range(ITERS):
-        shares[iteration, 2 * plane : (planes + 2) * plane] = (
+        lanes = slice(iteration * columns, (iteration + 1) * columns)
+        shares[2 * plane : (planes + 2) * plane, lanes] = (
             misfit[...] / counts[...]
         ).astype(BF16)
+        if iteration == ITERS - 1:
+            near = shares[pl.ds(first, WINDOW * span)]
+            gradients = jnp.dot(
+                high_ref[...], near, preferred_element_type=F32
+            ) + jnp.dot(low_ref[...], near, preferred_element_type=F32)
         power = jnp.zeros((plane, columns), F32)
         curvature = jnp.zeros((plane, columns), F32)
         for p in range(planes):
+            start, stop = max(p - 2, 0), min(p + 3, planes)
             both = jnp.dot(
-                band[p],
-                shares[iteration, p * plane : (p + 5) * plane],
+                band[p, :, (start - p + 2) * plane : (stop - p + 2) * plane],
+                shares[(start + 2) * plane : (stop + 2) * plane, lanes],
                 preferred_element_type=F32,
             )
             swept = both[:plane] + both[plane:]
-            here = shares[iteration, (p + 2) * plane : (p + 3) * plane].astype(F32)
+            here = shares[(p + 2) * plane : (p + 3) * plane, lanes].astype(F32)
             image = swept / counts[p * plane : (p + 1) * plane]
             warm[p * plane : (p + 1) * plane] = image
             power = power + here * swept
             curvature = curvature + image * image
         step = jnp.sum(power) / (jnp.sum(curvature) + 1e-06)
         steps.append(step)
-        misfit[...] = misfit[...] - step * warm[...]
-    misfit_out[...] = misfit[pl.ds(pl.multiple_of(me * bores, bores), bores)]
-    first = pl.multiple_of((me // 2 - CHIP_REACH) * span + 2 * plane, span)
+        if iteration < ITERS - 1:
+            misfit[...] = misfit[...] - step * warm[...]
+    mine = pl.ds(pl.multiple_of(me * bores, bores), bores)
+    misfit_out[...] = misfit[mine] - steps[-1] * warm[mine]
     fetch.wait()
     heat = heat_ref[...]
     for iteration in range(ITERS):
-        near = shares[iteration, pl.ds(first, WINDOW * span)]
-        gradient = jnp.dot(high_ref[...], near, preferred_element_type=F32) + jnp.dot(
-            low_ref[...], near, preferred_element_type=F32
-        )
-        heat = heat - steps[iteration] * gradient
+        heat = heat - steps[iteration] * gradients[
+            :, iteration * columns : (iteration + 1) * columns
+        ]
     heat_out[...] = heat
 
 
@@ -395,7 +402,7 @@
             pltpu.VMEM((ranks * bores, columns), F32),
             pltpu.VMEM((ranks * bores, columns), F32),
             pltpu.VMEM((ranks * bores, columns), F32),
-            pltpu.VMEM((ITERS, (ranks + 16) * bores, columns), BF16),
+            pltpu.VMEM(((ranks + 16) * bores, ITERS * columns), BF16),
             pltpu.VMEM((seg_rows, columns), F32),
             pltpu.SemaphoreType.DMA,
         ],

time: 46.2 us -> 45.7 us (0.989)
  Pallas kernels: 8.57 us -> 8.05 us
    pallas_call x1, Pallas kernels: 3.08 us -> 2.57 us  [on_device(): pl.pallas_call(functools.partial(descend_kernel, ranks, places), out_shap...]
where the time goes in v4:
time: 45.7 us; the launch traced here: 45.6 us
  starting transfers between devices  25.3 us (55%)
  waiting for transfers between devices  10.4 us (23%)
  Pallas kernels  8.05 us (18%)
  local copies, waits for them, and re-layouts  0.93 us (2%)
  between operations  0.81 us (2%)
    ppermute x25, starting transfers between devices, send(): return lax.ppermute(value, 'rows', pairs)  25.3 us
    ppermute x25, waiting for transfers between devices, send(): return lax.ppermute(value, 'rows', pairs)  10.4 us
    pallas_call x1, Pallas kernels, on_device(): pl.pallas_call(compress_kernel, out_shape=(piece,) * WINDOW, in_specs=[HB...  3.87 us
    pallas_call x1, Pallas kernels, on_device(): pl.pallas_call(functools.partial(descend_kernel, ranks, places), out_shap...  2.57 us
    pallas_call x1, Pallas kernels, on_device(): pl.pallas_call(gram_kernel, out_shape=(packed,) * WINDOW, in_specs=[VMEM]...  1.28 us
    reshape x1, local copies, waits for them, and re-layouts, on_device(): own = own.transpose(1, 0, 2).reshape(bores, per_chip * tile)  0.92 us
  transfers between devices with their start and end apart: 25, of which 13 were waited for; matrix products, arithmetic and copies ran while one was open for 2% of the time, Pallas kernels for 1%

profile of v4, /device:TPU:0, one launch (start us, length us, event | category | flops | bytes accessed | tf_op | source)
XLA Modules:
  0.0 45.6 jit_solution(9139499070164576390)
XLA Ops:
  0.7 3.9 %compress.1 = (f32[8,32,128]{2,1,0:T(8,128)}, f32[8,32,128]{2,1,0:T(8,128)}, f32[8,32,128]{2,1,0:T(8,128)}, f32[8,32,128]{2,1,0:T(8,128)}, f32[8,32,128]{2,1,0:T(8,128)}) custom-call(s32[4,30]{1,0:T(4,128)} %cols_hbm.1, s32[4]{0:T(128)} %count_hbm.1, s32[1,32]{1,0:T(1,128)} %lengths_ref.1, bf16[4,30,128,128]{3,2,1,0:T(8,128)(2,1)} %tiles_hbm.1), custom_call_target="tpu_custom_call" | custom-call | tf_op jit(solution)/shard_map/compress/pallas_call | solution.py:317
  4.5 0.5 %collective-permute-start.1 = (f32[8,32,128]{2,1,0:T(8,128)}, f32[8,32,128]{2,1,0:T(8,128)S(1)}, u32[]{:S(2)}, u32[]{:S(2)}) collective-permute-start(f32[8,32,128]{2,1,0:T(8,128)} %get-tuple-element.23), channel_id=1, source_target_pairs={{2,4},{4,2},{3,5},{5,3},{6,8},{8,6},{7,9},{9,7},{10,12},{12,10},{1... | collective-permute-start | bytes 393224 | tf_op jit(solution)/shard_map/ppermute | solution.py:311
  5.1 5.4 %collective-permute-start.2 = (f32[8,32,128]{2,1,0:T(8,128)}, f32[8,32,128]{2,1,0:T(8,128)S(1)}, u32[]{:S(2)}, u32[]{:S(2)}) collective-permute-start(f32[8,32,128]{2,1,0:T(8,128)} %get-tuple-element.29), channel_id=1, source_target_pairs={{0,4},{4,0},{1,5},{5,1},{2,6},{6,2},{3,7},{7,3},{8,12},{12,8},{9,1... | collective-permute-start | bytes 393224 | tf_op jit(solution)/shard_map/ppermute | solution.py:311
  10.5 1.7 %collective-permute-start.3 = (f32[8,32,128]{2,1,0:T(8,128)}, f32[8,32,128]{2,1,0:T(8,128)S(1)}, u32[]{:S(2)}, u32[]{:S(2)}) collective-permute-start(f32[8,32,128]{2,1,0:T(8,128)} %get-tuple-element.30), channel_id=1, source_target_pairs={{0,2},{2,0},{1,3},{3,1},{4,6},{6,4},{5,7},{7,5},{8,10},{10,8},{9,1... | collective-permute-start | bytes 393224 | tf_op jit(solution)/shard_map/ppermute | solution.py:311
  12.2 0.9 %copy_bitcast_fusion.rest_0_ = f32[32,1024]{1,0:T(8,128)S(1)} fusion(f32[8,32,128]{2,1,0:T(8,128)} %get-tuple-element.25), kind=kLoop, calls=%fused_computation | loop fusion | bytes 262144 | tf_op jit(solution)/shard_map/reshape | solution.py:338
  13.2 0.6 %collective-permute-start.6 = (f32[8,32,128]{2,1,0:T(8,128)S(1)}, f32[8,32,128]{2,1,0:T(8,128)S(1)}, u32[]{:S(2)}, u32[]{:S(2)}) collective-permute-start(f32[8,32,128]{2,1,0:T(8,128)S(1)} %collective-permute-done.rest_2_), channel_id=1, source_target_pairs={{0,1},{1,0},{2,3},{3,2},{4,5},{5,4},{6,7},{7,6},{8,9},{9,8},{10,11... | collective-permute-start | bytes 393224 | tf_op jit(solution)/shard_map/ppermute | solution.py:311
  13.8 1.4 %collective-permute-done.2.rest_3_ = f32[8,32,128]{2,1,0:T(8,128)S(1)} collective-permute-done((f32[8,32,128]{2,1,0:T(8,128)}, f32[8,32,128]{2,1,0:T(8,128)S(1)}, u32[]{:S(2)}, u32[]{:S(2)}) %collective-permute-start.2) | collective-permute-done | bytes 131104 | tf_op jit(solution)/shard_map/ppermute | solution.py:311
  15.2 0.5 %collective-permute-done.3.rest_4_ = f32[8,32,128]{2,1,0:T(8,128)S(1)} collective-permute-done((f32[8,32,128]{2,1,0:T(8,128)}, f32[8,32,128]{2,1,0:T(8,128)S(1)}, u32[]{:S(2)}, u32[]{:S(2)}) %collective-permute-start.3) | collective-permute-done | bytes 131104 | tf_op jit(solution)/shard_map/ppermute | solution.py:311
  16.6 0.5 %collective-permute-done.7.rest_8_ = f32[8,32,128]{2,1,0:T(8,128)S(1)} collective-permute-done((f32[8,32,128]{2,1,0:T(8,128)S(1)}, f32[8,32,128]{2,1,0:T(8,128)S(1)}, u32[]{:S(2)}, u32[]{:S(2)}) %collective-permute-start.7) | collective-permute-done | bytes 131104 | tf_op jit(solution)/shard_map/ppermute | solution.py:311
  17.2 1.3 %gram.1 = (f32[32,512]{1,0:T(8,128)S(1)}, f32[32,512]{1,0:T(8,128)S(1)}, f32[32,512]{1,0:T(8,128)S(1)}, f32[32,512]{1,0:T(8,128)S(1)}, f32[32,512]{1,0:T(8,128)S(1)}) custom-call(s32[1,32]{1,0:T(1,128)S(1)} %copy-done.2, f32[32,128]{1,0:T(8,128)S(1)} %copy-done.1, f32[32,1024]{1,0:T(8,128)S(1)} %copy_bitcast_fusion.rest_0_, ...), custom_call_target="tpu_custom_call" | custom-call | tf_op jit(solution)/shard_map/gram/pallas_call | solution.py:343
  19.1 3.7 %collective-permute-start.12 = (f32[32,512]{1,0:T(8,128)S(1)}, f32[32,512]{1,0:T(8,128)S(1)}, u32[]{:S(2)}, u32[]{:S(2)}) collective-permute-start(f32[32,512]{1,0:T(8,128)S(1)} %get-tuple-element.40), channel_id=1, source_target_pairs={{0,4},{4,0},{1,5},{5,1},{2,6},{6,2},{3,7},{7,3},{8,12},{12,8},{9,1... | collective-permute-start | bytes 196616 | tf_op jit(solution)/shard_map/ppermute | solution.py:311
  22.8 1.7 %collective-permute-start.13 = (f32[32,512]{1,0:T(8,128)S(1)}, f32[32,512]{1,0:T(8,128)S(1)}, u32[]{:S(2)}, u32[]{:S(2)}) collective-permute-start(f32[32,512]{1,0:T(8,128)S(1)} %get-tuple-element.41), channel_id=1, source_target_pairs={{0,2},{2,0},{1,3},{3,1},{4,6},{6,4},{5,7},{7,5},{8,10},{10,8},{9,1... | collective-permute-start | bytes 196616 | tf_op jit(solution)/shard_map/ppermute | solution.py:311
  24.8 0.6 %collective-permute-done.12 = f32[32,512]{1,0:T(8,128)S(1)} collective-permute-done((f32[32,512]{1,0:T(8,128)S(1)}, f32[32,512]{1,0:T(8,128)S(1)}, u32[]{:S(2)}, u32[]{:S(2)}) %collective-permute-start.12) | collective-permute-done | bytes 65568 | tf_op jit(solution)/shard_map/ppermute | solution.py:311
  25.4 1.6 %collective-permute-done.13 = f32[32,512]{1,0:T(8,128)S(1)} collective-permute-done((f32[32,512]{1,0:T(8,128)S(1)}, f32[32,512]{1,0:T(8,128)S(1)}, u32[]{:S(2)}, u32[]{:S(2)}) %collective-permute-start.13) | collective-permute-done | bytes 65568 | tf_op jit(solution)/shard_map/ppermute | solution.py:311
  27.1 1.9 %collective-permute-start.16 = (f32[32,512]{1,0:T(8,128)S(1)}, f32[32,512]{1,0:T(8,128)S(1)}, u32[]{:S(2)}, u32[]{:S(2)}) collective-permute-start(f32[32,512]{1,0:T(8,128)S(1)} %add_add_fusion.rest_0_), channel_id=1, source_target_pairs={{0,12},{1,13},{2,14},{3,15},{4,8},{5,9},{6,10},{7,11},{8,4},{9,5},... | collective-permute-start | bytes 196616 | tf_op jit(solution)/shard_map/ppermute | solution.py:311
  29.0 1.3 %collective-permute-start.17 = (f32[32,512]{1,0:T(8,128)S(1)}, f32[32,512]{1,0:T(8,128)S(1)}, u32[]{:S(2)}, u32[]{:S(2)}) collective-permute-start(f32[32,512]{1,0:T(8,128)S(1)} %add_add_fusion.rest_0_), channel_id=1, source_target_pairs={{0,2},{1,3},{2,0},{3,1},{4,6},{5,7},{6,4},{7,5},{8,10},{9,11},{10,... | collective-permute-start | bytes 196616 | tf_op jit(solution)/shard_map/ppermute | solution.py:311
  30.3 2.9 %collective-permute-start.14 = (f32[32,512]{1,0:T(8,128)S(1)}, f32[32,512]{1,0:T(8,128)S(1)}, u32[]{:S(2)}, u32[]{:S(2)}) collective-permute-start(f32[32,512]{1,0:T(8,128)S(1)} %add_add_fusion.rest_0_), channel_id=1, source_target_pairs={{0,8},{1,9},{2,10},{3,11},{4,12},{5,13},{6,14},{7,15},{8,0},{9,1},... | collective-permute-start | bytes 196616 | tf_op jit(solution)/shard_map/ppermute | solution.py:311
  33.5 2.1 %collective-permute-start.20 = (f32[32,512]{1,0:T(8,128)S(1)}, f32[32,512]{1,0:T(8,128)S(1)}, u32[]{:S(2)}, u32[]{:S(2)}) collective-permute-start(f32[32,512]{1,0:T(8,128)S(1)} %collective-permute-done.16.rest_3_), channel_id=1, source_target_pairs={{0,2},{1,3},{2,0},{3,1},{4,6},{5,7},{6,4},{7,5},{8,10},{9,11},{10,... | collective-permute-start | bytes 196616 | tf_op jit(solution)/shard_map/ppermute | solution.py:311
  35.7 0.8 %collective-permute-start.19 = (f32[32,512]{1,0:T(8,128)S(1)}, f32[32,512]{1,0:T(8,128)S(1)}, u32[]{:S(2)}, u32[]{:S(2)}) collective-permute-start(f32[32,512]{1,0:T(8,128)S(1)} %collective-permute-done.15.rest_2_), channel_id=1, source_target_pairs={{0,2},{1,3},{2,0},{3,1},{4,6},{5,7},{6,4},{7,5},{8,10},{9,11},{10,... | collective-permute-start | bytes 196616 | tf_op jit(solution)/shard_map/ppermute | solution.py:311
  36.5 1.3 %collective-permute-start.18 = (f32[32,512]{1,0:T(8,128)S(1)}, f32[32,512]{1,0:T(8,128)S(1)}, u32[]{:S(2)}, u32[]{:S(2)}) collective-permute-start(f32[32,512]{1,0:T(8,128)S(1)} %collective-permute-done.14.rest_1_), channel_id=1, source_target_pairs={{0,2},{1,3},{2,0},{3,1},{4,6},{5,7},{6,4},{7,5},{8,10},{9,11},{10,... | collective-permute-start | bytes 196616 | tf_op jit(solution)/shard_map/ppermute | solution.py:311
  38.0 2.6 %collective-permute-done.19.rest_6_ = f32[32,512]{1,0:T(8,128)S(1)} collective-permute-done((f32[32,512]{1,0:T(8,128)S(1)}, f32[32,512]{1,0:T(8,128)S(1)}, u32[]{:S(2)}, u32[]{:S(2)}) %collective-permute-start.19) | collective-permute-done | bytes 65568 | tf_op jit(solution)/shard_map/ppermute | solution.py:311
  40.7 0.9 %collective-permute-done.18.rest_5_ = f32[32,512]{1,0:T(8,128)S(1)} collective-permute-done((f32[32,512]{1,0:T(8,128)S(1)}, f32[32,512]{1,0:T(8,128)S(1)}, u32[]{:S(2)}, u32[]{:S(2)}) %collective-permute-start.18) | collective-permute-done | bytes 65568 | tf_op jit(solution)/shard_map/ppermute | solution.py:311
  42.0 0.9 %collective-permute-done.22.rest_9_ = f32[64,512]{1,0:T(8,128)S(1)} collective-permute-done((f32[64,512]{1,0:T(8,128)S(1)}, f32[64,512]{1,0:T(8,128)S(1)}, u32[]{:S(2)}, u32[]{:S(2)}) %collective-permute-start.22) | collective-permute-done | bytes 131104 | tf_op jit(solution)/shard_map/ppermute | solution.py:311
  43.0 2.6 %descend.1 = (f32[512,128]{1,0:T(8,128)}, f32[32,128]{1,0:T(8,128)}) custom-call(f32[512,128]{1,0:T(8,128)S(1)} %copy-done, bf16[512,320]{1,0:T(8,128)(2,1)S(1)} %get-tuple-element.35.high_ref, bf16[512,320]{1,0:T(8,128)(2,1)S(1)} %get-tuple-element.36.low_ref, f32[32,512]{1,0:T(8,128)S(1)} %add_add_fusion.rest_0_, ...), custom_call_target="tpu_custom_call" | custom-call | tf_op jit(solution)/shard_map/descend/pallas_call | solution.py:391
  (43 shorter events, 3.4 us)
Async XLA Ops:
  4.5 7.7 %collective-permute-start.1 = (f32[8,32,128]{2,1,0:T(8,128)}, f32[8,32,128]{2,1,0:T(8,128)S(1)}, u32[]{:S(2)}, u32[]{:S(2)}) collective-permute-start(f32[8,32,128]{2,1,0:T(8,128)} %get-tuple-element.23), channel_id=1, source_target_pairs={{2,4},{4,2},{3,5},{5,3},{6,8},{8,6},{7,9},{9,7},{10,12},{12,10},{1... | collective-permute-start | bytes 393224 | tf_op jit(solution)/shard_map/ppermute | solution.py:311
  5.1 8.1 %collective-permute-start = (f32[8,32,128]{2,1,0:T(8,128)}, f32[8,32,128]{2,1,0:T(8,128)S(1)}, u32[]{:S(2)}, u32[]{:S(2)}) collective-permute-start(f32[8,32,128]{2,1,0:T(8,128)} %get-tuple-element.22), channel_id=1, source_target_pairs={{4,8},{8,4},{5,9},{9,5},{6,10},{10,6},{7,11},{11,7},{0,1},{1,0},{2... | collective-permute-start | bytes 393224 | tf_op jit(solution)/shard_map/ppermute | solution.py:311
  5.1 10.1 %collective-permute-start.2 = (f32[8,32,128]{2,1,0:T(8,128)}, f32[8,32,128]{2,1,0:T(8,128)S(1)}, u32[]{:S(2)}, u32[]{:S(2)}) collective-permute-start(f32[8,32,128]{2,1,0:T(8,128)} %get-tuple-element.29), channel_id=1, source_target_pairs={{0,4},{4,0},{1,5},{5,1},{2,6},{6,2},{3,7},{7,3},{8,12},{12,8},{9,1... | collective-permute-start | bytes 393224 | tf_op jit(solution)/shard_map/ppermute | solution.py:311
  10.5 5.2 %collective-permute-start.3 = (f32[8,32,128]{2,1,0:T(8,128)}, f32[8,32,128]{2,1,0:T(8,128)S(1)}, u32[]{:S(2)}, u32[]{:S(2)}) collective-permute-start(f32[8,32,128]{2,1,0:T(8,128)} %get-tuple-element.30), channel_id=1, source_target_pairs={{0,2},{2,0},{1,3},{3,1},{4,6},{6,4},{5,7},{7,5},{8,10},{10,8},{9,1... | collective-permute-start | bytes 393224 | tf_op jit(solution)/shard_map/ppermute | solution.py:311
  12.2 3.5 %collective-permute-start.4 = (f32[8,32,128]{2,1,0:T(8,128)}, f32[8,32,128]{2,1,0:T(8,128)S(1)}, u32[]{:S(2)}, u32[]{:S(2)}) collective-permute-start(f32[8,32,128]{2,1,0:T(8,128)} %get-tuple-element.25), channel_id=1, source_target_pairs={{0,1},{1,0},{2,3},{3,2},{4,5},{5,4},{6,7},{7,6},{8,9},{9,8},{10,11... | collective-permute-start | bytes 393224 | tf_op jit(solution)/shard_map/ppermute | solution.py:311
  13.2 3.1 %collective-permute-start.6 = (f32[8,32,128]{2,1,0:T(8,128)S(1)}, f32[8,32,128]{2,1,0:T(8,128)S(1)}, u32[]{:S(2)}, u32[]{:S(2)}) collective-permute-start(f32[8,32,128]{2,1,0:T(8,128)S(1)} %collective-permute-done.rest_2_), channel_id=1, source_target_pairs={{0,1},{1,0},{2,3},{3,2},{4,5},{5,4},{6,7},{7,6},{8,9},{9,8},{10,11... | collective-permute-start | bytes 393224 | tf_op jit(solution)/shard_map/ppermute | solution.py:311
  13.7 2.5 %collective-permute-start.9 = (bf16[512,128]{1,0:T(8,128)(2,1)S(1)}, bf16[512,128]{1,0:T(8,128)(2,1)S(1)}, u32[]{:S(2)}, u32[]{:S(2)}) collective-permute-start(bf16[512,128]{1,0:T(8,128)(2,1)S(1)} %convert_element_type.3.rest_10_), channel_id=1, source_target_pairs={{0,1},{1,0},{2,3},{3,2},{4,5},{5,4},{6,7},{7,6},{8,9},{9,8},{10,11... | collective-permute-start | bytes 393224 | tf_op jit(solution)/shard_map/ppermute | solution.py:311
  15.2 1.3 %collective-permute-start.5 = (f32[8,32,128]{2,1,0:T(8,128)S(1)}, f32[8,32,128]{2,1,0:T(8,128)S(1)}, u32[]{:S(2)}, u32[]{:S(2)}) collective-permute-start(f32[8,32,128]{2,1,0:T(8,128)S(1)} %collective-permute-done.1.rest_1_), channel_id=1, source_target_pairs={{0,1},{1,0},{2,3},{3,2},{4,5},{5,4},{6,7},{7,6},{8,9},{9,8},{10,11... | collective-permute-start | bytes 393224 | tf_op jit(solution)/shard_map/ppermute | solution.py:311
  15.7 1.5 %collective-permute-start.8 = (f32[8,32,128]{2,1,0:T(8,128)S(1)}, f32[8,32,128]{2,1,0:T(8,128)S(1)}, u32[]{:S(2)}, u32[]{:S(2)}) collective-permute-start(f32[8,32,128]{2,1,0:T(8,128)S(1)} %collective-permute-done.3.rest_4_), channel_id=1, source_target_pairs={{0,1},{1,0},{2,3},{3,2},{4,5},{5,4},{6,7},{7,6},{8,9},{9,8},{10,11... | collective-permute-start | bytes 393224 | tf_op jit(solution)/shard_map/ppermute | solution.py:311
  18.5 6.2 %collective-permute-start.10 = (f32[32,512]{1,0:T(8,128)S(1)}, f32[32,512]{1,0:T(8,128)S(1)}, u32[]{:S(2)}, u32[]{:S(2)}) collective-permute-start(f32[32,512]{1,0:T(8,128)S(1)} %get-tuple-element.38), channel_id=1, source_target_pairs={{2,4},{4,2},{3,5},{5,3},{6,8},{8,6},{7,9},{9,7},{10,12},{12,10},{1... | collective-permute-start | bytes 196616 | tf_op jit(solution)/shard_map/ppermute | solution.py:311
  18.9 5.9 %collective-permute-start.11 = (f32[32,512]{1,0:T(8,128)S(1)}, f32[32,512]{1,0:T(8,128)S(1)}, u32[]{:S(2)}, u32[]{:S(2)}) collective-permute-start(f32[32,512]{1,0:T(8,128)S(1)} %get-tuple-element.39), channel_id=1, source_target_pairs={{4,8},{8,4},{5,9},{9,5},{6,10},{10,6},{7,11},{11,7},{0,1},{1,0},{2... | collective-permute-start | bytes 196616 | tf_op jit(solution)/shard_map/ppermute | solution.py:311
  19.1 6.3 %collective-permute-start.12 = (f32[32,512]{1,0:T(8,128)S(1)}, f32[32,512]{1,0:T(8,128)S(1)}, u32[]{:S(2)}, u32[]{:S(2)}) collective-permute-start(f32[32,512]{1,0:T(8,128)S(1)} %get-tuple-element.40), channel_id=1, source_target_pairs={{0,4},{4,0},{1,5},{5,1},{2,6},{6,2},{3,7},{7,3},{8,12},{12,8},{9,1... | collective-permute-start | bytes 196616 | tf_op jit(solution)/shard_map/ppermute | solution.py:311
  22.8 4.3 %collective-permute-start.13 = (f32[32,512]{1,0:T(8,128)S(1)}, f32[32,512]{1,0:T(8,128)S(1)}, u32[]{:S(2)}, u32[]{:S(2)}) collective-permute-start(f32[32,512]{1,0:T(8,128)S(1)} %get-tuple-element.41), channel_id=1, source_target_pairs={{0,2},{2,0},{1,3},{3,1},{4,6},{6,4},{5,7},{7,5},{8,10},{10,8},{9,1... | collective-permute-start | bytes 196616 | tf_op jit(solution)/shard_map/ppermute | solution.py:311
  27.1 6.4 %collective-permute-start.16 = (f32[32,512]{1,0:T(8,128)S(1)}, f32[32,512]{1,0:T(8,128)S(1)}, u32[]{:S(2)}, u32[]{:S(2)}) collective-permute-start(f32[32,512]{1,0:T(8,128)S(1)} %add_add_fusion.rest_0_), channel_id=1, source_target_pairs={{0,12},{1,13},{2,14},{3,15},{4,8},{5,9},{6,10},{7,11},{8,4},{9,5},... | collective-permute-start | bytes 196616 | tf_op jit(solution)/shard_map/ppermute | solution.py:311
  29.0 6.5 %collective-permute-start.17 = (f32[32,512]{1,0:T(8,128)S(1)}, f32[32,512]{1,0:T(8,128)S(1)}, u32[]{:S(2)}, u32[]{:S(2)}) collective-permute-start(f32[32,512]{1,0:T(8,128)S(1)} %add_add_fusion.rest_0_), channel_id=1, source_target_pairs={{0,2},{1,3},{2,0},{3,1},{4,6},{5,7},{6,4},{7,5},{8,10},{9,11},{10,... | collective-permute-start | bytes 196616 | tf_op jit(solution)/shard_map/ppermute | solution.py:311
  30.3 5.3 %collective-permute-start.15 = (f32[32,512]{1,0:T(8,128)S(1)}, f32[32,512]{1,0:T(8,128)S(1)}, u32[]{:S(2)}, u32[]{:S(2)}) collective-permute-start(f32[32,512]{1,0:T(8,128)S(1)} %add_add_fusion.rest_0_), channel_id=1, source_target_pairs={{0,4},{1,5},{2,6},{3,7},{4,0},{5,1},{6,2},{7,3},{8,12},{9,13},{10,... | collective-permute-start | bytes 196616 | tf_op jit(solution)/shard_map/ppermute | solution.py:311
  30.3 6.2 %collective-permute-start.14 = (f32[32,512]{1,0:T(8,128)S(1)}, f32[32,512]{1,0:T(8,128)S(1)}, u32[]{:S(2)}, u32[]{:S(2)}) collective-permute-start(f32[32,512]{1,0:T(8,128)S(1)} %add_add_fusion.rest_0_), channel_id=1, source_target_pairs={{0,8},{1,9},{2,10},{3,11},{4,12},{5,13},{6,14},{7,15},{8,0},{9,1},... | collective-permute-start | bytes 196616 | tf_op jit(solution)/shard_map/ppermute | solution.py:311
  33.5 4.5 %collective-permute-start.20 = (f32[32,512]{1,0:T(8,128)S(1)}, f32[32,512]{1,0:T(8,128)S(1)}, u32[]{:S(2)}, u32[]{:S(2)}) collective-permute-start(f32[32,512]{1,0:T(8,128)S(1)} %collective-permute-done.16.rest_3_), channel_id=1, source_target_pairs={{0,2},{1,3},{2,0},{3,1},{4,6},{5,7},{6,4},{7,5},{8,10},{9,11},{10,... | collective-permute-start | bytes 196616 | tf_op jit(solution)/shard_map/ppermute | solution.py:311
  35.6 6.1 %collective-permute-start.21 = (f32[64,512]{1,0:T(8,128)S(1)}, f32[64,512]{1,0:T(8,128)S(1)}, u32[]{:S(2)}, u32[]{:S(2)}) collective-permute-start(f32[64,512]{1,0:T(8,128)S(1)} %pad_maximum_fusion), channel_id=1, source_target_pairs={{0,1},{1,0},{2,3},{3,2},{4,5},{5,4},{6,7},{7,6},{8,9},{9,8},{10,11... | collective-permute-start | bytes 393224 | tf_op jit(solution)/shard_map/ppermute | solution.py:311
  35.7 5.0 %collective-permute-start.19 = (f32[32,512]{1,0:T(8,128)S(1)}, f32[32,512]{1,0:T(8,128)S(1)}, u32[]{:S(2)}, u32[]{:S(2)}) collective-permute-start(f32[32,512]{1,0:T(8,128)S(1)} %collective-permute-done.15.rest_2_), channel_id=1, source_target_pairs={{0,2},{1,3},{2,0},{3,1},{4,6},{5,7},{6,4},{7,5},{8,10},{9,11},{10,... | collective-permute-start | bytes 196616 | tf_op jit(solution)/shard_map/ppermute | solution.py:311
  36.5 5.1 %collective-permute-start.18 = (f32[32,512]{1,0:T(8,128)S(1)}, f32[32,512]{1,0:T(8,128)S(1)}, u32[]{:S(2)}, u32[]{:S(2)}) collective-permute-start(f32[32,512]{1,0:T(8,128)S(1)} %collective-permute-done.14.rest_1_), channel_id=1, source_target_pairs={{0,2},{1,3},{2,0},{3,1},{4,6},{5,7},{6,4},{7,5},{8,10},{9,11},{10,... | collective-permute-start | bytes 196616 | tf_op jit(solution)/shard_map/ppermute | solution.py:311
  38.0 3.7 %collective-permute-start.24 = (f32[64,512]{1,0:T(8,128)S(1)}, f32[64,512]{1,0:T(8,128)S(1)}, u32[]{:S(2)}, u32[]{:S(2)}) collective-permute-start(f32[64,512]{1,0:T(8,128)S(1)} %pad_maximum_fusion.3), channel_id=1, source_target_pairs={{0,1},{1,0},{2,3},{3,2},{4,5},{5,4},{6,7},{7,6},{8,9},{9,8},{10,11... | collective-permute-start | bytes 393224 | tf_op jit(solution)/shard_map/ppermute | solution.py:311
  40.6 1.4 %collective-permute-start.23 = (f32[64,512]{1,0:T(8,128)S(1)}, f32[64,512]{1,0:T(8,128)S(1)}, u32[]{:S(2)}, u32[]{:S(2)}) collective-permute-start(f32[64,512]{1,0:T(8,128)S(1)} %pad_maximum_fusion.2), channel_id=1, source_target_pairs={{0,1},{1,0},{2,3},{3,2},{4,5},{5,4},{6,7},{7,6},{8,9},{9,8},{10,11... | collective-permute-start | bytes 393224 | tf_op jit(solution)/shard_map/ppermute | solution.py:311
  41.6 1.4 %collective-permute-start.22 = (f32[64,512]{1,0:T(8,128)S(1)}, f32[64,512]{1,0:T(8,128)S(1)}, u32[]{:S(2)}, u32[]{:S(2)}) collective-permute-start(f32[64,512]{1,0:T(8,128)S(1)} %pad_maximum_fusion.1), channel_id=1, source_target_pairs={{0,1},{1,0},{2,3},{3,2},{4,5},{5,4},{6,7},{7,6},{8,9},{9,8},{10,11... | collective-permute-start | bytes 393224 | tf_op jit(solution)/shard_map/ppermute | solution.py:311
  (4 other events, 46.1 us)

commit v5 on v4

--- a/solution.py
+++ b/solution.py
@@ -13,6 +13,8 @@
 WINDOW = 2 * CHIP_REACH + 1
 F32 = jnp.float32
 BF16 = jnp.bfloat16
+I16 = jnp.int16
+CODE_BITS = 14.0
 VMEM = pl.BlockSpec(memory_space=pltpu.VMEM)
 HBM = pl.BlockSpec(memory_space=pltpu.HBM)
 
@@ -109,8 +111,16 @@
                     slab[place] += product[
                         i * bores : (i + 1) * bores, j * tile : (j + 1) * tile
                     ]
+    largest = jnp.max(jnp.abs(slab[: WINDOW * per_chip]), axis=0)
+    largest = jnp.max(largest, axis=1, keepdims=True)
+    exponent = jnp.ceil(jnp.log2(jnp.maximum(largest, 1e-30)))
+    scale = jnp.broadcast_to(jnp.exp2(CODE_BITS - exponent), (bores, tile))
+    exponent = jnp.broadcast_to(exponent, (bores, tile)).astype(jnp.int32).astype(I16)
     for out, offset in zip(outs, (0,) + hop_offsets(chip)):
-        out[...] = slab[pl.ds((offset + CHIP_REACH) * per_chip, per_chip)]
+        for block in range(per_chip):
+            value = slab[(offset + CHIP_REACH) * per_chip + block]
+            out[block] = jnp.round(value * scale).astype(jnp.int32).astype(I16)
+        out[per_chip] = exponent
 
 
 def split(value):
@@ -120,8 +130,10 @@
 
 def block_of(piece, block, tile):
     if len(piece.shape) == 3:
-        return piece[block]
-    return piece[:, pl.ds(pl.multiple_of(block * tile, tile), tile)]
+        code = piece[block]
+    else:
+        code = piece[:, pl.ds(pl.multiple_of(block * tile, tile), tile)]
+    return code.astype(jnp.int32).astype(F32)
 
 
 def gram_kernel(lengths_ref, recorded_ref, *rest):
@@ -130,6 +142,7 @@
     outs = rest[2 * WINDOW + 2 : 3 * WINDOW + 2]
     high, low, heat, left, shifted = rest[3 * WINDOW + 2 :]
     blocks, bores, tile = other[0].shape
+    blocks -= 1
     me = lax.axis_index("rows")
     chip, core = me // 2, lax.rem(me, 2)
     seg_rows = heat_mine.shape[0]
@@ -137,8 +150,9 @@
     for pieces, side in ((mine, core), (other, 1 - core)):
         for piece, offset in zip(pieces, offsets):
             at = pl.multiple_of((offset + CHIP_REACH) * 2 * bores + side * bores, bores)
+            scale = jnp.exp2(block_of(piece, blocks, tile) - CODE_BITS)
             for block in range(blocks):
-                top, rest_of = split(block_of(piece, block, tile))
+                top, rest_of = split(block_of(piece, block, tile) * scale)
                 high[pl.ds(at, bores), block * tile : (block + 1) * tile] = top
                 low[pl.ds(at, bores), block * tile : (block + 1) * tile] = rest_of
     heat[pl.ds(pl.multiple_of(core * seg_rows, seg_rows), seg_rows)] = heat_mine[...]
@@ -190,14 +204,16 @@
     high, low = rest[2 * WINDOW : 2 * WINDOW + 2]
     (rows_of,) = rest[2 * WINDOW + 2 :]
     blocks, bores, tile = other[0].shape
+    blocks -= 1
     own_blocks = blocks // 2
     me = lax.axis_index("rows")
     chip, core = me // 2, lax.rem(me, 2)
     for pieces, side in ((mine, core), (other, 1 - core)):
         for piece, offset in zip(pieces, (0,) + hop_offsets(chip)):
             at = pl.multiple_of((offset + CHIP_REACH) * 2 * bores + side * bores, bores)
+            scale = jnp.exp2(block_of(piece, blocks, tile) - CODE_BITS)
             for block in range(own_blocks):
-                rows_of[block, pl.ds(at, bores)] = block_of(
+                rows_of[block, pl.ds(at, bores)] = scale * block_of(
                     piece, core * own_blocks + block, tile
                 )
     for block in range(own_blocks):
@@ -313,7 +329,7 @@
     def swap(value, bit):
         return send(value, [(rank, rank ^ bit) for rank in range(ranks)])
 
-    piece = jax.ShapeDtypeStruct((per_chip, bores, tile), F32)
+    piece = jax.ShapeDtypeStruct((per_chip + 1, bores, tile), I16)
     sent = pl.pallas_call(
         compress_kernel,
         out_shape=(piece,) * WINDOW,
@@ -335,7 +351,7 @@
     mine[1], heat_late, own = lax.optimization_barrier((mine[1], heat_start, mine[0]))
     heat_low = heat_late.astype(BF16)
     heat_other = swap(heat_low, 1)
-    own = own.transpose(1, 0, 2).reshape(bores, per_chip * tile)
+    own = own.transpose(1, 0, 2).reshape(bores, (per_chip + 1) * tile)
     mine[2], own = lax.optimization_barrier((mine[2], own))
     other = [swap(value, 1) for value in mine]
     mine[0] = own

time: 45.7 us -> 44.2 us (0.967)
  starting transfers between devices: 25.3 us -> 24.4 us
  waiting for transfers between devices: 10.4 us -> 9.6 us
    ppermute x25, waiting for transfers between devices: 10.4 us -> 9.6 us  [send(): return lax.ppermute(value, 'rows', pairs)]
    ppermute x25, starting transfers between devices: 25.3 us -> 24.4 us  [send(): return lax.ppermute(value, 'rows', pairs)]
  transfers between devices with their start and end apart: 25 -> 25, of which waited for: 13 -> 11; matrix products, arithmetic and copies ran while one was open for 2% -> 2% of each run, Pallas kernels for 1% -> 1%
where the time goes in v5:
time: 44.2 us; the launch traced here: 44 us
  starting transfers between devices  24.4 us (55%)
  waiting for transfers between devices  9.6 us (22%)
  Pallas kernels  8.18 us (19%)
  local copies, waits for them, and re-layouts  0.9 us (2%)
  between operations  0.81 us (2%)
    ppermute x25, starting transfers between devices, send(): return lax.ppermute(value, 'rows', pairs)  24.4 us
    ppermute x25, waiting for transfers between devices, send(): return lax.ppermute(value, 'rows', pairs)  9.6 us
    pallas_call x1, Pallas kernels, on_device(): pl.pallas_call(compress_kernel, out_shape=(piece,) * WINDOW, in_specs=[HB...  3.89 us
    pallas_call x1, Pallas kernels, on_device(): pl.pallas_call(functools.partial(descend_kernel, ranks, places), out_shap...  2.58 us
    pallas_call x1, Pallas kernels, on_device(): pl.pallas_call(gram_kernel, out_shape=(packed,) * WINDOW, in_specs=[VMEM]...  1.35 us
    reshape x1, local copies, waits for them, and re-layouts, on_device(): own = own.transpose(1, 0, 2).reshape(bores, (per_chip + 1) * tile)  0.89 us
  transfers between devices with their start and end apart: 25, of which 11 were waited for; matrix products, arithmetic and copies ran while one was open for 2% of the time, Pallas kernels for 1%

profile of v5, /device:TPU:0, one launch (start us, length us, event | category | flops | bytes accessed | tf_op | source)
XLA Modules:
  0.0 44.0 jit_solution(1799137011102827774)
XLA Ops:
  0.7 3.9 %compress.1 = (s16[9,32,128]{2,1,0:T(8,128)(2,1)}, s16[9,32,128]{2,1,0:T(8,128)(2,1)}, s16[9,32,128]{2,1,0:T(8,128)(2,1)}, s16[9,32,128]{2,1,0:T(8,128)(2,1)}, s16[9,32,128]{2,1,0:T(8,128)(2,1)}) custom-call(s32[4,30]{1,0:T(4,128)} %cols_hbm.1, s32[4]{0:T(128)} %count_hbm.1, s32[1,32]{1,0:T(1,128)} %lengths_ref.1, bf16[4,30,128,128]{3,2,1,0:T(8,128)(2,1)} %tiles_hbm.1), custom_call_target="tpu_custom_call" | custom-call | tf_op jit(solution)/shard_map/compress/pallas_call | solution.py:333
  4.6 0.5 %collective-permute-start.1 = (s16[9,32,128]{2,1,0:T(8,128)(2,1)}, s16[9,32,128]{2,1,0:T(8,128)(2,1)S(1)}, u32[]{:S(2)}, u32[]{:S(2)}) collective-permute-start(s16[9,32,128]{2,1,0:T(8,128)(2,1)} %get-tuple-element.23), channel_id=1, source_target_pairs={{2,4},{4,2},{3,5},{5,3},{6,8},{8,6},{7,9},{9,7},{10,12},{12,10},{1... | collective-permute-start | bytes 221192 | tf_op jit(solution)/shard_map/ppermute | solution.py:327
  5.1 5.4 %collective-permute-start.2 = (s16[9,32,128]{2,1,0:T(8,128)(2,1)}, s16[9,32,128]{2,1,0:T(8,128)(2,1)S(1)}, u32[]{:S(2)}, u32[]{:S(2)}) collective-permute-start(s16[9,32,128]{2,1,0:T(8,128)(2,1)} %get-tuple-element.29), channel_id=1, source_target_pairs={{0,4},{4,0},{1,5},{5,1},{2,6},{6,2},{3,7},{7,3},{8,12},{12,8},{9,1... | collective-permute-start | bytes 221192 | tf_op jit(solution)/shard_map/ppermute | solution.py:327
  10.6 1.6 %collective-permute-start.3 = (s16[9,32,128]{2,1,0:T(8,128)(2,1)}, s16[9,32,128]{2,1,0:T(8,128)(2,1)S(1)}, u32[]{:S(2)}, u32[]{:S(2)}) collective-permute-start(s16[9,32,128]{2,1,0:T(8,128)(2,1)} %get-tuple-element.30), channel_id=1, source_target_pairs={{0,2},{2,0},{1,3},{3,1},{4,6},{6,4},{5,7},{7,5},{8,10},{10,8},{9,1... | collective-permute-start | bytes 221192 | tf_op jit(solution)/shard_map/ppermute | solution.py:327
  12.2 0.6 %collective-permute-start.9 = (bf16[512,128]{1,0:T(8,128)(2,1)S(1)}, bf16[512,128]{1,0:T(8,128)(2,1)S(1)}, u32[]{:S(2)}, u32[]{:S(2)}) collective-permute-start(bf16[512,128]{1,0:T(8,128)(2,1)S(1)} %convert_element_type.3.rest_10_), channel_id=1, source_target_pairs={{0,1},{1,0},{2,3},{3,2},{4,5},{5,4},{6,7},{7,6},{8,9},{9,8},{10,11... | collective-permute-start | bytes 393224 | tf_op jit(solution)/shard_map/ppermute | solution.py:327
  12.8 0.9 %copy_bitcast_fusion.rest_0_ = s16[32,1152]{1,0:T(8,128)(2,1)S(1)} fusion(s16[9,32,128]{2,1,0:T(8,128)(2,1)} %get-tuple-element.25), kind=kLoop, calls=%fused_computation.4 | loop fusion | bytes 147456 | tf_op jit(solution)/shard_map/reshape | solution.py:354
  14.2 0.9 %collective-permute-done.3.rest_4_ = s16[9,32,128]{2,1,0:T(8,128)(2,1)S(1)} collective-permute-done((s16[9,32,128]{2,1,0:T(8,128)(2,1)}, s16[9,32,128]{2,1,0:T(8,128)(2,1)S(1)}, u32[]{:S(2)}, u32[]{:S(2)}) %collective-permute-start.3) | collective-permute-done | bytes 73760 | tf_op jit(solution)/shard_map/ppermute | solution.py:327
  15.1 0.5 %collective-permute-start.8 = (s16[9,32,128]{2,1,0:T(8,128)(2,1)S(1)}, s16[9,32,128]{2,1,0:T(8,128)(2,1)S(1)}, u32[]{:S(2)}, u32[]{:S(2)}) collective-permute-start(s16[9,32,128]{2,1,0:T(8,128)(2,1)S(1)} %collective-permute-done.3.rest_4_), channel_id=1, source_target_pairs={{0,1},{1,0},{2,3},{3,2},{4,5},{5,4},{6,7},{7,6},{8,9},{9,8},{10,11... | collective-permute-start | bytes 221192 | tf_op jit(solution)/shard_map/ppermute | solution.py:327
  15.7 0.7 %collective-permute-done.7.rest_8_ = s16[9,32,128]{2,1,0:T(8,128)(2,1)S(1)} collective-permute-done((s16[9,32,128]{2,1,0:T(8,128)(2,1)S(1)}, s16[9,32,128]{2,1,0:T(8,128)(2,1)S(1)}, u32[]{:S(2)}, u32[]{:S(2)}) %collective-permute-start.7) | collective-permute-done | bytes 73760 | tf_op jit(solution)/shard_map/ppermute | solution.py:327
  16.6 1.4 %gram.1 = (f32[32,512]{1,0:T(8,128)S(1)}, f32[32,512]{1,0:T(8,128)S(1)}, f32[32,512]{1,0:T(8,128)S(1)}, f32[32,512]{1,0:T(8,128)S(1)}, f32[32,512]{1,0:T(8,128)S(1)}) custom-call(s32[1,32]{1,0:T(1,128)S(1)} %copy-done.2, f32[32,128]{1,0:T(8,128)S(1)} %copy-done.1, s16[32,1152]{1,0:T(8,128)(2,1)S(1)} %copy_bitcast_fusion.rest_0_, ...), custom_call_target="tpu_custom_call" | custom-call | tf_op jit(solution)/shard_map/gram/pallas_call | solution.py:359
  18.5 2.9 %collective-permute-start.12 = (f32[32,512]{1,0:T(8,128)S(1)}, f32[32,512]{1,0:T(8,128)S(1)}, u32[]{:S(2)}, u32[]{:S(2)}) collective-permute-start(f32[32,512]{1,0:T(8,128)S(1)} %get-tuple-element.40), channel_id=1, source_target_pairs={{0,4},{4,0},{1,5},{5,1},{2,6},{6,2},{3,7},{7,3},{8,12},{12,8},{9,1... | collective-permute-start | bytes 196616 | tf_op jit(solution)/shard_map/ppermute | solution.py:327
  21.4 1.6 %collective-permute-start.13 = (f32[32,512]{1,0:T(8,128)S(1)}, f32[32,512]{1,0:T(8,128)S(1)}, u32[]{:S(2)}, u32[]{:S(2)}) collective-permute-start(f32[32,512]{1,0:T(8,128)S(1)} %get-tuple-element.41), channel_id=1, source_target_pairs={{0,2},{2,0},{1,3},{3,1},{4,6},{6,4},{5,7},{7,5},{8,10},{10,8},{9,1... | collective-permute-start | bytes 196616 | tf_op jit(solution)/shard_map/ppermute | solution.py:327
  23.5 1.3 %collective-permute-done.12 = f32[32,512]{1,0:T(8,128)S(1)} collective-permute-done((f32[32,512]{1,0:T(8,128)S(1)}, f32[32,512]{1,0:T(8,128)S(1)}, u32[]{:S(2)}, u32[]{:S(2)}) %collective-permute-start.12) | collective-permute-done | bytes 65568 | tf_op jit(solution)/shard_map/ppermute | solution.py:327
  24.8 0.9 %collective-permute-done.13 = f32[32,512]{1,0:T(8,128)S(1)} collective-permute-done((f32[32,512]{1,0:T(8,128)S(1)}, f32[32,512]{1,0:T(8,128)S(1)}, u32[]{:S(2)}, u32[]{:S(2)}) %collective-permute-start.13) | collective-permute-done | bytes 65568 | tf_op jit(solution)/shard_map/ppermute | solution.py:327
  25.7 2.6 %collective-permute-start.16 = (f32[32,512]{1,0:T(8,128)S(1)}, f32[32,512]{1,0:T(8,128)S(1)}, u32[]{:S(2)}, u32[]{:S(2)}) collective-permute-start(f32[32,512]{1,0:T(8,128)S(1)} %add_add_fusion.rest_0_), channel_id=1, source_target_pairs={{0,12},{1,13},{2,14},{3,15},{4,8},{5,9},{6,10},{7,11},{8,4},{9,5},... | collective-permute-start | bytes 196616 | tf_op jit(solution)/shard_map/ppermute | solution.py:327
  28.7 3.1 %collective-permute-start.14 = (f32[32,512]{1,0:T(8,128)S(1)}, f32[32,512]{1,0:T(8,128)S(1)}, u32[]{:S(2)}, u32[]{:S(2)}) collective-permute-start(f32[32,512]{1,0:T(8,128)S(1)} %add_add_fusion.rest_0_), channel_id=1, source_target_pairs={{0,8},{1,9},{2,10},{3,11},{4,12},{5,13},{6,14},{7,15},{8,0},{9,1},... | collective-permute-start | bytes 196616 | tf_op jit(solution)/shard_map/ppermute | solution.py:327
  31.8 0.6 %collective-permute-done.16.rest_3_ = f32[32,512]{1,0:T(8,128)S(1)} collective-permute-done((f32[32,512]{1,0:T(8,128)S(1)}, f32[32,512]{1,0:T(8,128)S(1)}, u32[]{:S(2)}, u32[]{:S(2)}) %collective-permute-start.16) | collective-permute-done | bytes 65568 | tf_op jit(solution)/shard_map/ppermute | solution.py:327
  32.4 1.6 %collective-permute-start.20 = (f32[32,512]{1,0:T(8,128)S(1)}, f32[32,512]{1,0:T(8,128)S(1)}, u32[]{:S(2)}, u32[]{:S(2)}) collective-permute-start(f32[32,512]{1,0:T(8,128)S(1)} %collective-permute-done.16.rest_3_), channel_id=1, source_target_pairs={{0,2},{1,3},{2,0},{3,1},{4,6},{5,7},{6,4},{7,5},{8,10},{9,11},{10,... | collective-permute-start | bytes 196616 | tf_op jit(solution)/shard_map/ppermute | solution.py:327
  34.1 0.6 %collective-permute-start.19 = (f32[32,512]{1,0:T(8,128)S(1)}, f32[32,512]{1,0:T(8,128)S(1)}, u32[]{:S(2)}, u32[]{:S(2)}) collective-permute-start(f32[32,512]{1,0:T(8,128)S(1)} %collective-permute-done.15.rest_2_), channel_id=1, source_target_pairs={{0,2},{1,3},{2,0},{3,1},{4,6},{5,7},{6,4},{7,5},{8,10},{9,11},{10,... | collective-permute-start | bytes 196616 | tf_op jit(solution)/shard_map/ppermute | solution.py:327
  34.7 1.5 %collective-permute-start.18 = (f32[32,512]{1,0:T(8,128)S(1)}, f32[32,512]{1,0:T(8,128)S(1)}, u32[]{:S(2)}, u32[]{:S(2)}) collective-permute-start(f32[32,512]{1,0:T(8,128)S(1)} %collective-permute-done.14.rest_1_), channel_id=1, source_target_pairs={{0,2},{1,3},{2,0},{3,1},{4,6},{5,7},{6,4},{7,5},{8,10},{9,11},{10,... | collective-permute-start | bytes 196616 | tf_op jit(solution)/shard_map/ppermute | solution.py:327
  36.8 2.3 %collective-permute-done.19.rest_6_ = f32[32,512]{1,0:T(8,128)S(1)} collective-permute-done((f32[32,512]{1,0:T(8,128)S(1)}, f32[32,512]{1,0:T(8,128)S(1)}, u32[]{:S(2)}, u32[]{:S(2)}) %collective-permute-start.19) | collective-permute-done | bytes 65568 | tf_op jit(solution)/shard_map/ppermute | solution.py:327
  39.2 0.9 %collective-permute-done.18.rest_5_ = f32[32,512]{1,0:T(8,128)S(1)} collective-permute-done((f32[32,512]{1,0:T(8,128)S(1)}, f32[32,512]{1,0:T(8,128)S(1)}, u32[]{:S(2)}, u32[]{:S(2)}) %collective-permute-start.18) | collective-permute-done | bytes 65568 | tf_op jit(solution)/shard_map/ppermute | solution.py:327
  40.5 0.9 %collective-permute-done.22.rest_9_ = f32[64,512]{1,0:T(8,128)S(1)} collective-permute-done((f32[64,512]{1,0:T(8,128)S(1)}, f32[64,512]{1,0:T(8,128)S(1)}, u32[]{:S(2)}, u32[]{:S(2)}) %collective-permute-start.22) | collective-permute-done | bytes 131104 | tf_op jit(solution)/shard_map/ppermute | solution.py:327
  41.4 2.6 %descend.1 = (f32[512,128]{1,0:T(8,128)}, f32[32,128]{1,0:T(8,128)}) custom-call(f32[512,128]{1,0:T(8,128)S(1)} %copy-done, bf16[512,320]{1,0:T(8,128)(2,1)S(1)} %get-tuple-element.35.high_ref, bf16[512,320]{1,0:T(8,128)(2,1)S(1)} %get-tuple-element.36.low_ref, f32[32,512]{1,0:T(8,128)S(1)} %add_add_fusion.rest_0_, ...), custom_call_target="tpu_custom_call" | custom-call | tf_op jit(solution)/shard_map/descend/pallas_call | solution.py:407
  (43 shorter events, 3.4 us)
Async XLA Ops:
  4.6 7.6 %collective-permute-start.1 = (s16[9,32,128]{2,1,0:T(8,128)(2,1)}, s16[9,32,128]{2,1,0:T(8,128)(2,1)S(1)}, u32[]{:S(2)}, u32[]{:S(2)}) collective-permute-start(s16[9,32,128]{2,1,0:T(8,128)(2,1)} %get-tuple-element.23), channel_id=1, source_target_pairs={{2,4},{4,2},{3,5},{5,3},{6,8},{8,6},{7,9},{9,7},{10,12},{12,10},{1... | collective-permute-start | bytes 221192 | tf_op jit(solution)/shard_map/ppermute | solution.py:327
  5.1 8.6 %collective-permute-start = (s16[9,32,128]{2,1,0:T(8,128)(2,1)}, s16[9,32,128]{2,1,0:T(8,128)(2,1)S(1)}, u32[]{:S(2)}, u32[]{:S(2)}) collective-permute-start(s16[9,32,128]{2,1,0:T(8,128)(2,1)} %get-tuple-element.22), channel_id=1, source_target_pairs={{4,8},{8,4},{5,9},{9,5},{6,10},{10,6},{7,11},{11,7},{0,1},{1,0},{2... | collective-permute-start | bytes 221192 | tf_op jit(solution)/shard_map/ppermute | solution.py:327
  5.1 8.6 %collective-permute-start.2 = (s16[9,32,128]{2,1,0:T(8,128)(2,1)}, s16[9,32,128]{2,1,0:T(8,128)(2,1)S(1)}, u32[]{:S(2)}, u32[]{:S(2)}) collective-permute-start(s16[9,32,128]{2,1,0:T(8,128)(2,1)} %get-tuple-element.29), channel_id=1, source_target_pairs={{0,4},{4,0},{1,5},{5,1},{2,6},{6,2},{3,7},{7,3},{8,12},{12,8},{9,1... | collective-permute-start | bytes 221192 | tf_op jit(solution)/shard_map/ppermute | solution.py:327
  10.6 4.6 %collective-permute-start.3 = (s16[9,32,128]{2,1,0:T(8,128)(2,1)}, s16[9,32,128]{2,1,0:T(8,128)(2,1)S(1)}, u32[]{:S(2)}, u32[]{:S(2)}) collective-permute-start(s16[9,32,128]{2,1,0:T(8,128)(2,1)} %get-tuple-element.30), channel_id=1, source_target_pairs={{0,2},{2,0},{1,3},{3,1},{4,6},{6,4},{5,7},{7,5},{8,10},{10,8},{9,1... | collective-permute-start | bytes 221192 | tf_op jit(solution)/shard_map/ppermute | solution.py:327
  12.2 3.0 %collective-permute-start.4 = (s16[9,32,128]{2,1,0:T(8,128)(2,1)}, s16[9,32,128]{2,1,0:T(8,128)(2,1)S(1)}, u32[]{:S(2)}, u32[]{:S(2)}) collective-permute-start(s16[9,32,128]{2,1,0:T(8,128)(2,1)} %get-tuple-element.25), channel_id=1, source_target_pairs={{0,1},{1,0},{2,3},{3,2},{4,5},{5,4},{6,7},{7,6},{8,9},{9,8},{10,11... | collective-permute-start | bytes 221192 | tf_op jit(solution)/shard_map/ppermute | solution.py:327
  12.2 4.4 %collective-permute-start.9 = (bf16[512,128]{1,0:T(8,128)(2,1)S(1)}, bf16[512,128]{1,0:T(8,128)(2,1)S(1)}, u32[]{:S(2)}, u32[]{:S(2)}) collective-permute-start(bf16[512,128]{1,0:T(8,128)(2,1)S(1)} %convert_element_type.3.rest_10_), channel_id=1, source_target_pairs={{0,1},{1,0},{2,3},{3,2},{4,5},{5,4},{6,7},{7,6},{8,9},{9,8},{10,11... | collective-permute-start | bytes 393224 | tf_op jit(solution)/shard_map/ppermute | solution.py:327
  13.7 2.0 %collective-permute-start.6 = (s16[9,32,128]{2,1,0:T(8,128)(2,1)S(1)}, s16[9,32,128]{2,1,0:T(8,128)(2,1)S(1)}, u32[]{:S(2)}, u32[]{:S(2)}) collective-permute-start(s16[9,32,128]{2,1,0:T(8,128)(2,1)S(1)} %collective-permute-done.rest_2_), channel_id=1, source_target_pairs={{0,1},{1,0},{2,3},{3,2},{4,5},{5,4},{6,7},{7,6},{8,9},{9,8},{10,11... | collective-permute-start | bytes 221192 | tf_op jit(solution)/shard_map/ppermute | solution.py:327
  13.7 1.9 %collective-permute-start.5 = (s16[9,32,128]{2,1,0:T(8,128)(2,1)S(1)}, s16[9,32,128]{2,1,0:T(8,128)(2,1)S(1)}, u32[]{:S(2)}, u32[]{:S(2)}) collective-permute-start(s16[9,32,128]{2,1,0:T(8,128)(2,1)S(1)} %collective-permute-done.1.rest_1_), channel_id=1, source_target_pairs={{0,1},{1,0},{2,3},{3,2},{4,5},{5,4},{6,7},{7,6},{8,9},{9,8},{10,11... | collective-permute-start | bytes 221192 | tf_op jit(solution)/shard_map/ppermute | solution.py:327
  15.1 1.4 %collective-permute-start.8 = (s16[9,32,128]{2,1,0:T(8,128)(2,1)S(1)}, s16[9,32,128]{2,1,0:T(8,128)(2,1)S(1)}, u32[]{:S(2)}, u32[]{:S(2)}) collective-permute-start(s16[9,32,128]{2,1,0:T(8,128)(2,1)S(1)} %collective-permute-done.3.rest_4_), channel_id=1, source_target_pairs={{0,1},{1,0},{2,3},{3,2},{4,5},{5,4},{6,7},{7,6},{8,9},{9,8},{10,11... | collective-permute-start | bytes 221192 | tf_op jit(solution)/shard_map/ppermute | solution.py:327
  17.9 5.5 %collective-permute-start.10 = (f32[32,512]{1,0:T(8,128)S(1)}, f32[32,512]{1,0:T(8,128)S(1)}, u32[]{:S(2)}, u32[]{:S(2)}) collective-permute-start(f32[32,512]{1,0:T(8,128)S(1)} %get-tuple-element.38), channel_id=1, source_target_pairs={{2,4},{4,2},{3,5},{5,3},{6,8},{8,6},{7,9},{9,7},{10,12},{12,10},{1... | collective-permute-start | bytes 196616 | tf_op jit(solution)/shard_map/ppermute | solution.py:327
  18.4 5.1 %collective-permute-start.11 = (f32[32,512]{1,0:T(8,128)S(1)}, f32[32,512]{1,0:T(8,128)S(1)}, u32[]{:S(2)}, u32[]{:S(2)}) collective-permute-start(f32[32,512]{1,0:T(8,128)S(1)} %get-tuple-element.39), channel_id=1, source_target_pairs={{4,8},{8,4},{5,9},{9,5},{6,10},{10,6},{7,11},{11,7},{0,1},{1,0},{2... | collective-permute-start | bytes 196616 | tf_op jit(solution)/shard_map/ppermute | solution.py:327
  18.5 6.3 %collective-permute-start.12 = (f32[32,512]{1,0:T(8,128)S(1)}, f32[32,512]{1,0:T(8,128)S(1)}, u32[]{:S(2)}, u32[]{:S(2)}) collective-permute-start(f32[32,512]{1,0:T(8,128)S(1)} %get-tuple-element.40), channel_id=1, source_target_pairs={{0,4},{4,0},{1,5},{5,1},{2,6},{6,2},{3,7},{7,3},{8,12},{12,8},{9,1... | collective-permute-start | bytes 196616 | tf_op jit(solution)/shard_map/ppermute | solution.py:327
  21.4 4.3 %collective-permute-start.13 = (f32[32,512]{1,0:T(8,128)S(1)}, f32[32,512]{1,0:T(8,128)S(1)}, u32[]{:S(2)}, u32[]{:S(2)}) collective-permute-start(f32[32,512]{1,0:T(8,128)S(1)} %get-tuple-element.41), channel_id=1, source_target_pairs={{0,2},{2,0},{1,3},{3,1},{4,6},{6,4},{5,7},{7,5},{8,10},{10,8},{9,1... | collective-permute-start | bytes 196616 | tf_op jit(solution)/shard_map/ppermute | solution.py:327
  25.7 6.7 %collective-permute-start.16 = (f32[32,512]{1,0:T(8,128)S(1)}, f32[32,512]{1,0:T(8,128)S(1)}, u32[]{:S(2)}, u32[]{:S(2)}) collective-permute-start(f32[32,512]{1,0:T(8,128)S(1)} %add_add_fusion.rest_0_), channel_id=1, source_target_pairs={{0,12},{1,13},{2,14},{3,15},{4,8},{5,9},{6,10},{7,11},{8,4},{9,5},... | collective-permute-start | bytes 196616 | tf_op jit(solution)/shard_map/ppermute | solution.py:327
  28.4 5.7 %collective-permute-start.17 = (f32[32,512]{1,0:T(8,128)S(1)}, f32[32,512]{1,0:T(8,128)S(1)}, u32[]{:S(2)}, u32[]{:S(2)}) collective-permute-start(f32[32,512]{1,0:T(8,128)S(1)} %add_add_fusion.rest_0_), channel_id=1, source_target_pairs={{0,2},{1,3},{2,0},{3,1},{4,6},{5,7},{6,4},{7,5},{8,10},{9,11},{10,... | collective-permute-start | bytes 196616 | tf_op jit(solution)/shard_map/ppermute | solution.py:327
  28.7 5.4 %collective-permute-start.15 = (f32[32,512]{1,0:T(8,128)S(1)}, f32[32,512]{1,0:T(8,128)S(1)}, u32[]{:S(2)}, u32[]{:S(2)}) collective-permute-start(f32[32,512]{1,0:T(8,128)S(1)} %add_add_fusion.rest_0_), channel_id=1, source_target_pairs={{0,4},{1,5},{2,6},{3,7},{4,0},{5,1},{6,2},{7,3},{8,12},{9,13},{10,... | collective-permute-start | bytes 196616 | tf_op jit(solution)/shard_map/ppermute | solution.py:327
  28.7 6.0 %collective-permute-start.14 = (f32[32,512]{1,0:T(8,128)S(1)}, f32[32,512]{1,0:T(8,128)S(1)}, u32[]{:S(2)}, u32[]{:S(2)}) collective-permute-start(f32[32,512]{1,0:T(8,128)S(1)} %add_add_fusion.rest_0_), channel_id=1, source_target_pairs={{0,8},{1,9},{2,10},{3,11},{4,12},{5,13},{6,14},{7,15},{8,0},{9,1},... | collective-permute-start | bytes 196616 | tf_op jit(solution)/shard_map/ppermute | solution.py:327
  32.4 4.3 %collective-permute-start.20 = (f32[32,512]{1,0:T(8,128)S(1)}, f32[32,512]{1,0:T(8,128)S(1)}, u32[]{:S(2)}, u32[]{:S(2)}) collective-permute-start(f32[32,512]{1,0:T(8,128)S(1)} %collective-permute-done.16.rest_3_), channel_id=1, source_target_pairs={{0,2},{1,3},{2,0},{3,1},{4,6},{5,7},{6,4},{7,5},{8,10},{9,11},{10,... | collective-permute-start | bytes 196616 | tf_op jit(solution)/shard_map/ppermute | solution.py:327
  34.0 6.1 %collective-permute-start.21 = (f32[64,512]{1,0:T(8,128)S(1)}, f32[64,512]{1,0:T(8,128)S(1)}, u32[]{:S(2)}, u32[]{:S(2)}) collective-permute-start(f32[64,512]{1,0:T(8,128)S(1)} %pad_maximum_fusion), channel_id=1, source_target_pairs={{0,1},{1,0},{2,3},{3,2},{4,5},{5,4},{6,7},{7,6},{8,9},{9,8},{10,11... | collective-permute-start | bytes 393224 | tf_op jit(solution)/shard_map/ppermute | solution.py:327
  34.1 5.0 %collective-permute-start.19 = (f32[32,512]{1,0:T(8,128)S(1)}, f32[32,512]{1,0:T(8,128)S(1)}, u32[]{:S(2)}, u32[]{:S(2)}) collective-permute-start(f32[32,512]{1,0:T(8,128)S(1)} %collective-permute-done.15.rest_2_), channel_id=1, source_target_pairs={{0,2},{1,3},{2,0},{3,1},{4,6},{5,7},{6,4},{7,5},{8,10},{9,11},{10,... | collective-permute-start | bytes 196616 | tf_op jit(solution)/shard_map/ppermute | solution.py:327
  34.7 5.3 %collective-permute-start.18 = (f32[32,512]{1,0:T(8,128)S(1)}, f32[32,512]{1,0:T(8,128)S(1)}, u32[]{:S(2)}, u32[]{:S(2)}) collective-permute-start(f32[32,512]{1,0:T(8,128)S(1)} %collective-permute-done.14.rest_1_), channel_id=1, source_target_pairs={{0,2},{1,3},{2,0},{3,1},{4,6},{5,7},{6,4},{7,5},{8,10},{9,11},{10,... | collective-permute-start | bytes 196616 | tf_op jit(solution)/shard_map/ppermute | solution.py:327
  36.7 3.4 %collective-permute-start.24 = (f32[64,512]{1,0:T(8,128)S(1)}, f32[64,512]{1,0:T(8,128)S(1)}, u32[]{:S(2)}, u32[]{:S(2)}) collective-permute-start(f32[64,512]{1,0:T(8,128)S(1)} %pad_maximum_fusion.3), channel_id=1, source_target_pairs={{0,1},{1,0},{2,3},{3,2},{4,5},{5,4},{6,7},{7,6},{8,9},{9,8},{10,11... | collective-permute-start | bytes 393224 | tf_op jit(solution)/shard_map/ppermute | solution.py:327
  39.1 1.4 %collective-permute-start.23 = (f32[64,512]{1,0:T(8,128)S(1)}, f32[64,512]{1,0:T(8,128)S(1)}, u32[]{:S(2)}, u32[]{:S(2)}) collective-permute-start(f32[64,512]{1,0:T(8,128)S(1)} %pad_maximum_fusion.2), channel_id=1, source_target_pairs={{0,1},{1,0},{2,3},{3,2},{4,5},{5,4},{6,7},{7,6},{8,9},{9,8},{10,11... | collective-permute-start | bytes 393224 | tf_op jit(solution)/shard_map/ppermute | solution.py:327
  40.0 1.4 %collective-permute-start.22 = (f32[64,512]{1,0:T(8,128)S(1)}, f32[64,512]{1,0:T(8,128)S(1)}, u32[]{:S(2)}, u32[]{:S(2)}) collective-permute-start(f32[64,512]{1,0:T(8,128)S(1)} %pad_maximum_fusion.1), channel_id=1, source_target_pairs={{0,1},{1,0},{2,3},{3,2},{4,5},{5,4},{6,7},{7,6},{8,9},{9,8},{10,11... | collective-permute-start | bytes 393224 | tf_op jit(solution)/shard_map/ppermute | solution.py:327
  (4 other events, 44.7 us)

commit v6 on v5

--- a/solution.py
+++ b/solution.py
@@ -14,7 +14,8 @@
 F32 = jnp.float32
 BF16 = jnp.bfloat16
 I16 = jnp.int16
-CODE_BITS = 14.0
+CODE_BITS = 15.0
+CODE_MOST = 32767.0
 VMEM = pl.BlockSpec(memory_space=pltpu.VMEM)
 HBM = pl.BlockSpec(memory_space=pltpu.HBM)
 
@@ -69,7 +70,7 @@
     copies = []
     for row in range(block_rows):
         copy = pltpu.make_async_copy(tiles_hbm.at[row], tiles.at[row], sems.at[row])
-        copy.start()
+        copy.start(priority=row // 2)
         copies.append(copy)
     slab[...] = jnp.zeros_like(slab)
     chip = lax.axis_index("rows") // 2
@@ -119,7 +120,8 @@
     for out, offset in zip(outs, (0,) + hop_offsets(chip)):
         for block in range(per_chip):
             value = slab[(offset + CHIP_REACH) * per_chip + block]
-            out[block] = jnp.round(value * scale).astype(jnp.int32).astype(I16)
+            code = jnp.minimum(jnp.round(value * scale), CODE_MOST)
+            out[block] = code.astype(jnp.int32).astype(I16)
         out[per_chip] = exponent
 
 

time: 44.2 us -> 43.9 us (level)
  no operation moved by 1% of the time
where the time goes in v6:
time: 43.9 us; the launch traced here: 43.6 us
  starting transfers between devices  24.1 us (55%)
  waiting for transfers between devices  9.84 us (22%)
  Pallas kernels  7.95 us (18%)
  local copies, waits for them, and re-layouts  0.9 us (2%)
  between operations  0.81 us (2%)
    ppermute x25, starting transfers between devices, send(): return lax.ppermute(value, 'rows', pairs)  24.1 us
    ppermute x25, waiting for transfers between devices, send(): return lax.ppermute(value, 'rows', pairs)  9.84 us
    pallas_call x1, Pallas kernels, on_device(): pl.pallas_call(compress_kernel, out_shape=(piece,) * WINDOW, in_specs=[HB...  3.66 us
    pallas_call x1, Pallas kernels, on_device(): pl.pallas_call(functools.partial(descend_kernel, ranks, places), out_shap...  2.57 us
    pallas_call x1, Pallas kernels, on_device(): pl.pallas_call(gram_kernel, out_shape=(packed,) * WINDOW, in_specs=[VMEM]...  1.35 us
    reshape x1, local copies, waits for them, and re-layouts, on_device(): own = own.transpose(1, 0, 2).reshape(bores, (per_chip + 1) * tile)  0.89 us
  transfers between devices with their start and end apart: 25, of which 11 were waited for; matrix products, arithmetic and copies ran while one was open for 2% of the time, Pallas kernels for 1%

profile of v6, /device:TPU:0, one launch (start us, length us, event | category | flops | bytes accessed | tf_op | source)
XLA Modules:
  0.0 43.6 jit_solution(1807266299506267433)
XLA Ops:
  0.7 3.7 %compress.1 = (s16[9,32,128]{2,1,0:T(8,128)(2,1)}, s16[9,32,128]{2,1,0:T(8,128)(2,1)}, s16[9,32,128]{2,1,0:T(8,128)(2,1)}, s16[9,32,128]{2,1,0:T(8,128)(2,1)}, s16[9,32,128]{2,1,0:T(8,128)(2,1)}) custom-call(s32[4,30]{1,0:T(4,128)} %cols_hbm.1, s32[4]{0:T(128)} %count_hbm.1, s32[1,32]{1,0:T(1,128)} %lengths_ref.1, bf16[4,30,128,128]{3,2,1,0:T(8,128)(2,1)} %tiles_hbm.1), custom_call_target="tpu_custom_call" | custom-call | tf_op jit(solution)/shard_map/compress/pallas_call | solution.py:335
  4.9 5.4 %collective-permute-start.2 = (s16[9,32,128]{2,1,0:T(8,128)(2,1)}, s16[9,32,128]{2,1,0:T(8,128)(2,1)S(1)}, u32[]{:S(2)}, u32[]{:S(2)}) collective-permute-start(s16[9,32,128]{2,1,0:T(8,128)(2,1)} %get-tuple-element.29), channel_id=1, source_target_pairs={{0,4},{4,0},{1,5},{5,1},{2,6},{6,2},{3,7},{7,3},{8,12},{12,8},{9,1... | collective-permute-start | bytes 221192 | tf_op jit(solution)/shard_map/ppermute | solution.py:329
  10.3 1.7 %collective-permute-start.3 = (s16[9,32,128]{2,1,0:T(8,128)(2,1)}, s16[9,32,128]{2,1,0:T(8,128)(2,1)S(1)}, u32[]{:S(2)}, u32[]{:S(2)}) collective-permute-start(s16[9,32,128]{2,1,0:T(8,128)(2,1)} %get-tuple-element.30), channel_id=1, source_target_pairs={{0,2},{2,0},{1,3},{3,1},{4,6},{6,4},{5,7},{7,5},{8,10},{10,8},{9,1... | collective-permute-start | bytes 221192 | tf_op jit(solution)/shard_map/ppermute | solution.py:329
  12.1 0.6 %collective-permute-start.9 = (bf16[512,128]{1,0:T(8,128)(2,1)S(1)}, bf16[512,128]{1,0:T(8,128)(2,1)S(1)}, u32[]{:S(2)}, u32[]{:S(2)}) collective-permute-start(bf16[512,128]{1,0:T(8,128)(2,1)S(1)} %convert_element_type.3.rest_10_), channel_id=1, source_target_pairs={{0,1},{1,0},{2,3},{3,2},{4,5},{5,4},{6,7},{7,6},{8,9},{9,8},{10,11... | collective-permute-start | bytes 393224 | tf_op jit(solution)/shard_map/ppermute | solution.py:329
  12.6 0.9 %copy_bitcast_fusion.rest_0_ = s16[32,1152]{1,0:T(8,128)(2,1)S(1)} fusion(s16[9,32,128]{2,1,0:T(8,128)(2,1)} %get-tuple-element.25), kind=kLoop, calls=%fused_computation.4 | loop fusion | bytes 147456 | tf_op jit(solution)/shard_map/reshape | solution.py:356
  14.1 0.8 %collective-permute-done.3.rest_4_ = s16[9,32,128]{2,1,0:T(8,128)(2,1)S(1)} collective-permute-done((s16[9,32,128]{2,1,0:T(8,128)(2,1)}, s16[9,32,128]{2,1,0:T(8,128)(2,1)S(1)}, u32[]{:S(2)}, u32[]{:S(2)}) %collective-permute-start.3) | collective-permute-done | bytes 73760 | tf_op jit(solution)/shard_map/ppermute | solution.py:329
  14.9 0.5 %collective-permute-start.8 = (s16[9,32,128]{2,1,0:T(8,128)(2,1)S(1)}, s16[9,32,128]{2,1,0:T(8,128)(2,1)S(1)}, u32[]{:S(2)}, u32[]{:S(2)}) collective-permute-start(s16[9,32,128]{2,1,0:T(8,128)(2,1)S(1)} %collective-permute-done.3.rest_4_), channel_id=1, source_target_pairs={{0,1},{1,0},{2,3},{3,2},{4,5},{5,4},{6,7},{7,6},{8,9},{9,8},{10,11... | collective-permute-start | bytes 221192 | tf_op jit(solution)/shard_map/ppermute | solution.py:329
  15.4 0.7 %collective-permute-done.7.rest_8_ = s16[9,32,128]{2,1,0:T(8,128)(2,1)S(1)} collective-permute-done((s16[9,32,128]{2,1,0:T(8,128)(2,1)S(1)}, s16[9,32,128]{2,1,0:T(8,128)(2,1)S(1)}, u32[]{:S(2)}, u32[]{:S(2)}) %collective-permute-start.7) | collective-permute-done | bytes 73760 | tf_op jit(solution)/shard_map/ppermute | solution.py:329
  16.3 1.4 %gram.1 = (f32[32,512]{1,0:T(8,128)S(1)}, f32[32,512]{1,0:T(8,128)S(1)}, f32[32,512]{1,0:T(8,128)S(1)}, f32[32,512]{1,0:T(8,128)S(1)}, f32[32,512]{1,0:T(8,128)S(1)}) custom-call(s32[1,32]{1,0:T(1,128)S(1)} %copy-done.2, f32[32,128]{1,0:T(8,128)S(1)} %copy-done.1, s16[32,1152]{1,0:T(8,128)(2,1)S(1)} %copy_bitcast_fusion.rest_0_, ...), custom_call_target="tpu_custom_call" | custom-call | tf_op jit(solution)/shard_map/gram/pallas_call | solution.py:361
  18.3 3.0 %collective-permute-start.12 = (f32[32,512]{1,0:T(8,128)S(1)}, f32[32,512]{1,0:T(8,128)S(1)}, u32[]{:S(2)}, u32[]{:S(2)}) collective-permute-start(f32[32,512]{1,0:T(8,128)S(1)} %get-tuple-element.40), channel_id=1, source_target_pairs={{0,4},{4,0},{1,5},{5,1},{2,6},{6,2},{3,7},{7,3},{8,12},{12,8},{9,1... | collective-permute-start | bytes 196616 | tf_op jit(solution)/shard_map/ppermute | solution.py:329
  21.3 1.5 %collective-permute-start.13 = (f32[32,512]{1,0:T(8,128)S(1)}, f32[32,512]{1,0:T(8,128)S(1)}, u32[]{:S(2)}, u32[]{:S(2)}) collective-permute-start(f32[32,512]{1,0:T(8,128)S(1)} %get-tuple-element.41), channel_id=1, source_target_pairs={{0,2},{2,0},{1,3},{3,1},{4,6},{6,4},{5,7},{7,5},{8,10},{10,8},{9,1... | collective-permute-start | bytes 196616 | tf_op jit(solution)/shard_map/ppermute | solution.py:329
  23.1 1.5 %collective-permute-done.12 = f32[32,512]{1,0:T(8,128)S(1)} collective-permute-done((f32[32,512]{1,0:T(8,128)S(1)}, f32[32,512]{1,0:T(8,128)S(1)}, u32[]{:S(2)}, u32[]{:S(2)}) %collective-permute-start.12) | collective-permute-done | bytes 65568 | tf_op jit(solution)/shard_map/ppermute | solution.py:329
  24.7 0.9 %collective-permute-done.13 = f32[32,512]{1,0:T(8,128)S(1)} collective-permute-done((f32[32,512]{1,0:T(8,128)S(1)}, f32[32,512]{1,0:T(8,128)S(1)}, u32[]{:S(2)}, u32[]{:S(2)}) %collective-permute-start.13) | collective-permute-done | bytes 65568 | tf_op jit(solution)/shard_map/ppermute | solution.py:329
  25.6 2.6 %collective-permute-start.16 = (f32[32,512]{1,0:T(8,128)S(1)}, f32[32,512]{1,0:T(8,128)S(1)}, u32[]{:S(2)}, u32[]{:S(2)}) collective-permute-start(f32[32,512]{1,0:T(8,128)S(1)} %add_add_fusion.rest_0_), channel_id=1, source_target_pairs={{0,12},{1,13},{2,14},{3,15},{4,8},{5,9},{6,10},{7,11},{8,4},{9,5},... | collective-permute-start | bytes 196616 | tf_op jit(solution)/shard_map/ppermute | solution.py:329
  28.6 2.9 %collective-permute-start.14 = (f32[32,512]{1,0:T(8,128)S(1)}, f32[32,512]{1,0:T(8,128)S(1)}, u32[]{:S(2)}, u32[]{:S(2)}) collective-permute-start(f32[32,512]{1,0:T(8,128)S(1)} %add_add_fusion.rest_0_), channel_id=1, source_target_pairs={{0,8},{1,9},{2,10},{3,11},{4,12},{5,13},{6,14},{7,15},{8,0},{9,1},... | collective-permute-start | bytes 196616 | tf_op jit(solution)/shard_map/ppermute | solution.py:329
  31.5 0.8 %collective-permute-done.16.rest_3_ = f32[32,512]{1,0:T(8,128)S(1)} collective-permute-done((f32[32,512]{1,0:T(8,128)S(1)}, f32[32,512]{1,0:T(8,128)S(1)}, u32[]{:S(2)}, u32[]{:S(2)}) %collective-permute-start.16) | collective-permute-done | bytes 65568 | tf_op jit(solution)/shard_map/ppermute | solution.py:329
  32.3 1.4 %collective-permute-start.20 = (f32[32,512]{1,0:T(8,128)S(1)}, f32[32,512]{1,0:T(8,128)S(1)}, u32[]{:S(2)}, u32[]{:S(2)}) collective-permute-start(f32[32,512]{1,0:T(8,128)S(1)} %collective-permute-done.16.rest_3_), channel_id=1, source_target_pairs={{0,2},{1,3},{2,0},{3,1},{4,6},{5,7},{6,4},{7,5},{8,10},{9,11},{10,... | collective-permute-start | bytes 196616 | tf_op jit(solution)/shard_map/ppermute | solution.py:329
  33.7 0.8 %collective-permute-start.19 = (f32[32,512]{1,0:T(8,128)S(1)}, f32[32,512]{1,0:T(8,128)S(1)}, u32[]{:S(2)}, u32[]{:S(2)}) collective-permute-start(f32[32,512]{1,0:T(8,128)S(1)} %collective-permute-done.15.rest_2_), channel_id=1, source_target_pairs={{0,2},{1,3},{2,0},{3,1},{4,6},{5,7},{6,4},{7,5},{8,10},{9,11},{10,... | collective-permute-start | bytes 196616 | tf_op jit(solution)/shard_map/ppermute | solution.py:329
  34.5 1.3 %collective-permute-start.18 = (f32[32,512]{1,0:T(8,128)S(1)}, f32[32,512]{1,0:T(8,128)S(1)}, u32[]{:S(2)}, u32[]{:S(2)}) collective-permute-start(f32[32,512]{1,0:T(8,128)S(1)} %collective-permute-done.14.rest_1_), channel_id=1, source_target_pairs={{0,2},{1,3},{2,0},{3,1},{4,6},{5,7},{6,4},{7,5},{8,10},{9,11},{10,... | collective-permute-start | bytes 196616 | tf_op jit(solution)/shard_map/ppermute | solution.py:329
  35.8 0.7 %collective-permute-done.20.rest_7_ = f32[32,512]{1,0:T(8,128)S(1)} collective-permute-done((f32[32,512]{1,0:T(8,128)S(1)}, f32[32,512]{1,0:T(8,128)S(1)}, u32[]{:S(2)}, u32[]{:S(2)}) %collective-permute-start.20) | collective-permute-done | bytes 65568 | tf_op jit(solution)/shard_map/ppermute | solution.py:329
  36.6 2.1 %collective-permute-done.19.rest_6_ = f32[32,512]{1,0:T(8,128)S(1)} collective-permute-done((f32[32,512]{1,0:T(8,128)S(1)}, f32[32,512]{1,0:T(8,128)S(1)}, u32[]{:S(2)}, u32[]{:S(2)}) %collective-permute-start.19) | collective-permute-done | bytes 65568 | tf_op jit(solution)/shard_map/ppermute | solution.py:329
  38.8 0.9 %collective-permute-done.18.rest_5_ = f32[32,512]{1,0:T(8,128)S(1)} collective-permute-done((f32[32,512]{1,0:T(8,128)S(1)}, f32[32,512]{1,0:T(8,128)S(1)}, u32[]{:S(2)}, u32[]{:S(2)}) %collective-permute-start.18) | collective-permute-done | bytes 65568 | tf_op jit(solution)/shard_map/ppermute | solution.py:329
  40.1 0.9 %collective-permute-done.22.rest_9_ = f32[64,512]{1,0:T(8,128)S(1)} collective-permute-done((f32[64,512]{1,0:T(8,128)S(1)}, f32[64,512]{1,0:T(8,128)S(1)}, u32[]{:S(2)}, u32[]{:S(2)}) %collective-permute-start.22) | collective-permute-done | bytes 131104 | tf_op jit(solution)/shard_map/ppermute | solution.py:329
  41.1 2.6 %descend.1 = (f32[512,128]{1,0:T(8,128)}, f32[32,128]{1,0:T(8,128)}) custom-call(f32[512,128]{1,0:T(8,128)S(1)} %copy-done, bf16[512,320]{1,0:T(8,128)(2,1)S(1)} %get-tuple-element.35.high_ref, bf16[512,320]{1,0:T(8,128)(2,1)S(1)} %get-tuple-element.36.low_ref, f32[32,512]{1,0:T(8,128)S(1)} %add_add_fusion.rest_0_, ...), custom_call_target="tpu_custom_call" | custom-call | tf_op jit(solution)/shard_map/descend/pallas_call | solution.py:409
  (43 shorter events, 3.4 us)
Async XLA Ops:
  4.3 7.7 %collective-permute-start.1 = (s16[9,32,128]{2,1,0:T(8,128)(2,1)}, s16[9,32,128]{2,1,0:T(8,128)(2,1)S(1)}, u32[]{:S(2)}, u32[]{:S(2)}) collective-permute-start(s16[9,32,128]{2,1,0:T(8,128)(2,1)} %get-tuple-element.23), channel_id=1, source_target_pairs={{2,4},{4,2},{3,5},{5,3},{6,8},{8,6},{7,9},{9,7},{10,12},{12,10},{1... | collective-permute-start | bytes 221192 | tf_op jit(solution)/shard_map/ppermute | solution.py:329
  4.8 8.7 %collective-permute-start = (s16[9,32,128]{2,1,0:T(8,128)(2,1)}, s16[9,32,128]{2,1,0:T(8,128)(2,1)S(1)}, u32[]{:S(2)}, u32[]{:S(2)}) collective-permute-start(s16[9,32,128]{2,1,0:T(8,128)(2,1)} %get-tuple-element.22), channel_id=1, source_target_pairs={{4,8},{8,4},{5,9},{9,5},{6,10},{10,6},{7,11},{11,7},{0,1},{1,0},{2... | collective-permute-start | bytes 221192 | tf_op jit(solution)/shard_map/ppermute | solution.py:329
  4.9 8.7 %collective-permute-start.2 = (s16[9,32,128]{2,1,0:T(8,128)(2,1)}, s16[9,32,128]{2,1,0:T(8,128)(2,1)S(1)}, u32[]{:S(2)}, u32[]{:S(2)}) collective-permute-start(s16[9,32,128]{2,1,0:T(8,128)(2,1)} %get-tuple-element.29), channel_id=1, source_target_pairs={{0,4},{4,0},{1,5},{5,1},{2,6},{6,2},{3,7},{7,3},{8,12},{12,8},{9,1... | collective-permute-start | bytes 221192 | tf_op jit(solution)/shard_map/ppermute | solution.py:329
  10.3 4.6 %collective-permute-start.3 = (s16[9,32,128]{2,1,0:T(8,128)(2,1)}, s16[9,32,128]{2,1,0:T(8,128)(2,1)S(1)}, u32[]{:S(2)}, u32[]{:S(2)}) collective-permute-start(s16[9,32,128]{2,1,0:T(8,128)(2,1)} %get-tuple-element.30), channel_id=1, source_target_pairs={{0,2},{2,0},{1,3},{3,1},{4,6},{6,4},{5,7},{7,5},{8,10},{10,8},{9,1... | collective-permute-start | bytes 221192 | tf_op jit(solution)/shard_map/ppermute | solution.py:329
  12.0 2.9 %collective-permute-start.4 = (s16[9,32,128]{2,1,0:T(8,128)(2,1)}, s16[9,32,128]{2,1,0:T(8,128)(2,1)S(1)}, u32[]{:S(2)}, u32[]{:S(2)}) collective-permute-start(s16[9,32,128]{2,1,0:T(8,128)(2,1)} %get-tuple-element.25), channel_id=1, source_target_pairs={{0,1},{1,0},{2,3},{3,2},{4,5},{5,4},{6,7},{7,6},{8,9},{9,8},{10,11... | collective-permute-start | bytes 221192 | tf_op jit(solution)/shard_map/ppermute | solution.py:329
  12.1 4.3 %collective-permute-start.9 = (bf16[512,128]{1,0:T(8,128)(2,1)S(1)}, bf16[512,128]{1,0:T(8,128)(2,1)S(1)}, u32[]{:S(2)}, u32[]{:S(2)}) collective-permute-start(bf16[512,128]{1,0:T(8,128)(2,1)S(1)} %convert_element_type.3.rest_10_), channel_id=1, source_target_pairs={{0,1},{1,0},{2,3},{3,2},{4,5},{5,4},{6,7},{7,6},{8,9},{9,8},{10,11... | collective-permute-start | bytes 393224 | tf_op jit(solution)/shard_map/ppermute | solution.py:329
  13.5 1.9 %collective-permute-start.6 = (s16[9,32,128]{2,1,0:T(8,128)(2,1)S(1)}, s16[9,32,128]{2,1,0:T(8,128)(2,1)S(1)}, u32[]{:S(2)}, u32[]{:S(2)}) collective-permute-start(s16[9,32,128]{2,1,0:T(8,128)(2,1)S(1)} %collective-permute-done.rest_2_), channel_id=1, source_target_pairs={{0,1},{1,0},{2,3},{3,2},{4,5},{5,4},{6,7},{7,6},{8,9},{9,8},{10,11... | collective-permute-start | bytes 221192 | tf_op jit(solution)/shard_map/ppermute | solution.py:329
  13.6 1.8 %collective-permute-start.5 = (s16[9,32,128]{2,1,0:T(8,128)(2,1)S(1)}, s16[9,32,128]{2,1,0:T(8,128)(2,1)S(1)}, u32[]{:S(2)}, u32[]{:S(2)}) collective-permute-start(s16[9,32,128]{2,1,0:T(8,128)(2,1)S(1)} %collective-permute-done.1.rest_1_), channel_id=1, source_target_pairs={{0,1},{1,0},{2,3},{3,2},{4,5},{5,4},{6,7},{7,6},{8,9},{9,8},{10,11... | collective-permute-start | bytes 221192 | tf_op jit(solution)/shard_map/ppermute | solution.py:329
  14.9 1.4 %collective-permute-start.8 = (s16[9,32,128]{2,1,0:T(8,128)(2,1)S(1)}, s16[9,32,128]{2,1,0:T(8,128)(2,1)S(1)}, u32[]{:S(2)}, u32[]{:S(2)}) collective-permute-start(s16[9,32,128]{2,1,0:T(8,128)(2,1)S(1)} %collective-permute-done.3.rest_4_), channel_id=1, source_target_pairs={{0,1},{1,0},{2,3},{3,2},{4,5},{5,4},{6,7},{7,6},{8,9},{9,8},{10,11... | collective-permute-start | bytes 221192 | tf_op jit(solution)/shard_map/ppermute | solution.py:329
  17.7 5.4 %collective-permute-start.10 = (f32[32,512]{1,0:T(8,128)S(1)}, f32[32,512]{1,0:T(8,128)S(1)}, u32[]{:S(2)}, u32[]{:S(2)}) collective-permute-start(f32[32,512]{1,0:T(8,128)S(1)} %get-tuple-element.38), channel_id=1, source_target_pairs={{2,4},{4,2},{3,5},{5,3},{6,8},{8,6},{7,9},{9,7},{10,12},{12,10},{1... | collective-permute-start | bytes 196616 | tf_op jit(solution)/shard_map/ppermute | solution.py:329
  18.1 5.0 %collective-permute-start.11 = (f32[32,512]{1,0:T(8,128)S(1)}, f32[32,512]{1,0:T(8,128)S(1)}, u32[]{:S(2)}, u32[]{:S(2)}) collective-permute-start(f32[32,512]{1,0:T(8,128)S(1)} %get-tuple-element.39), channel_id=1, source_target_pairs={{4,8},{8,4},{5,9},{9,5},{6,10},{10,6},{7,11},{11,7},{0,1},{1,0},{2... | collective-permute-start | bytes 196616 | tf_op jit(solution)/shard_map/ppermute | solution.py:329
  18.3 6.4 %collective-permute-start.12 = (f32[32,512]{1,0:T(8,128)S(1)}, f32[32,512]{1,0:T(8,128)S(1)}, u32[]{:S(2)}, u32[]{:S(2)}) collective-permute-start(f32[32,512]{1,0:T(8,128)S(1)} %get-tuple-element.40), channel_id=1, source_target_pairs={{0,4},{4,0},{1,5},{5,1},{2,6},{6,2},{3,7},{7,3},{8,12},{12,8},{9,1... | collective-permute-start | bytes 196616 | tf_op jit(solution)/shard_map/ppermute | solution.py:329
  21.3 4.3 %collective-permute-start.13 = (f32[32,512]{1,0:T(8,128)S(1)}, f32[32,512]{1,0:T(8,128)S(1)}, u32[]{:S(2)}, u32[]{:S(2)}) collective-permute-start(f32[32,512]{1,0:T(8,128)S(1)} %get-tuple-element.41), channel_id=1, source_target_pairs={{0,2},{2,0},{1,3},{3,1},{4,6},{6,4},{5,7},{7,5},{8,10},{10,8},{9,1... | collective-permute-start | bytes 196616 | tf_op jit(solution)/shard_map/ppermute | solution.py:329
  25.6 6.7 %collective-permute-start.16 = (f32[32,512]{1,0:T(8,128)S(1)}, f32[32,512]{1,0:T(8,128)S(1)}, u32[]{:S(2)}, u32[]{:S(2)}) collective-permute-start(f32[32,512]{1,0:T(8,128)S(1)} %add_add_fusion.rest_0_), channel_id=1, source_target_pairs={{0,12},{1,13},{2,14},{3,15},{4,8},{5,9},{6,10},{7,11},{8,4},{9,5},... | collective-permute-start | bytes 196616 | tf_op jit(solution)/shard_map/ppermute | solution.py:329
  28.2 5.4 %collective-permute-start.17 = (f32[32,512]{1,0:T(8,128)S(1)}, f32[32,512]{1,0:T(8,128)S(1)}, u32[]{:S(2)}, u32[]{:S(2)}) collective-permute-start(f32[32,512]{1,0:T(8,128)S(1)} %add_add_fusion.rest_0_), channel_id=1, source_target_pairs={{0,2},{1,3},{2,0},{3,1},{4,6},{5,7},{6,4},{7,5},{8,10},{9,11},{10,... | collective-permute-start | bytes 196616 | tf_op jit(solution)/shard_map/ppermute | solution.py:329
  28.6 5.2 %collective-permute-start.15 = (f32[32,512]{1,0:T(8,128)S(1)}, f32[32,512]{1,0:T(8,128)S(1)}, u32[]{:S(2)}, u32[]{:S(2)}) collective-permute-start(f32[32,512]{1,0:T(8,128)S(1)} %add_add_fusion.rest_0_), channel_id=1, source_target_pairs={{0,4},{1,5},{2,6},{3,7},{4,0},{5,1},{6,2},{7,3},{8,12},{9,13},{10,... | collective-permute-start | bytes 196616 | tf_op jit(solution)/shard_map/ppermute | solution.py:329
  28.6 6.0 %collective-permute-start.14 = (f32[32,512]{1,0:T(8,128)S(1)}, f32[32,512]{1,0:T(8,128)S(1)}, u32[]{:S(2)}, u32[]{:S(2)}) collective-permute-start(f32[32,512]{1,0:T(8,128)S(1)} %add_add_fusion.rest_0_), channel_id=1, source_target_pairs={{0,8},{1,9},{2,10},{3,11},{4,12},{5,13},{6,14},{7,15},{8,0},{9,1},... | collective-permute-start | bytes 196616 | tf_op jit(solution)/shard_map/ppermute | solution.py:329
  32.3 4.3 %collective-permute-start.20 = (f32[32,512]{1,0:T(8,128)S(1)}, f32[32,512]{1,0:T(8,128)S(1)}, u32[]{:S(2)}, u32[]{:S(2)}) collective-permute-start(f32[32,512]{1,0:T(8,128)S(1)} %collective-permute-done.16.rest_3_), channel_id=1, source_target_pairs={{0,2},{1,3},{2,0},{3,1},{4,6},{5,7},{6,4},{7,5},{8,10},{9,11},{10,... | collective-permute-start | bytes 196616 | tf_op jit(solution)/shard_map/ppermute | solution.py:329
  33.6 6.1 %collective-permute-start.21 = (f32[64,512]{1,0:T(8,128)S(1)}, f32[64,512]{1,0:T(8,128)S(1)}, u32[]{:S(2)}, u32[]{:S(2)}) collective-permute-start(f32[64,512]{1,0:T(8,128)S(1)} %pad_maximum_fusion), channel_id=1, source_target_pairs={{0,1},{1,0},{2,3},{3,2},{4,5},{5,4},{6,7},{7,6},{8,9},{9,8},{10,11... | collective-permute-start | bytes 393224 | tf_op jit(solution)/shard_map/ppermute | solution.py:329
  33.7 5.0 %collective-permute-start.19 = (f32[32,512]{1,0:T(8,128)S(1)}, f32[32,512]{1,0:T(8,128)S(1)}, u32[]{:S(2)}, u32[]{:S(2)}) collective-permute-start(f32[32,512]{1,0:T(8,128)S(1)} %collective-permute-done.15.rest_2_), channel_id=1, source_target_pairs={{0,2},{1,3},{2,0},{3,1},{4,6},{5,7},{6,4},{7,5},{8,10},{9,11},{10,... | collective-permute-start | bytes 196616 | tf_op jit(solution)/shard_map/ppermute | solution.py:329
  34.5 5.1 %collective-permute-start.18 = (f32[32,512]{1,0:T(8,128)S(1)}, f32[32,512]{1,0:T(8,128)S(1)}, u32[]{:S(2)}, u32[]{:S(2)}) collective-permute-start(f32[32,512]{1,0:T(8,128)S(1)} %collective-permute-done.14.rest_1_), channel_id=1, source_target_pairs={{0,2},{1,3},{2,0},{3,1},{4,6},{5,7},{6,4},{7,5},{8,10},{9,11},{10,... | collective-permute-start | bytes 196616 | tf_op jit(solution)/shard_map/ppermute | solution.py:329
  36.5 3.2 %collective-permute-start.24 = (f32[64,512]{1,0:T(8,128)S(1)}, f32[64,512]{1,0:T(8,128)S(1)}, u32[]{:S(2)}, u32[]{:S(2)}) collective-permute-start(f32[64,512]{1,0:T(8,128)S(1)} %pad_maximum_fusion.3), channel_id=1, source_target_pairs={{0,1},{1,0},{2,3},{3,2},{4,5},{5,4},{6,7},{7,6},{8,9},{9,8},{10,11... | collective-permute-start | bytes 393224 | tf_op jit(solution)/shard_map/ppermute | solution.py:329
  38.7 1.4 %collective-permute-start.23 = (f32[64,512]{1,0:T(8,128)S(1)}, f32[64,512]{1,0:T(8,128)S(1)}, u32[]{:S(2)}, u32[]{:S(2)}) collective-permute-start(f32[64,512]{1,0:T(8,128)S(1)} %pad_maximum_fusion.2), channel_id=1, source_target_pairs={{0,1},{1,0},{2,3},{3,2},{4,5},{5,4},{6,7},{7,6},{8,9},{9,8},{10,11... | collective-permute-start | bytes 393224 | tf_op jit(solution)/shard_map/ppermute | solution.py:329
  39.7 1.4 %collective-permute-start.22 = (f32[64,512]{1,0:T(8,128)S(1)}, f32[64,512]{1,0:T(8,128)S(1)}, u32[]{:S(2)}, u32[]{:S(2)}) collective-permute-start(f32[64,512]{1,0:T(8,128)S(1)} %pad_maximum_fusion.1), channel_id=1, source_target_pairs={{0,1},{1,0},{2,3},{3,2},{4,5},{5,4},{6,7},{7,6},{8,9},{9,8},{10,11... | collective-permute-start | bytes 393224 | tf_op jit(solution)/shard_map/ppermute | solution.py:329
  (4 other events, 44.1 us)

commit v7 on v6

--- a/solution.py
+++ b/solution.py
@@ -179,14 +179,10 @@
     for slot in range(WINDOW):
         offset = slot - CHIP_REACH
         base = padded[slot * bores : (slot + 1) * bores]
-        odd = lax.rem(chip + offset + 2, 2)
-        places = []
-        for parity in (0, 1):
-            shift = (CHIP_REACH - offset + parity) * span
-            moved = pltpu.roll(base, shift % width, 1) if shift % width else base
-            keep = (lane >= shift) & (lane < (WINDOW + parity) * span)
-            places.append(jnp.where(keep, moved, 0.0))
-        shifted[slot, :, :width] = jnp.where(odd == 1, places[1], places[0])
+        parity = lax.rem(chip + offset + 2, 2)
+        shift = (CHIP_REACH - offset + parity) * span
+        keep = (lane >= shift) & (lane < (WINDOW + parity) * span)
+        shifted[slot, :, :width] = jnp.where(keep, pltpu.roll(base, shift, 1), 0.0)
         shifted[slot, :, width:] = warm[slot * bores : (slot + 1) * bores]
     _, counts = bounds(lengths_ref[...], bores)
     odd = lax.rem(chip, 2)

time: 43.9 us -> 43.9 us (level)
  no operation moved by 1% of the time
where the time goes in v7:
time: 43.9 us; the launch traced here: 43.8 us
  starting transfers between devices  24.4 us (56%)
  waiting for transfers between devices  9.65 us (22%)
  Pallas kernels  7.96 us (18%)
  local copies, waits for them, and re-layouts  0.9 us (2%)
  between operations  0.81 us (2%)
    ppermute x25, starting transfers between devices, send(): return lax.ppermute(value, 'rows', pairs)  24.4 us
    ppermute x25, waiting for transfers between devices, send(): return lax.ppermute(value, 'rows', pairs)  9.65 us
    pallas_call x1, Pallas kernels, on_device(): pl.pallas_call(compress_kernel, out_shape=(piece,) * WINDOW, in_specs=[HB...  3.66 us
    pallas_call x1, Pallas kernels, on_device(): pl.pallas_call(functools.partial(descend_kernel, ranks, places), out_shap...  2.58 us
    pallas_call x1, Pallas kernels, on_device(): pl.pallas_call(gram_kernel, out_shape=(packed,) * WINDOW, in_specs=[VMEM]...  1.36 us
    reshape x1, local copies, waits for them, and re-layouts, on_device(): own = own.transpose(1, 0, 2).reshape(bores, (per_chip + 1) * tile)  0.89 us
  transfers between devices with their start and end apart: 25, of which 11 were waited for; matrix products, arithmetic and copies ran while one was open for 2% of the time, Pallas kernels for 1%

profile of v7, /device:TPU:0, one launch (start us, length us, event | category | flops | bytes accessed | tf_op | source)
XLA Modules:
  0.0 43.8 jit_solution(15140427747050332154)
XLA Ops:
  0.7 3.7 %compress.1 = (s16[9,32,128]{2,1,0:T(8,128)(2,1)}, s16[9,32,128]{2,1,0:T(8,128)(2,1)}, s16[9,32,128]{2,1,0:T(8,128)(2,1)}, s16[9,32,128]{2,1,0:T(8,128)(2,1)}, s16[9,32,128]{2,1,0:T(8,128)(2,1)}) custom-call(s32[4,30]{1,0:T(4,128)} %cols_hbm.1, s32[4]{0:T(128)} %count_hbm.1, s32[1,32]{1,0:T(1,128)} %lengths_ref.1, bf16[4,30,128,128]{3,2,1,0:T(8,128)(2,1)} %tiles_hbm.1), custom_call_target="tpu_custom_call" | custom-call | tf_op jit(solution)/shard_map/compress/pallas_call | solution.py:331
  4.3 0.5 %collective-permute-start.1 = (s16[9,32,128]{2,1,0:T(8,128)(2,1)}, s16[9,32,128]{2,1,0:T(8,128)(2,1)S(1)}, u32[]{:S(2)}, u32[]{:S(2)}) collective-permute-start(s16[9,32,128]{2,1,0:T(8,128)(2,1)} %get-tuple-element.23), channel_id=1, source_target_pairs={{2,4},{4,2},{3,5},{5,3},{6,8},{8,6},{7,9},{9,7},{10,12},{12,10},{1... | collective-permute-start | bytes 221192 | tf_op jit(solution)/shard_map/ppermute | solution.py:325
  4.9 5.5 %collective-permute-start.2 = (s16[9,32,128]{2,1,0:T(8,128)(2,1)}, s16[9,32,128]{2,1,0:T(8,128)(2,1)S(1)}, u32[]{:S(2)}, u32[]{:S(2)}) collective-permute-start(s16[9,32,128]{2,1,0:T(8,128)(2,1)} %get-tuple-element.29), channel_id=1, source_target_pairs={{0,4},{4,0},{1,5},{5,1},{2,6},{6,2},{3,7},{7,3},{8,12},{12,8},{9,1... | collective-permute-start | bytes 221192 | tf_op jit(solution)/shard_map/ppermute | solution.py:325
  10.4 1.6 %collective-permute-start.3 = (s16[9,32,128]{2,1,0:T(8,128)(2,1)}, s16[9,32,128]{2,1,0:T(8,128)(2,1)S(1)}, u32[]{:S(2)}, u32[]{:S(2)}) collective-permute-start(s16[9,32,128]{2,1,0:T(8,128)(2,1)} %get-tuple-element.30), channel_id=1, source_target_pairs={{0,2},{2,0},{1,3},{3,1},{4,6},{6,4},{5,7},{7,5},{8,10},{10,8},{9,1... | collective-permute-start | bytes 221192 | tf_op jit(solution)/shard_map/ppermute | solution.py:325
  12.0 0.6 %collective-permute-start.9 = (bf16[512,128]{1,0:T(8,128)(2,1)S(1)}, bf16[512,128]{1,0:T(8,128)(2,1)S(1)}, u32[]{:S(2)}, u32[]{:S(2)}) collective-permute-start(bf16[512,128]{1,0:T(8,128)(2,1)S(1)} %convert_element_type.3.rest_10_), channel_id=1, source_target_pairs={{0,1},{1,0},{2,3},{3,2},{4,5},{5,4},{6,7},{7,6},{8,9},{9,8},{10,11... | collective-permute-start | bytes 393224 | tf_op jit(solution)/shard_map/ppermute | solution.py:325
  12.6 0.9 %copy_bitcast_fusion.rest_0_ = s16[32,1152]{1,0:T(8,128)(2,1)S(1)} fusion(s16[9,32,128]{2,1,0:T(8,128)(2,1)} %get-tuple-element.25), kind=kLoop, calls=%fused_computation.4 | loop fusion | bytes 147456 | tf_op jit(solution)/shard_map/reshape | solution.py:352
  14.1 0.9 %collective-permute-done.3.rest_4_ = s16[9,32,128]{2,1,0:T(8,128)(2,1)S(1)} collective-permute-done((s16[9,32,128]{2,1,0:T(8,128)(2,1)}, s16[9,32,128]{2,1,0:T(8,128)(2,1)S(1)}, u32[]{:S(2)}, u32[]{:S(2)}) %collective-permute-start.3) | collective-permute-done | bytes 73760 | tf_op jit(solution)/shard_map/ppermute | solution.py:325
  14.9 0.5 %collective-permute-start.8 = (s16[9,32,128]{2,1,0:T(8,128)(2,1)S(1)}, s16[9,32,128]{2,1,0:T(8,128)(2,1)S(1)}, u32[]{:S(2)}, u32[]{:S(2)}) collective-permute-start(s16[9,32,128]{2,1,0:T(8,128)(2,1)S(1)} %collective-permute-done.3.rest_4_), channel_id=1, source_target_pairs={{0,1},{1,0},{2,3},{3,2},{4,5},{5,4},{6,7},{7,6},{8,9},{9,8},{10,11... | collective-permute-start | bytes 221192 | tf_op jit(solution)/shard_map/ppermute | solution.py:325
  15.5 0.7 %collective-permute-done.7.rest_8_ = s16[9,32,128]{2,1,0:T(8,128)(2,1)S(1)} collective-permute-done((s16[9,32,128]{2,1,0:T(8,128)(2,1)S(1)}, s16[9,32,128]{2,1,0:T(8,128)(2,1)S(1)}, u32[]{:S(2)}, u32[]{:S(2)}) %collective-permute-start.7) | collective-permute-done | bytes 73760 | tf_op jit(solution)/shard_map/ppermute | solution.py:325
  16.4 1.4 %gram.1 = (f32[32,512]{1,0:T(8,128)S(1)}, f32[32,512]{1,0:T(8,128)S(1)}, f32[32,512]{1,0:T(8,128)S(1)}, f32[32,512]{1,0:T(8,128)S(1)}, f32[32,512]{1,0:T(8,128)S(1)}) custom-call(s32[1,32]{1,0:T(1,128)S(1)} %copy-done.2, f32[32,128]{1,0:T(8,128)S(1)} %copy-done.1, s16[32,1152]{1,0:T(8,128)(2,1)S(1)} %copy_bitcast_fusion.rest_0_, ...), custom_call_target="tpu_custom_call" | custom-call | tf_op jit(solution)/shard_map/gram/pallas_call | solution.py:357
  18.3 2.9 %collective-permute-start.12 = (f32[32,512]{1,0:T(8,128)S(1)}, f32[32,512]{1,0:T(8,128)S(1)}, u32[]{:S(2)}, u32[]{:S(2)}) collective-permute-start(f32[32,512]{1,0:T(8,128)S(1)} %get-tuple-element.40), channel_id=1, source_target_pairs={{0,4},{4,0},{1,5},{5,1},{2,6},{6,2},{3,7},{7,3},{8,12},{12,8},{9,1... | collective-permute-start | bytes 196616 | tf_op jit(solution)/shard_map/ppermute | solution.py:325
  21.2 1.6 %collective-permute-start.13 = (f32[32,512]{1,0:T(8,128)S(1)}, f32[32,512]{1,0:T(8,128)S(1)}, u32[]{:S(2)}, u32[]{:S(2)}) collective-permute-start(f32[32,512]{1,0:T(8,128)S(1)} %get-tuple-element.41), channel_id=1, source_target_pairs={{0,2},{2,0},{1,3},{3,1},{4,6},{6,4},{5,7},{7,5},{8,10},{10,8},{9,1... | collective-permute-start | bytes 196616 | tf_op jit(solution)/shard_map/ppermute | solution.py:325
  23.2 1.4 %collective-permute-done.12 = f32[32,512]{1,0:T(8,128)S(1)} collective-permute-done((f32[32,512]{1,0:T(8,128)S(1)}, f32[32,512]{1,0:T(8,128)S(1)}, u32[]{:S(2)}, u32[]{:S(2)}) %collective-permute-start.12) | collective-permute-done | bytes 65568 | tf_op jit(solution)/shard_map/ppermute | solution.py:325
  24.6 0.9 %collective-permute-done.13 = f32[32,512]{1,0:T(8,128)S(1)} collective-permute-done((f32[32,512]{1,0:T(8,128)S(1)}, f32[32,512]{1,0:T(8,128)S(1)}, u32[]{:S(2)}, u32[]{:S(2)}) %collective-permute-start.13) | collective-permute-done | bytes 65568 | tf_op jit(solution)/shard_map/ppermute | solution.py:325
  25.5 2.6 %collective-permute-start.16 = (f32[32,512]{1,0:T(8,128)S(1)}, f32[32,512]{1,0:T(8,128)S(1)}, u32[]{:S(2)}, u32[]{:S(2)}) collective-permute-start(f32[32,512]{1,0:T(8,128)S(1)} %add_add_fusion.rest_0_), channel_id=1, source_target_pairs={{0,12},{1,13},{2,14},{3,15},{4,8},{5,9},{6,10},{7,11},{8,4},{9,5},... | collective-permute-start | bytes 196616 | tf_op jit(solution)/shard_map/ppermute | solution.py:325
  28.6 3.0 %collective-permute-start.14 = (f32[32,512]{1,0:T(8,128)S(1)}, f32[32,512]{1,0:T(8,128)S(1)}, u32[]{:S(2)}, u32[]{:S(2)}) collective-permute-start(f32[32,512]{1,0:T(8,128)S(1)} %add_add_fusion.rest_0_), channel_id=1, source_target_pairs={{0,8},{1,9},{2,10},{3,11},{4,12},{5,13},{6,14},{7,15},{8,0},{9,1},... | collective-permute-start | bytes 196616 | tf_op jit(solution)/shard_map/ppermute | solution.py:325
  31.6 0.6 %collective-permute-done.16.rest_3_ = f32[32,512]{1,0:T(8,128)S(1)} collective-permute-done((f32[32,512]{1,0:T(8,128)S(1)}, f32[32,512]{1,0:T(8,128)S(1)}, u32[]{:S(2)}, u32[]{:S(2)}) %collective-permute-start.16) | collective-permute-done | bytes 65568 | tf_op jit(solution)/shard_map/ppermute | solution.py:325
  32.2 1.6 %collective-permute-start.20 = (f32[32,512]{1,0:T(8,128)S(1)}, f32[32,512]{1,0:T(8,128)S(1)}, u32[]{:S(2)}, u32[]{:S(2)}) collective-permute-start(f32[32,512]{1,0:T(8,128)S(1)} %collective-permute-done.16.rest_3_), channel_id=1, source_target_pairs={{0,2},{1,3},{2,0},{3,1},{4,6},{5,7},{6,4},{7,5},{8,10},{9,11},{10,... | collective-permute-start | bytes 196616 | tf_op jit(solution)/shard_map/ppermute | solution.py:325
  33.9 0.6 %collective-permute-start.19 = (f32[32,512]{1,0:T(8,128)S(1)}, f32[32,512]{1,0:T(8,128)S(1)}, u32[]{:S(2)}, u32[]{:S(2)}) collective-permute-start(f32[32,512]{1,0:T(8,128)S(1)} %collective-permute-done.15.rest_2_), channel_id=1, source_target_pairs={{0,2},{1,3},{2,0},{3,1},{4,6},{5,7},{6,4},{7,5},{8,10},{9,11},{10,... | collective-permute-start | bytes 196616 | tf_op jit(solution)/shard_map/ppermute | solution.py:325
  34.5 1.5 %collective-permute-start.18 = (f32[32,512]{1,0:T(8,128)S(1)}, f32[32,512]{1,0:T(8,128)S(1)}, u32[]{:S(2)}, u32[]{:S(2)}) collective-permute-start(f32[32,512]{1,0:T(8,128)S(1)} %collective-permute-done.14.rest_1_), channel_id=1, source_target_pairs={{0,2},{1,3},{2,0},{3,1},{4,6},{5,7},{6,4},{7,5},{8,10},{9,11},{10,... | collective-permute-start | bytes 196616 | tf_op jit(solution)/shard_map/ppermute | solution.py:325
  36.5 2.3 %collective-permute-done.19.rest_6_ = f32[32,512]{1,0:T(8,128)S(1)} collective-permute-done((f32[32,512]{1,0:T(8,128)S(1)}, f32[32,512]{1,0:T(8,128)S(1)}, u32[]{:S(2)}, u32[]{:S(2)}) %collective-permute-start.19) | collective-permute-done | bytes 65568 | tf_op jit(solution)/shard_map/ppermute | solution.py:325
  38.9 0.9 %collective-permute-done.18.rest_5_ = f32[32,512]{1,0:T(8,128)S(1)} collective-permute-done((f32[32,512]{1,0:T(8,128)S(1)}, f32[32,512]{1,0:T(8,128)S(1)}, u32[]{:S(2)}, u32[]{:S(2)}) %collective-permute-start.18) | collective-permute-done | bytes 65568 | tf_op jit(solution)/shard_map/ppermute | solution.py:325
  40.2 0.9 %collective-permute-done.22.rest_9_ = f32[64,512]{1,0:T(8,128)S(1)} collective-permute-done((f32[64,512]{1,0:T(8,128)S(1)}, f32[64,512]{1,0:T(8,128)S(1)}, u32[]{:S(2)}, u32[]{:S(2)}) %collective-permute-start.22) | collective-permute-done | bytes 131104 | tf_op jit(solution)/shard_map/ppermute | solution.py:325
  41.2 2.6 %descend.1 = (f32[512,128]{1,0:T(8,128)}, f32[32,128]{1,0:T(8,128)}) custom-call(f32[512,128]{1,0:T(8,128)S(1)} %copy-done, bf16[512,320]{1,0:T(8,128)(2,1)S(1)} %get-tuple-element.35.high_ref, bf16[512,320]{1,0:T(8,128)(2,1)S(1)} %get-tuple-element.36.low_ref, f32[32,512]{1,0:T(8,128)S(1)} %add_add_fusion.rest_0_, ...), custom_call_target="tpu_custom_call" | custom-call | tf_op jit(solution)/shard_map/descend/pallas_call | solution.py:405
  (43 shorter events, 3.5 us)
Async XLA Ops:
  4.3 7.7 %collective-permute-start.1 = (s16[9,32,128]{2,1,0:T(8,128)(2,1)}, s16[9,32,128]{2,1,0:T(8,128)(2,1)S(1)}, u32[]{:S(2)}, u32[]{:S(2)}) collective-permute-start(s16[9,32,128]{2,1,0:T(8,128)(2,1)} %get-tuple-element.23), channel_id=1, source_target_pairs={{2,4},{4,2},{3,5},{5,3},{6,8},{8,6},{7,9},{9,7},{10,12},{12,10},{1... | collective-permute-start | bytes 221192 | tf_op jit(solution)/shard_map/ppermute | solution.py:325
  4.8 8.6 %collective-permute-start = (s16[9,32,128]{2,1,0:T(8,128)(2,1)}, s16[9,32,128]{2,1,0:T(8,128)(2,1)S(1)}, u32[]{:S(2)}, u32[]{:S(2)}) collective-permute-start(s16[9,32,128]{2,1,0:T(8,128)(2,1)} %get-tuple-element.22), channel_id=1, source_target_pairs={{4,8},{8,4},{5,9},{9,5},{6,10},{10,6},{7,11},{11,7},{0,1},{1,0},{2... | collective-permute-start | bytes 221192 | tf_op jit(solution)/shard_map/ppermute | solution.py:325
  4.9 8.7 %collective-permute-start.2 = (s16[9,32,128]{2,1,0:T(8,128)(2,1)}, s16[9,32,128]{2,1,0:T(8,128)(2,1)S(1)}, u32[]{:S(2)}, u32[]{:S(2)}) collective-permute-start(s16[9,32,128]{2,1,0:T(8,128)(2,1)} %get-tuple-element.29), channel_id=1, source_target_pairs={{0,4},{4,0},{1,5},{5,1},{2,6},{6,2},{3,7},{7,3},{8,12},{12,8},{9,1... | collective-permute-start | bytes 221192 | tf_op jit(solution)/shard_map/ppermute | solution.py:325
  10.4 4.6 %collective-permute-start.3 = (s16[9,32,128]{2,1,0:T(8,128)(2,1)}, s16[9,32,128]{2,1,0:T(8,128)(2,1)S(1)}, u32[]{:S(2)}, u32[]{:S(2)}) collective-permute-start(s16[9,32,128]{2,1,0:T(8,128)(2,1)} %get-tuple-element.30), channel_id=1, source_target_pairs={{0,2},{2,0},{1,3},{3,1},{4,6},{6,4},{5,7},{7,5},{8,10},{10,8},{9,1... | collective-permute-start | bytes 221192 | tf_op jit(solution)/shard_map/ppermute | solution.py:325
  12.0 3.0 %collective-permute-start.4 = (s16[9,32,128]{2,1,0:T(8,128)(2,1)}, s16[9,32,128]{2,1,0:T(8,128)(2,1)S(1)}, u32[]{:S(2)}, u32[]{:S(2)}) collective-permute-start(s16[9,32,128]{2,1,0:T(8,128)(2,1)} %get-tuple-element.25), channel_id=1, source_target_pairs={{0,1},{1,0},{2,3},{3,2},{4,5},{5,4},{6,7},{7,6},{8,9},{9,8},{10,11... | collective-permute-start | bytes 221192 | tf_op jit(solution)/shard_map/ppermute | solution.py:325
  12.0 4.3 %collective-permute-start.9 = (bf16[512,128]{1,0:T(8,128)(2,1)S(1)}, bf16[512,128]{1,0:T(8,128)(2,1)S(1)}, u32[]{:S(2)}, u32[]{:S(2)}) collective-permute-start(bf16[512,128]{1,0:T(8,128)(2,1)S(1)} %convert_element_type.3.rest_10_), channel_id=1, source_target_pairs={{0,1},{1,0},{2,3},{3,2},{4,5},{5,4},{6,7},{7,6},{8,9},{9,8},{10,11... | collective-permute-start | bytes 393224 | tf_op jit(solution)/shard_map/ppermute | solution.py:325
  13.5 2.0 %collective-permute-start.6 = (s16[9,32,128]{2,1,0:T(8,128)(2,1)S(1)}, s16[9,32,128]{2,1,0:T(8,128)(2,1)S(1)}, u32[]{:S(2)}, u32[]{:S(2)}) collective-permute-start(s16[9,32,128]{2,1,0:T(8,128)(2,1)S(1)} %collective-permute-done.rest_2_), channel_id=1, source_target_pairs={{0,1},{1,0},{2,3},{3,2},{4,5},{5,4},{6,7},{7,6},{8,9},{9,8},{10,11... | collective-permute-start | bytes 221192 | tf_op jit(solution)/shard_map/ppermute | solution.py:325
  13.6 1.9 %collective-permute-start.5 = (s16[9,32,128]{2,1,0:T(8,128)(2,1)S(1)}, s16[9,32,128]{2,1,0:T(8,128)(2,1)S(1)}, u32[]{:S(2)}, u32[]{:S(2)}) collective-permute-start(s16[9,32,128]{2,1,0:T(8,128)(2,1)S(1)} %collective-permute-done.1.rest_1_), channel_id=1, source_target_pairs={{0,1},{1,0},{2,3},{3,2},{4,5},{5,4},{6,7},{7,6},{8,9},{9,8},{10,11... | collective-permute-start | bytes 221192 | tf_op jit(solution)/shard_map/ppermute | solution.py:325
  14.9 1.4 %collective-permute-start.8 = (s16[9,32,128]{2,1,0:T(8,128)(2,1)S(1)}, s16[9,32,128]{2,1,0:T(8,128)(2,1)S(1)}, u32[]{:S(2)}, u32[]{:S(2)}) collective-permute-start(s16[9,32,128]{2,1,0:T(8,128)(2,1)S(1)} %collective-permute-done.3.rest_4_), channel_id=1, source_target_pairs={{0,1},{1,0},{2,3},{3,2},{4,5},{5,4},{6,7},{7,6},{8,9},{9,8},{10,11... | collective-permute-start | bytes 221192 | tf_op jit(solution)/shard_map/ppermute | solution.py:325
  17.7 5.5 %collective-permute-start.10 = (f32[32,512]{1,0:T(8,128)S(1)}, f32[32,512]{1,0:T(8,128)S(1)}, u32[]{:S(2)}, u32[]{:S(2)}) collective-permute-start(f32[32,512]{1,0:T(8,128)S(1)} %get-tuple-element.38), channel_id=1, source_target_pairs={{2,4},{4,2},{3,5},{5,3},{6,8},{8,6},{7,9},{9,7},{10,12},{12,10},{1... | collective-permute-start | bytes 196616 | tf_op jit(solution)/shard_map/ppermute | solution.py:325
  18.2 5.0 %collective-permute-start.11 = (f32[32,512]{1,0:T(8,128)S(1)}, f32[32,512]{1,0:T(8,128)S(1)}, u32[]{:S(2)}, u32[]{:S(2)}) collective-permute-start(f32[32,512]{1,0:T(8,128)S(1)} %get-tuple-element.39), channel_id=1, source_target_pairs={{4,8},{8,4},{5,9},{9,5},{6,10},{10,6},{7,11},{11,7},{0,1},{1,0},{2... | collective-permute-start | bytes 196616 | tf_op jit(solution)/shard_map/ppermute | solution.py:325
  18.3 6.3 %collective-permute-start.12 = (f32[32,512]{1,0:T(8,128)S(1)}, f32[32,512]{1,0:T(8,128)S(1)}, u32[]{:S(2)}, u32[]{:S(2)}) collective-permute-start(f32[32,512]{1,0:T(8,128)S(1)} %get-tuple-element.40), channel_id=1, source_target_pairs={{0,4},{4,0},{1,5},{5,1},{2,6},{6,2},{3,7},{7,3},{8,12},{12,8},{9,1... | collective-permute-start | bytes 196616 | tf_op jit(solution)/shard_map/ppermute | solution.py:325
  21.2 4.3 %collective-permute-start.13 = (f32[32,512]{1,0:T(8,128)S(1)}, f32[32,512]{1,0:T(8,128)S(1)}, u32[]{:S(2)}, u32[]{:S(2)}) collective-permute-start(f32[32,512]{1,0:T(8,128)S(1)} %get-tuple-element.41), channel_id=1, source_target_pairs={{0,2},{2,0},{1,3},{3,1},{4,6},{6,4},{5,7},{7,5},{8,10},{10,8},{9,1... | collective-permute-start | bytes 196616 | tf_op jit(solution)/shard_map/ppermute | solution.py:325
  25.5 6.7 %collective-permute-start.16 = (f32[32,512]{1,0:T(8,128)S(1)}, f32[32,512]{1,0:T(8,128)S(1)}, u32[]{:S(2)}, u32[]{:S(2)}) collective-permute-start(f32[32,512]{1,0:T(8,128)S(1)} %add_add_fusion.rest_0_), channel_id=1, source_target_pairs={{0,12},{1,13},{2,14},{3,15},{4,8},{5,9},{6,10},{7,11},{8,4},{9,5},... | collective-permute-start | bytes 196616 | tf_op jit(solution)/shard_map/ppermute | solution.py:325
  28.2 5.6 %collective-permute-start.17 = (f32[32,512]{1,0:T(8,128)S(1)}, f32[32,512]{1,0:T(8,128)S(1)}, u32[]{:S(2)}, u32[]{:S(2)}) collective-permute-start(f32[32,512]{1,0:T(8,128)S(1)} %add_add_fusion.rest_0_), channel_id=1, source_target_pairs={{0,2},{1,3},{2,0},{3,1},{4,6},{5,7},{6,4},{7,5},{8,10},{9,11},{10,... | collective-permute-start | bytes 196616 | tf_op jit(solution)/shard_map/ppermute | solution.py:325
  28.6 5.2 %collective-permute-start.15 = (f32[32,512]{1,0:T(8,128)S(1)}, f32[32,512]{1,0:T(8,128)S(1)}, u32[]{:S(2)}, u32[]{:S(2)}) collective-permute-start(f32[32,512]{1,0:T(8,128)S(1)} %add_add_fusion.rest_0_), channel_id=1, source_target_pairs={{0,4},{1,5},{2,6},{3,7},{4,0},{5,1},{6,2},{7,3},{8,12},{9,13},{10,... | collective-permute-start | bytes 196616 | tf_op jit(solution)/shard_map/ppermute | solution.py:325
  28.6 5.8 %collective-permute-start.14 = (f32[32,512]{1,0:T(8,128)S(1)}, f32[32,512]{1,0:T(8,128)S(1)}, u32[]{:S(2)}, u32[]{:S(2)}) collective-permute-start(f32[32,512]{1,0:T(8,128)S(1)} %add_add_fusion.rest_0_), channel_id=1, source_target_pairs={{0,8},{1,9},{2,10},{3,11},{4,12},{5,13},{6,14},{7,15},{8,0},{9,1},... | collective-permute-start | bytes 196616 | tf_op jit(solution)/shard_map/ppermute | solution.py:325
  32.2 4.3 %collective-permute-start.20 = (f32[32,512]{1,0:T(8,128)S(1)}, f32[32,512]{1,0:T(8,128)S(1)}, u32[]{:S(2)}, u32[]{:S(2)}) collective-permute-start(f32[32,512]{1,0:T(8,128)S(1)} %collective-permute-done.16.rest_3_), channel_id=1, source_target_pairs={{0,2},{1,3},{2,0},{3,1},{4,6},{5,7},{6,4},{7,5},{8,10},{9,11},{10,... | collective-permute-start | bytes 196616 | tf_op jit(solution)/shard_map/ppermute | solution.py:325
  33.8 6.1 %collective-permute-start.21 = (f32[64,512]{1,0:T(8,128)S(1)}, f32[64,512]{1,0:T(8,128)S(1)}, u32[]{:S(2)}, u32[]{:S(2)}) collective-permute-start(f32[64,512]{1,0:T(8,128)S(1)} %pad_maximum_fusion), channel_id=1, source_target_pairs={{0,1},{1,0},{2,3},{3,2},{4,5},{5,4},{6,7},{7,6},{8,9},{9,8},{10,11... | collective-permute-start | bytes 393224 | tf_op jit(solution)/shard_map/ppermute | solution.py:325
  33.9 5.0 %collective-permute-start.19 = (f32[32,512]{1,0:T(8,128)S(1)}, f32[32,512]{1,0:T(8,128)S(1)}, u32[]{:S(2)}, u32[]{:S(2)}) collective-permute-start(f32[32,512]{1,0:T(8,128)S(1)} %collective-permute-done.15.rest_2_), channel_id=1, source_target_pairs={{0,2},{1,3},{2,0},{3,1},{4,6},{5,7},{6,4},{7,5},{8,10},{9,11},{10,... | collective-permute-start | bytes 196616 | tf_op jit(solution)/shard_map/ppermute | solution.py:325
  34.5 5.3 %collective-permute-start.18 = (f32[32,512]{1,0:T(8,128)S(1)}, f32[32,512]{1,0:T(8,128)S(1)}, u32[]{:S(2)}, u32[]{:S(2)}) collective-permute-start(f32[32,512]{1,0:T(8,128)S(1)} %collective-permute-done.14.rest_1_), channel_id=1, source_target_pairs={{0,2},{1,3},{2,0},{3,1},{4,6},{5,7},{6,4},{7,5},{8,10},{9,11},{10,... | collective-permute-start | bytes 196616 | tf_op jit(solution)/shard_map/ppermute | solution.py:325
  36.5 3.4 %collective-permute-start.24 = (f32[64,512]{1,0:T(8,128)S(1)}, f32[64,512]{1,0:T(8,128)S(1)}, u32[]{:S(2)}, u32[]{:S(2)}) collective-permute-start(f32[64,512]{1,0:T(8,128)S(1)} %pad_maximum_fusion.3), channel_id=1, source_target_pairs={{0,1},{1,0},{2,3},{3,2},{4,5},{5,4},{6,7},{7,6},{8,9},{9,8},{10,11... | collective-permute-start | bytes 393224 | tf_op jit(solution)/shard_map/ppermute | solution.py:325
  38.8 1.4 %collective-permute-start.23 = (f32[64,512]{1,0:T(8,128)S(1)}, f32[64,512]{1,0:T(8,128)S(1)}, u32[]{:S(2)}, u32[]{:S(2)}) collective-permute-start(f32[64,512]{1,0:T(8,128)S(1)} %pad_maximum_fusion.2), channel_id=1, source_target_pairs={{0,1},{1,0},{2,3},{3,2},{4,5},{5,4},{6,7},{7,6},{8,9},{9,8},{10,11... | collective-permute-start | bytes 393224 | tf_op jit(solution)/shard_map/ppermute | solution.py:325
  39.8 1.4 %collective-permute-start.22 = (f32[64,512]{1,0:T(8,128)S(1)}, f32[64,512]{1,0:T(8,128)S(1)}, u32[]{:S(2)}, u32[]{:S(2)}) collective-permute-start(f32[64,512]{1,0:T(8,128)S(1)} %pad_maximum_fusion.1), channel_id=1, source_target_pairs={{0,1},{1,0},{2,3},{3,2},{4,5},{5,4},{6,7},{7,6},{8,9},{9,8},{10,11... | collective-permute-start | bytes 393224 | tf_op jit(solution)/shard_map/ppermute | solution.py:325
  (4 other events, 44.1 us)
